TPU v7x, 128 devices: a whole 4x4x4 slice. The times are simulated.
128 devices in a mesh: gz: 128 (over z, y, x, core).
Axes of the slice: x: 4, y: 4, z: 4, core: 2. Of those that a mesh axis runs over, the one named last changes fastest.
Arguments:
- order_param: float32 [128, 512, 512], P('gz'), may hold values from 0.05 to 0.95
- concentration: float32 [128, 512, 512], P('gz'), may hold values from 0 to 1
- strain: float32 [6, 128, 512, 512], P(None, 'gz'), may hold values from -6 to 6
- grain_ids: int32 [128, 512, 512], P('gz'), may hold values from 0 to 15
- seed_labels: int32 [128, 512, 512], P('gz'), may hold values from 0 to 8
- grain_moduli: float32 [2, 16], replicated, may hold values from 0.5 to 2
- grain_mobility: float32 [16], replicated, may hold values from 0.25 to 1
- seed_rate: float32 [8], replicated, may hold values from 0.5 to 4
Outputs:
- order_next: float32 [128, 512, 512], P('gz')
- conc_next: float32 [128, 512, 512], P('gz')
- strain_next: float32 [6, 128, 512, 512], P(None, 'gz')
Inputs may be any that keep to these rules, and one draw needn't show every extreme that they name: `seed_labels`: 0 marks a voxel without seed; label k > 0 names entry k - 1 of seed_rate.
All inputs are finite; a program needn't handle non-finite values.
Results may differ from a plain program's by a relative error of at most 0.0003.
Values sent between devices are 32-bit elements; how exact they have to be, the bound alone decides.
No kernel may reach another device: no remote copies, remote signals or barrier semaphores. Data moves between devices by JAX's collectives and lax.ppermute only.
A program may use at most 256 MiB of HBM per device.

v0:
```python
import math

import jax
import jax.numpy as jnp
from jax import lax
from jax.sharding import PartitionSpec as P

SUBSTEPS = 2


time_step = 0.05
grad_coef = 1.0
well_height = 1.0
drive_coef = 2.0
conc_eq = 0.5
mech_boost = 1.0
diffusivity = 1.0
release_coef = 1.0
residual_stiff = 0.1
lame_ref = 1.0
shear_ref = 1.0
coupling = (lame_ref + shear_ref) / (shear_ref * (lame_ref + 2.0 * shear_ref))


def with_halo(cells, sides, width):
    for axis, dim in sides:
        count = lax.axis_size(axis)
        head = lax.slice_in_dim(cells, 0, width, axis=dim)
        tail = lax.slice_in_dim(cells, cells.shape[dim] - width, cells.shape[dim], axis=dim)
        cells = jnp.concatenate(
            [
                lax.ppermute(tail, axis, [(i, (i + 1) % count) for i in range(count)]),
                cells,
                lax.ppermute(head, axis, [((i + 1) % count, i) for i in range(count)]),
            ],
            axis=dim,
        )
    return cells


def product(form, left, right):
    return jnp.einsum(form, left, right, precision=lax.Precision.HIGHEST)


def lookup(labels, table, first):
    count = table.shape[0]
    values = jnp.arange(count, dtype=jnp.int32) + first
    hits = labels[None] == values[:, None, None, None]
    return jnp.sum(jnp.where(hits, table[:, None, None, None], 0.0), axis=0)


def laplace_ext(extended):
    center = extended[1:-1]
    z_sum = extended[:-2] + extended[2:]
    y_sum = jnp.roll(center, 1, 1) + jnp.roll(center, -1, 1)
    x_sum = jnp.roll(center, 1, 2) + jnp.roll(center, -1, 2)
    return z_sum + y_sum + x_sum - 6.0 * center


def advance(order_ext, conc_ext, kinetic, decay):
    order_now = order_ext[1:-1]
    conc_now = conc_ext[1:-1]
    lap_order = laplace_ext(order_ext)
    lap_conc = laplace_ext(conc_ext)
    well_grad = 2.0 * order_now * (1.0 - order_now) * (1.0 - 2.0 * order_now)
    interp_grad = 6.0 * order_now * (1.0 - order_now)
    force = (
        grad_coef * lap_order
        - well_height * well_grad
        + drive_coef * interp_grad * (conc_now - conc_eq)
    )
    order_new = order_now + kinetic * force - decay * order_now
    conc_new = (
        conc_now + time_step * diffusivity * lap_conc + release_coef * (order_now - order_new)
    )
    return (order_new, conc_new)


def dft_table(length, count, weighted):
    rows = lax.broadcasted_iota(jnp.int32, (length, count), 0)
    cols = lax.broadcasted_iota(jnp.int32, (length, count), 1)
    phase = (rows * cols % max(length, count)).astype(jnp.float32) * (
        2.0 * math.pi / max(length, count)
    )
    cosine = jnp.cos(phase)
    sine = jnp.sin(phase)
    if weighted:
        weight = jnp.where(rows == 0, 1.0, 2.0)
        cosine = cosine * weight
        sine = sine * weight
    return (cosine, sine)


def signed_waves(index, count):
    return jnp.where(index < count // 2, index, index - count).astype(jnp.float32)


def green(tau, xi_x, xi_y, xi_z, limit):
    t_xx, t_yy, t_zz, t_yz, t_xz, t_xy = tau
    v_x = t_xx * xi_x + t_xy * xi_y + t_xz * xi_z
    v_y = t_xy * xi_x + t_yy * xi_y + t_yz * xi_z
    v_z = t_xz * xi_x + t_yz * xi_y + t_zz * xi_z
    inner = xi_x * v_x + xi_y * v_y + xi_z * v_z
    wave_sq = xi_x * xi_x + xi_y * xi_y + xi_z * xi_z
    live = (wave_sq > 0.5) & (xi_x < limit)
    safe_sq = jnp.where(live, wave_sq, 1.0)
    first = jnp.where(live, 1.0 / (2.0 * shear_ref * safe_sq), 0.0)
    second = jnp.where(live, coupling / (safe_sq * safe_sq), 0.0)
    xis = (xi_x, xi_y, xi_z)
    vees = (v_x, v_y, v_z)
    pairs = ((0, 0), (1, 1), (2, 2), (1, 2), (0, 2), (0, 1))
    result = []
    for left, right in pairs:
        term = (xis[right] * vees[left] + xis[left] * vees[right]) * first - xis[left] * xis[
            right
        ] * inner * second
        result.append(term)
    return result


def plane_spectra(stress_part, cos_x, sin_x, cos_y, sin_y):
    real_part = product("czyx,xk->czyk", stress_part, cos_x)
    imag_part = -product("czyx,xk->czyk", stress_part, sin_x)
    real_y = product("czyk,yq->czqk", real_part, cos_y) + product("czyk,yq->czqk", imag_part, sin_y)
    imag_y = product("czyk,yq->czqk", imag_part, cos_y) - product("czyk,yq->czqk", real_part, sin_y)
    return jnp.stack([real_y, imag_y])


def shards(
    order_param,
    concentration,
    strain,
    grain_ids,
    seed_labels,
    grain_moduli,
    grain_mobility,
    seed_rate,
):
    lame = lookup(grain_ids, grain_moduli[0], 0)
    shear = lookup(grain_ids, grain_moduli[1], 0)
    mobility = lookup(grain_ids, grain_mobility, 0)
    rate = lookup(seed_labels, seed_rate, 1)
    trace = strain[0] + strain[1] + strain[2]
    square = (
        strain[0] * strain[0]
        + strain[1] * strain[1]
        + strain[2] * strain[2]
        + 2.0 * (strain[3] * strain[3] + strain[4] * strain[4] + strain[5] * strain[5])
    )
    energy = 0.5 * lame * trace * trace + shear * square
    mech = 1.0 + mech_boost * energy / (1.0 + energy)
    kinetic = time_step * mobility * mech
    decay = time_step * rate
    order_now = order_param
    conc_now = concentration
    for step_index in range(SUBSTEPS):
        extended = with_halo(jnp.stack([order_now, conc_now]), (("gz", 1),), 1)
        order_now, conc_now = advance(extended[0], extended[1], kinetic, decay)
    scale = order_now * order_now * (3.0 - 2.0 * order_now) + residual_stiff
    lame_now = scale * lame
    shear_now = scale * shear
    parts = []
    for comp in range(6):
        if comp < 3:
            parts.append(lame_now * trace + 2.0 * shear_now * strain[comp])
        else:
            parts.append(2.0 * shear_now * strain[comp])
    stress = jnp.stack(parts)
    planes = strain.shape[1]
    width_y = strain.shape[2]
    width_x = strain.shape[3]
    half_x = width_x // 2
    devices = lax.axis_size("gz")
    depth = planes * devices
    band = width_y // devices
    cos_x, sin_x = dft_table(width_x, half_x, False)
    cos_y, sin_y = dft_table(width_y, width_y, False)
    cos_z, sin_z = dft_table(depth, depth, False)
    back_cos_x, back_sin_x = dft_table(half_x, width_x, True)
    spectral = lax.all_to_all(
        plane_spectra(stress, cos_x, sin_x, cos_y, sin_y),
        "gz",
        split_axis=3,
        concat_axis=2,
        tiled=True,
    )
    real_z = product("cznk,zw->cwnk", spectral[0], cos_z) + product(
        "cznk,zw->cwnk", spectral[1], sin_z
    )
    imag_z = product("cznk,zw->cwnk", spectral[1], cos_z) - product(
        "cznk,zw->cwnk", spectral[0], sin_z
    )
    xi_z = signed_waves(jnp.arange(depth, dtype=jnp.int32), depth)[:, None, None]
    band_rows = lax.axis_index("gz") * band + jnp.arange(band, dtype=jnp.int32)
    xi_y = signed_waves(band_rows, width_y)[None, :, None]
    xi_x = jnp.arange(half_x, dtype=jnp.int32).astype(jnp.float32)[None, None, :]
    tau = [jnp.stack([real_z[comp], imag_z[comp]]) for comp in range(6)]
    updated = jnp.stack(green(tau, xi_x, xi_y, xi_z, float(half_x)), axis=1)
    back_real = product("cwnk,wz->cznk", updated[0], cos_z) - product(
        "cwnk,wz->cznk", updated[1], sin_z
    )
    back_imag = product("cwnk,wz->cznk", updated[1], cos_z) + product(
        "cwnk,wz->cznk", updated[0], sin_z
    )
    returned = lax.all_to_all(
        jnp.stack([back_real, back_imag]), "gz", split_axis=2, concat_axis=3, tiled=True
    )
    real_y = product("czqk,qy->czyk", returned[0], cos_y) - product(
        "czqk,qy->czyk", returned[1], sin_y
    )
    imag_y = product("czqk,qy->czyk", returned[1], cos_y) + product(
        "czqk,qy->czyk", returned[0], sin_y
    )
    increment = product("czyk,kx->czyx", real_y, back_cos_x) - product(
        "czyk,kx->czyx", imag_y, back_sin_x
    )
    increment = increment * (1.0 / float(width_x * width_y * depth))
    strain_next = strain - increment
    return (order_now, conc_now, strain_next)


def solution(mesh):
    return jax.shard_map(
        shards,
        mesh=mesh,
        in_specs=(
            P("gz", None, None),
            P("gz", None, None),
            P(None, "gz", None, None),
            P("gz", None, None),
            P("gz", None, None),
            P(),
            P(),
            P(),
        ),
        out_specs=(P("gz", None, None), P("gz", None, None), P(None, "gz", None, None)),
        check_vma=False,
    )
```

profile of v0, /device:TPU:0, one launch (start us, length us, event | category | flops | bytes accessed | tf_op | source)
XLA Modules:
  0.0 454.6 jit_solution(12239536775563765541)
XLA Ops:
  2.6 8.3 %collective-permute-start.1 = (f32[2,1,512,512]{3,2,1,0:T(8,128)S(1)}, f32[2,1,512,512]{3,2,1,0:T(8,128)S(1)}, u32[]{:S(2)}, u32[]{:S(2)}) collective-permute-start(f32[2,1,512,512]{3,2,1,0:T(8,128)S(1)} %pad_maximum_fusion.2), channel_id=1, source_target_pairs={{1,0},{2,1},{3,2},{4,3},{5,4},{6,5},{7,6},{8,7},{9,8},{10,9},{11,1... | collective-permute-start | bytes 6291464 | tf_op jit(solution)/shard_map/ppermute | solution.py:34
  15.7 5.8 %select_reduce_fusion.2 = (f32[512,512]{1,0:T(8,128)S(1)}, f32[512,512]{1,0:T(8,128)S(1)}, f32[512,512]{1,0:T(8,128)S(1)}) fusion(f32[16]{0:T(128)S(1)} %copy-done.37, s32[512,512]{1,0:T(8,128)S(1)} %bitcast.338, f32[16]{0:T(128)S(1)} %get-tuple-element.97, f32[16]{0:T(128)S(1)} %get-tuple-element.96), kind=kLoop, calls=%fused_computation.2 | loop fusion | flops 28573696 | bytes 4194496 | tf_op jit(solution)/shard_map/reduce_sum | solution.py:49
  21.6 12.8 %collective-permute-done.1 = f32[2,1,512,512]{3,2,1,0:T(8,128)S(1)} collective-permute-done((f32[2,1,512,512]{3,2,1,0:T(8,128)S(1)}, f32[2,1,512,512]{3,2,1,0:T(8,128)S(1)}, u32[]{:S(2)}, u32[]{:S(2)}) %collective-permute-start.1) | collective-permute-done | bytes 2097184 | tf_op jit(solution)/shard_map/ppermute | solution.py:34
  34.4 7.3 %collective-permute-done = f32[2,1,512,512]{3,2,1,0:T(8,128)S(1)} collective-permute-done((f32[2,1,512,512]{3,2,1,0:T(8,128)S(1)}, f32[2,1,512,512]{3,2,1,0:T(8,128)S(1)}, u32[]{:S(2)}, u32[]{:S(2)}) %collective-permute-start) | collective-permute-done | bytes 2097184 | tf_op jit(solution)/shard_map/ppermute | solution.py:32
  43.1 6.2 %fusion.61 = (f32[1,1,512,512]{3,2,1,0:T(8,128)S(1)}, f32[1,1,512,512]{3,2,1,0:T(8,128)S(1)}, f32[1,1,512,512]{3,2,1,0:T(8,128)S(1)}, f32[1,1,512,512]{3,2,0,1:T(8,128)}, f32[1,1,512,512]{3,2,1,0:T(8,128)S(1)}) fusion(f32[2,1,512,512]{3,2,1,0:T(8,128)} %copy-done.23, f32[2,1,512,512]{3,2,1,0:T(8,128)} %copy-done.24, ...), kind=kLoop, calls=%fused_computation.79 | loop fusion | flops 17301504 | bytes 30408704 | tf_op jit(solution)/shard_map/add | solution.py:74
  55.1 18.6 %collective-permute-done.3 = f32[2,1,512,512]{3,2,1,0:T(8,128)S(1)} collective-permute-done((f32[2,1,512,512]{3,2,1,0:T(8,128)S(1)}, f32[2,1,512,512]{3,2,1,0:T(8,128)S(1)}, u32[]{:S(2)}, u32[]{:S(2)}) %collective-permute-start.3) | collective-permute-done | bytes 2097184 | tf_op jit(solution)/shard_map/ppermute | solution.py:34
  73.7 7.3 %collective-permute-done.2 = f32[2,1,512,512]{3,2,1,0:T(8,128)S(1)} collective-permute-done((f32[2,1,512,512]{3,2,1,0:T(8,128)S(1)}, f32[2,1,512,512]{3,2,1,0:T(8,128)S(1)}, u32[]{:S(2)}, u32[]{:S(2)}) %collective-permute-start.2) | collective-permute-done | bytes 2097184 | tf_op jit(solution)/shard_map/ppermute | solution.py:32
  84.8 7.1 %fusion.3 = f32[6,512,256]{2,1,0:T(8,128)S(1)} fusion(f32[6,1,512,512]{3,2,0,1:T(8,128)S(1)} %fusion.95), kind=kOutput, calls=%fused_computation.11 | convolution fusion | flops 4833673216 | bytes 9437184 | tf_op jit(solution)/shard_map/czyx,xk->czyk/dot_general | solution.py:42
  91.9 7.5 %fusion.1 = f32[6,512,256]{2,1,0:T(8,128)S(1)} fusion(f32[6,1,512,512]{3,2,0,1:T(8,128)S(1)} %fusion.95), kind=kOutput, calls=%fused_computation.9 | convolution fusion | flops 4833673216 | bytes 9437184 | tf_op jit(solution)/shard_map/czyx,xk->czyk/dot_general | solution.py:42
  99.4 9.4 %fusion.92 = f32[512,6,256]{2,0,1:T(8,128)S(1)} fusion(f32[6,512,256]{2,1,0:T(8,128)S(1)} %fusion.3), kind=kOutput, calls=%fused_computation.127 | convolution fusion | flops 4835508224 | bytes 6291456 | tf_op jit(solution)/shard_map/czyk,yq->czqk/dot_general | solution.py:42
  108.7 9.1 %fusion.101 = f32[512,6,256]{2,0,1:T(8,128)S(1)} fusion(f32[6,512,256]{2,1,0:T(8,128)S(1)} %fusion.3), kind=kOutput, calls=%fused_computation.142 | convolution fusion | flops 4835508224 | bytes 6291456 | tf_op jit(solution)/shard_map/czyk,yq->czqk/dot_general | solution.py:42
  117.9 9.4 %subtract_bitcast_fusion.2 = f32[1,6,1,512,256]{4,3,1,2,0:T(8,128)S(1)} fusion(f32[512,6,256]{2,0,1:T(8,128)S(1)} %fusion.92, f32[6,512,256]{2,1,0:T(8,128)S(1)} %fusion.1), kind=kOutput, calls=%fused_computation.25 | convolution fusion | flops 4837081088 | bytes 9437184 | tf_op jit(solution)/shard_map/czyk,yq->czqk/dot_general | solution.py:42
  127.2 9.6 %add_bitcast_fusion.2 = f32[1,6,1,512,256]{4,3,1,2,0:T(8,128)S(1)} fusion(f32[512,6,256]{2,0,1:T(8,128)S(1)} %fusion.101, f32[6,512,256]{2,1,0:T(8,128)S(1)} %fusion.1), kind=kOutput, calls=%fused_computation.26 | convolution fusion | flops 4837081088 | bytes 9437184 | tf_op jit(solution)/shard_map/czyk,yq->czqk/dot_general | solution.py:42
  139.9 10.3 %copy.121 = f32[2,6,1,512,256]{4,0,2,1,3:T(2,128)} copy(f32[2,6,1,512,256]{4,3,1,2,0:T(8,128)} %pad_maximum_fusion) | data formatting | bytes 12582912 | tf_op jit(solution)/shard_map/stack | solution.py:126
  150.3 6.0 %all-to-all-start = ((f32[2,6,1,512,256]{4,0,2,1,3:T(2,128)}), f32[2,6,1,512,256]{4,0,2,1,3:T(2,128)}, u32[]{:S(2)}, u32[]{:S(2)}) async-start(f32[2,6,1,512,256]{4,0,2,1,3:T(2,128)} %copy.121), calls=%async_computation | async-start | bytes 12582912 | tf_op jit(solution)/shard_map/all_to_all | solution.py:180
  157.6 73.5 %all-to-all-done = f32[2,6,1,512,256]{4,0,2,1,3:T(2,128)} async-done(((f32[2,6,1,512,256]{4,0,2,1,3:T(2,128)}), f32[2,6,1,512,256]{4,0,2,1,3:T(2,128)}, u32[]{:S(2)}, u32[]{:S(2)}) %all-to-all-start) | async-done | bytes 6291488 | tf_op jit(solution)/shard_map/all_to_all | solution.py:180
  231.1 12.7 %fusion.275 = (f32[1,6,1,512,256]{4,0,2,1,3:T(1,128)}, f32[1,6,1,512,256]{4,0,2,1,3:T(1,128)}) fusion(f32[2,6,1,512,256]{4,0,2,1,3:T(2,128)} %all-to-all-done), kind=kLoop, calls=%fused_computation.363 | loop fusion | bytes 12582912 | tf_op jit(solution)/shard_map/slice | solution.py:187
  250.9 4.9 %fusion.23 = f32[128,6,4,256]{3,0,2,1:T(8,128)S(1)} fusion(f32[6,128,4,256]{3,0,2,1:T(8,128)S(1)} %bitcast.337), kind=kOutput, calls=%fused_computation.37 | convolution fusion | flops 1208188928 | bytes 6291456 | tf_op jit(solution)/shard_map/cznk,zw->cwnk/dot_general | solution.py:42
  261.3 5.1 %add_bitcast_fusion.1 = f32[6,128,4,256]{3,1,2,0:T(8,128)S(1)} fusion(f32[128,6,4,256]{3,0,2,1:T(8,128)S(1)} %fusion.23, f32[6,128,4,256]{3,0,2,1:T(8,128)S(1)} %bitcast.335), kind=kOutput, calls=%fused_computation.24 | convolution fusion | flops 1208975360 | bytes 9437184 | tf_op jit(solution)/shard_map/cznk,zw->cwnk/dot_general | solution.py:42
  284.7 6.7 %copy.128 = f32[2,6,128,4,256]{4,3,1,0,2:T(4,128)} copy(f32[2,6,128,4,256]{4,2,3,1,0:T(8,128)S(1)} %pad_maximum_fusion.1) | data formatting | bytes 12582912 | tf_op jit(solution)/shard_map/stack | solution.py:206
  291.4 6.7 %all-to-all-start.1 = ((f32[2,6,128,4,256]{4,3,1,0,2:T(4,128)}), f32[2,6,128,4,256]{4,3,1,0,2:T(4,128)}, u32[]{:S(2)}, u32[]{:S(2)}) async-start(f32[2,6,128,4,256]{4,3,1,0,2:T(4,128)} %copy.128), calls=%async_computation.1 | async-start | bytes 12582912 | tf_op jit(solution)/shard_map/all_to_all | solution.py:205
  302.0 5.6 %fusion.55 = (f32[1,512,512]{2,1,0:T(8,128)}, f32[1,512,512]{2,1,0:T(8,128)}) fusion(f32[2,1,512,512]{3,2,1,0:T(8,128)S(1)} %copy-done.15, f32[2,1,512,512]{3,2,1,0:T(8,128)S(1)} %copy-done.17, f32[1,511,512]{2,1,0:T(8,128)S(1)} %get-tuple-element.75, f32[1,1,512]{2,1,0:T(1,128)S(1)} %get-tuple-element.77, f32[1,1,512]{2,1,0:T(1,128)S(1)} %get-tuple-element.76, ...), kind=kLoop, calls=%fused_computation.71 | loop fusion | flops 13631488 | bytes 23068672 | tf_op jit(solution)/shard_map/add | solution.py:74
  307.5 65.6 %all-to-all-done.1 = f32[2,6,128,4,256]{4,3,1,0,2:T(4,128)} async-done(((f32[2,6,128,4,256]{4,3,1,0,2:T(4,128)}), f32[2,6,128,4,256]{4,3,1,0,2:T(4,128)}, u32[]{:S(2)}, u32[]{:S(2)}) %all-to-all-start.1) | async-done | bytes 6291488 | tf_op jit(solution)/shard_map/all_to_all | solution.py:205
  373.1 5.6 %fusion.274 = (f32[1,6,128,4,256]{4,3,1,0,2:T(4,128)S(1)}, f32[1,6,128,4,256]{4,3,1,0,2:T(4,128)}) fusion(f32[2,6,128,4,256]{4,3,1,0,2:T(4,128)} %all-to-all-done.1), kind=kLoop, calls=%fused_computation.362 | loop fusion | bytes 12582912 | tf_op jit(solution)/shard_map/slice | solution.py:208
  380.9 4.9 %reshape.2862 = f32[6,512,256]{2,1,0:T(8,128)} reshape(f32[1,6,128,4,256]{4,3,2,1,0:T(4,128)} %copy.129) | data formatting | bytes 6291456 | tf_op jit(solution)/shard_map/reshape.56
  385.8 12.7 %fusion.88 = f32[512,6,256]{2,0,1:T(8,128)} fusion(f32[6,512,256]{2,1,0:T(8,128)} %reshape.2862), kind=kOutput, calls=%fused_computation.123 | convolution fusion | flops 4835508224 | bytes 6291456 | tf_op jit(solution)/shard_map/czqk,qy->czyk/dot_general | solution.py:42
  398.5 11.4 %fusion.98 = f32[512,6,256]{2,0,1:T(8,128)} fusion(f32[6,512,256]{2,1,0:T(8,128)S(1)} %copy-done.20), kind=kOutput, calls=%fused_computation.139 | convolution fusion | flops 4835508224 | bytes 6291456 | tf_op jit(solution)/shard_map/czqk,qy->czyk/dot_general | solution.py:42
  412.1 5.0 %reshape.2863 = f32[6,512,256]{2,1,0:T(8,128)} reshape(f32[1,6,128,4,256]{4,3,2,1,0:T(4,128)} %copy.130) | data formatting | bytes 6291456 | tf_op jit(solution)/shard_map/reshape.61
  417.2 11.0 %fusion.96 = f32[512,6,256]{2,0,1:T(8,128)S(1)} fusion(f32[6,512,256]{2,1,0:T(8,128)} %reshape.2863), kind=kOutput, calls=%fused_computation.137 | convolution fusion | flops 4835508224 | bytes 6291456 | tf_op jit(solution)/shard_map/czqk,qy->czyk/dot_general | solution.py:42
  428.2 9.2 %fusion.90 = f32[512,6,256]{2,0,1:T(8,128)S(1)} fusion(f32[6,512,256]{2,1,0:T(8,128)S(1)} %copy-done.21), kind=kOutput, calls=%fused_computation.125 | convolution fusion | flops 4835508224 | bytes 6291456 | tf_op jit(solution)/shard_map/czqk,qy->czyk/dot_general | solution.py:42
  437.5 7.5 %fusion.5 = f32[6,512,512]{2,1,0:T(8,128)S(1)} fusion(f32[512,6,256]{2,0,1:T(8,128)S(1)} %fusion.96, f32[512,6,256]{2,0,1:T(8,128)S(1)} %copy-done.22, f32[256]{0:T(256)S(1)} %compare_select_fusion.2), kind=kOutput, calls=%fused_computation.15 | convolution fusion | flops 4834590720 | bytes 12583936 | tf_op jit(solution)/shard_map/czyk,kx->czyx/dot_general | solution.py:42
  445.0 9.1 %fusion = f32[6,1,512,512]{3,2,1,0:T(8,128)} fusion(f32[6,512,512]{2,1,0:T(8,128)S(1)} %fusion.5, f32[512,6,256]{2,0,1:T(8,128)S(1)} %copy-done.19, f32[512,6,256]{2,0,1:T(8,128)S(1)} %fusion.90, f32[256]{0:T(256)S(1)} %compare_select_fusion.2, f32[6,1,512,512]{3,2,1,0:T(8,128)S(1)} %bitcast.331), kind=kOutput, calls=%fused_computation.8 | convolution fusion | flops 4839309312 | bytes 25166848 | tf_op jit(solution)/shard_map/czyk,kx->czyx/dot_general | solution.py:42
  (147 shorter events, 60.6 us)
Async XLA Ops:
  0.6 10.2 %copy-start = (f32[1,512,512]{2,1,0:T(8,128)S(1)}, f32[1,512,512]{2,1,0:T(8,128)}, u32[]{:S(2)}) copy-start(f32[1,512,512]{2,1,0:T(8,128)} %param.9) | copy-start | bytes 3145732
  0.6 10.2 %copy-start.1 = (f32[1,512,512]{2,1,0:T(8,128)S(1)}, f32[1,512,512]{2,1,0:T(8,128)}, u32[]{:S(2)}) copy-start(f32[1,512,512]{2,1,0:T(8,128)} %param.8) | copy-start | bytes 3145732
  0.7 11.4 %copy-start.26 = (s32[1,512,512]{2,1,0:T(8,128)S(1)}, s32[1,512,512]{2,1,0:T(8,128)}, u32[]{:S(2)}) copy-start(s32[1,512,512]{2,1,0:T(8,128)} %param.12) | copy-start | bytes 3145732
  0.7 11.3 %copy-start.38 = (f32[8]{0:T(128)S(1)}, f32[8]{0:T(128)}, u32[]{:S(2)}) copy-start(f32[8]{0:T(128)} %param.15) | copy-start | bytes 100
  2.5 10.4 %copy-start.36 = (f32[2,16]{1,0:T(2,128)S(1)}, f32[2,16]{1,0:T(2,128)}, u32[]{:S(2)}) copy-start(f32[2,16]{1,0:T(2,128)} %param.13) | copy-start | bytes 388
  2.6 31.8 %collective-permute-start.1 = (f32[2,1,512,512]{3,2,1,0:T(8,128)S(1)}, f32[2,1,512,512]{3,2,1,0:T(8,128)S(1)}, u32[]{:S(2)}, u32[]{:S(2)}) collective-permute-start(f32[2,1,512,512]{3,2,1,0:T(8,128)S(1)} %pad_maximum_fusion.2), channel_id=1, source_target_pairs={{1,0},{2,1},{3,2},{4,3},{5,4},{6,5},{7,6},{8,7},{9,8},{10,9},{11,1... | collective-permute-start | bytes 6291464 | tf_op jit(solution)/shard_map/ppermute | solution.py:34
  10.8 30.9 %collective-permute-start = (f32[2,1,512,512]{3,2,1,0:T(8,128)S(1)}, f32[2,1,512,512]{3,2,1,0:T(8,128)S(1)}, u32[]{:S(2)}, u32[]{:S(2)}) collective-permute-start(f32[2,1,512,512]{3,2,1,0:T(8,128)S(1)} %pad_maximum_fusion.2), channel_id=1, source_target_pairs={{0,1},{1,2},{2,3},{3,4},{4,5},{5,6},{6,7},{7,8},{8,9},{9,10},{10,1... | collective-permute-start | bytes 6291464 | tf_op jit(solution)/shard_map/ppermute | solution.py:32
  12.9 68.1 %copy-start.6 = (f32[512,512]{1,0:T(8,128)}, f32[512,512]{1,0:T(8,128)S(1)}, u32[]{:S(2)}) copy-start(f32[512,512]{1,0:T(8,128)S(1)} %select_reduce_fusion.3) | copy-start | bytes 3145732
  13.0 30.1 %slice-start = ((s8[6291456]{0:T(1024)(128)(4,1)}), s8[4194304]{0:T(1024)(128)(4,1)S(1)}, s32[]{:S(2)}) async-start(s8[6291456]{0:T(1024)(128)(4,1)} %bitcast.326), calls=%async_computation.2 | async-start | bytes 8388608
  13.5 29.6 %slice-start.1 = ((s8[6291456]{0:T(1024)(128)(4,1)}), s8[2097152]{0:T(1024)(128)(4,1)S(1)}, s32[]{:S(2)}) async-start(s8[6291456]{0:T(1024)(128)(4,1)} %bitcast.326), calls=%async_computation.3 | async-start | bytes 4194304
  21.5 27.7 %copy-start.10 = (f32[512,512]{1,0:T(8,128)}, f32[512,512]{1,0:T(8,128)S(1)}, u32[]{:S(2)}) copy-start(f32[512,512]{1,0:T(8,128)S(1)} %get-tuple-element.21) | copy-start | bytes 3145732
  21.5 59.5 %copy-start.2 = (f32[512,512]{1,0:T(8,128)}, f32[512,512]{1,0:T(8,128)S(1)}, u32[]{:S(2)}) copy-start(f32[512,512]{1,0:T(8,128)S(1)} %get-tuple-element.22) | copy-start | bytes 3145732
  21.5 59.5 %copy-start.4 = (f32[512,512]{1,0:T(8,128)}, f32[512,512]{1,0:T(8,128)S(1)}, u32[]{:S(2)}) copy-start(f32[512,512]{1,0:T(8,128)S(1)} %get-tuple-element.23) | copy-start | bytes 3145732
  34.4 7.3 %copy-start.23 = (f32[2,1,512,512]{3,2,1,0:T(8,128)}, f32[2,1,512,512]{3,2,1,0:T(8,128)S(1)}, u32[]{:S(2)}) copy-start(f32[2,1,512,512]{3,2,1,0:T(8,128)S(1)} %collective-permute-done.1) | copy-start | bytes 6291460
  49.2 31.9 %copy-start.12 = (f32[1,1,512,512]{3,2,1,0:T(8,128)}, f32[1,1,512,512]{3,2,1,0:T(8,128)S(1)}, u32[]{:S(2)}) copy-start(f32[1,1,512,512]{3,2,1,0:T(8,128)S(1)} %get-tuple-element.37) | copy-start | bytes 3145732
  49.4 24.3 %collective-permute-start.3 = (f32[2,1,512,512]{3,2,1,0:T(8,128)S(1)}, f32[2,1,512,512]{3,2,1,0:T(8,128)S(1)}, u32[]{:S(2)}, u32[]{:S(2)}) collective-permute-start(f32[2,1,512,512]{3,2,1,0:T(8,128)S(1)} %pad_maximum_fusion.3), channel_id=1, source_target_pairs={{1,0},{2,1},{3,2},{4,3},{5,4},{6,5},{7,6},{8,7},{9,8},{10,9},{11,1... | collective-permute-start | bytes 6291464 | tf_op jit(solution)/shard_map/ppermute | solution.py:34
  50.2 30.9 %collective-permute-start.2 = (f32[2,1,512,512]{3,2,1,0:T(8,128)S(1)}, f32[2,1,512,512]{3,2,1,0:T(8,128)S(1)}, u32[]{:S(2)}, u32[]{:S(2)}) collective-permute-start(f32[2,1,512,512]{3,2,1,0:T(8,128)S(1)} %pad_maximum_fusion.3), channel_id=1, source_target_pairs={{0,1},{1,2},{2,3},{3,4},{4,5},{5,6},{6,7},{7,8},{8,9},{9,10},{10,1... | collective-permute-start | bytes 6291464 | tf_op jit(solution)/shard_map/ppermute | solution.py:32
  73.7 9.7 %copy-start.14 = (f32[2,1,512,512]{3,2,1,0:T(8,128)}, f32[2,1,512,512]{3,2,1,0:T(8,128)S(1)}, u32[]{:S(2)}) copy-start(f32[2,1,512,512]{3,2,1,0:T(8,128)S(1)} %collective-permute-done.3) | copy-start | bytes 6291460
  150.3 80.8 %all-to-all-start = ((f32[2,6,1,512,256]{4,0,2,1,3:T(2,128)}), f32[2,6,1,512,256]{4,0,2,1,3:T(2,128)}, u32[]{:S(2)}, u32[]{:S(2)}) async-start(f32[2,6,1,512,256]{4,0,2,1,3:T(2,128)} %copy.121), calls=%async_computation | async-start | bytes 12582912 | tf_op jit(solution)/shard_map/all_to_all | solution.py:180
  250.9 4.9 %copy-start.8 = (f32[1,6,1,512,256]{4,0,2,1,3:T(1,128)S(1)}, f32[1,6,1,512,256]{4,0,2,1,3:T(1,128)}, u32[]{:S(2)}) copy-start(f32[1,6,1,512,256]{4,0,2,1,3:T(1,128)} %get-tuple-element.40) | copy-start | bytes 9437188
  291.4 7.6 %copy-start.18 = (f32[1,1,512,512]{3,2,0,1:T(8,128)S(1)}, f32[1,1,512,512]{3,2,0,1:T(8,128)}, u32[]{:S(2)}) copy-start(f32[1,1,512,512]{3,2,0,1:T(8,128)} %get-tuple-element.36) | copy-start | bytes 3145732
  291.4 81.7 %all-to-all-start.1 = ((f32[2,6,128,4,256]{4,3,1,0,2:T(4,128)}), f32[2,6,128,4,256]{4,3,1,0,2:T(4,128)}, u32[]{:S(2)}, u32[]{:S(2)}) async-start(f32[2,6,128,4,256]{4,3,1,0,2:T(4,128)} %copy.128), calls=%async_computation.1 | async-start | bytes 12582912 | tf_op jit(solution)/shard_map/all_to_all | solution.py:205
  298.6 3.4 copy-start.11
  298.6 3.4 copy-start.28
  298.6 3.3 copy-start.29
  385.8 12.7 %copy-start.20 = (f32[6,512,256]{2,1,0:T(8,128)S(1)}, f32[6,512,256]{2,1,0:T(8,128)}, u32[]{:S(2)}) copy-start(f32[6,512,256]{2,1,0:T(8,128)} %reshape.2862) | copy-start | bytes 9437188
  398.5 11.4 %copy-start.9 = (f32[1,6,128,4,256]{4,3,1,0,2:T(4,128)S(1)}, f32[1,6,128,4,256]{4,3,1,0,2:T(4,128)}, u32[]{:S(2)}) copy-start(f32[1,6,128,4,256]{4,3,1,0,2:T(4,128)} %get-tuple-element.39) | copy-start | bytes 9437188
  417.2 11.0 %copy-start.21 = (f32[6,512,256]{2,1,0:T(8,128)S(1)}, f32[6,512,256]{2,1,0:T(8,128)}, u32[]{:S(2)}) copy-start(f32[6,512,256]{2,1,0:T(8,128)} %reshape.2863) | copy-start | bytes 9437188
  417.2 20.3 %copy-start.22 = (f32[512,6,256]{2,0,1:T(8,128)S(1)}, f32[512,6,256]{2,0,1:T(8,128)}, u32[]{:S(2)}) copy-start(f32[512,6,256]{2,0,1:T(8,128)} %fusion.88) | copy-start | bytes 9437188
  428.2 16.8 %slice-start.2 = ((s8[6291456]{0:T(1024)(128)(4,1)}), s8[4194304]{0:T(1024)(128)(4,1)S(1)}, s32[]{:S(2)}) async-start(s8[6291456]{0:T(1024)(128)(4,1)} %bitcast.330), calls=%async_computation.4 | async-start | bytes 8388608
  437.4 7.5 %slice-start.3 = ((s8[6291456]{0:T(1024)(128)(4,1)}), s8[2097152]{0:T(1024)(128)(4,1)S(1)}, s32[]{:S(2)}) async-start(s8[6291456]{0:T(1024)(128)(4,1)} %bitcast.330), calls=%async_computation.5 | async-start | bytes 4194304
  437.5 7.5 %copy-start.19 = (f32[512,6,256]{2,0,1:T(8,128)S(1)}, f32[512,6,256]{2,0,1:T(8,128)}, u32[]{:S(2)}) copy-start(f32[512,6,256]{2,0,1:T(8,128)} %fusion.98) | copy-start | bytes 9437188
  (17 other events, 27.8 us)
where the time goes:
time: 463 us; the launch traced here: 455 us
  waiting for transfers between devices  185 us (40%)
  matrix products  145 us (31%)
  local copies, waits for them, and re-layouts  67.8 us (15%)
  other arithmetic  32.6 us (7%)
  starting transfers between devices  21.7 us (5%)
    dot_general x20, matrix products, product(): return jnp.einsum(form, left, right, precision=lax.Precision.HIGHEST)  145 us
    all_to_all x1, waiting for transfers between devices, shards(): lax.all_to_all(plane_spectra(stress, cos_x, sin_x, cos_y, sin_y), 'gz', s...  73.5 us
    all_to_all x1, waiting for transfers between devices, shards(): lax.all_to_all(jnp.stack([back_real, back_imag]), 'gz', split_axis=2, con...  65.6 us
    ppermute x2, waiting for transfers between devices, with_halo(): lax.ppermute(head, axis, [((i + 1) % count, i) for i in range(count)])  31.4 us
    ppermute x2, waiting for transfers between devices, with_halo(): lax.ppermute(tail, axis, [(i, (i + 1) % count) for i in range(count)])  14.7 us
    slice x1, local copies, waits for them, and re-layouts, shards(): spectral[0]  12.7 us
    add x2, other arithmetic, advance(): conc_now + time_step * diffusivity * lap_conc  11.7 us
    another operation x1, local copies, waits for them, and re-layouts, plane_spectra(): return jnp.stack([real_y, imag_y])  10.3 us
  transfers between devices with their start and end apart: 6, of which 6 were waited for; matrix products, arithmetic and copies ran while one was open for 5% of the time, Pallas kernels for 0%

commit v1 on v0

v1 whole, which is shorter than its diff:
```python
import functools
import math

import jax
import jax.numpy as jnp
from jax import lax
from jax.experimental import pallas as pl
from jax.experimental.pallas import tpu as pltpu
from jax.sharding import PartitionSpec as P

SUBSTEPS = 2
N = 512
HALF = 256
LANE = 128
DEPTH = 128
COMPS = 6
RADIX = 4
ROWS = COMPS * RADIX * 2
BLOCK = LANE * ROWS

time_step = 0.05
grad_coef = 1.0
well_height = 1.0
drive_coef = 2.0
conc_eq = 0.5
mech_boost = 1.0
diffusivity = 1.0
release_coef = 1.0
residual_stiff = 0.1
lame_ref = 1.0
shear_ref = 1.0
coupling = (lame_ref + shear_ref) / (shear_ref * (lame_ref + 2.0 * shear_ref))

f32 = jnp.float32
bf16 = jnp.bfloat16
VMEM_LIMIT = 40 * 1024 * 1024


def params(dims=1):
    return pltpu.CompilerParams(
        dimension_semantics=("arbitrary",) * dims, vmem_limit_bytes=VMEM_LIMIT
    )


def split(value):
    high = value.astype(bf16)
    low = (value - high.astype(f32)).astype(bf16)
    return high, low


def mul(left, right):
    return lax.dot_general(
        left, right, (((1,), (0,)), ((), ())), preferred_element_type=f32
    )


def table_times(table, value):
    high, low = split(value)
    return mul(table[0], high) + mul(table[0], low) + mul(table[1], high)


def times_table(value, table):
    high, low = split(value)
    return mul(high, table[0]) + mul(low, table[0]) + mul(high, table[1])


def unit_cos(index):
    wrapped = ((index + 256) & 511) - 256
    angle = (128 - jnp.abs(wrapped)).astype(f32) * (2.0 * math.pi / 512.0)
    square = angle * angle
    poly = 1.0 / 6227020800.0
    for power in (39916800.0, 362880.0, 5040.0, 120.0, 6.0):
        poly = 1.0 / power - square * poly
    return angle * (1.0 - square * poly)


def table_body(txf_ref, mq_ref, mz_ref, mqi_ref, txi_ref):
    rows = lax.broadcasted_iota(jnp.int32, (HALF, HALF), 0)
    cols = lax.broadcasted_iota(jnp.int32, (HALF, HALF), 1)
    row_low = rows & 127
    row_top = rows >> 7
    col_low = cols & 127
    col_top = cols >> 7

    def put(ref, slot, value):
        high, low = split(value)
        ref[slot, 0] = high
        ref[slot, 1] = low

    turn = (row_top - col_top) * 128
    for parity in range(2):
        wave = 2 * col_low + parity
        put(txf_ref, parity, unit_cos(rows * wave + col_top * 128))
        wave = 2 * row_low + parity
        weight = jnp.where(wave == 0, 1.0, 2.0) * (1.0 / float(N * N * DEPTH))
        put(txi_ref, parity, unit_cos(wave * cols + row_top * 128) * weight)
    for rest in range(RADIX):
        put(mq_ref, rest, unit_cos((4 * row_low + rest) * col_low + turn))
        put(mqi_ref, rest, unit_cos((4 * col_low + rest) * row_low - turn))
    put(mz_ref, 0, unit_cos(4 * row_low * col_low + turn))
    put(mz_ref, 1, unit_cos(4 * row_low * col_low - turn))


def make_tables():
    shape = lambda count: jax.ShapeDtypeStruct((count, 2, HALF, HALF), bf16)
    return pl.pallas_call(
        table_body,
        out_shape=(shape(2), shape(4), shape(2), shape(4), shape(2)),
        compiler_params=pltpu.CompilerParams(vmem_limit_bytes=VMEM_LIMIT),
        name="tables",
    )()


TILE = 128
STRIP = 16


def coef_body(moduli, mobility, rates, grain_ref, label_ref, strain_ref, lame_ref_, shear_ref_, kin_ref, dec_ref):
    def strip(step, carry):
        where = pl.ds(pl.multiple_of(step * STRIP, STRIP), STRIP)
        grain = grain_ref[where, :]
        label = label_ref[where, :]
        lame = jnp.zeros(grain.shape, f32)
        shear = jnp.zeros(grain.shape, f32)
        mob = jnp.zeros(grain.shape, f32)
        rate = jnp.zeros(grain.shape, f32)
        for index in range(mobility.shape[0]):
            hit = grain == index
            lame = jnp.where(hit, moduli[0, index], lame)
            shear = jnp.where(hit, moduli[1, index], shear)
            mob = jnp.where(hit, mobility[index], mob)
        for index in range(rates.shape[0]):
            rate = jnp.where(label == index + 1, rates[index], rate)
        parts = [strain_ref[comp, where, :] for comp in range(COMPS)]
        trace = parts[0] + parts[1] + parts[2]
        square = (
            parts[0] * parts[0]
            + parts[1] * parts[1]
            + parts[2] * parts[2]
            + 2.0 * (parts[3] * parts[3] + parts[4] * parts[4] + parts[5] * parts[5])
        )
        energy = 0.5 * lame * trace * trace + shear * square
        mech = 1.0 + mech_boost * energy / (1.0 + energy)
        lame_ref_[where, :] = lame
        shear_ref_[where, :] = shear
        kin_ref[where, :] = time_step * mob * mech
        dec_ref[where, :] = time_step * rate
        return carry

    lax.fori_loop(0, TILE // STRIP, strip, 0)


def coefficients(moduli, mobility, rates, grain, label, strain):
    plane = jax.ShapeDtypeStruct((N, N), f32)
    block = pl.BlockSpec((TILE, N), lambda i: (i, 0))
    smem = pl.BlockSpec(memory_space=pltpu.SMEM)
    return pl.pallas_call(
        coef_body,
        grid=(N // TILE,),
        in_specs=[smem, smem, smem, block, block, pl.BlockSpec((COMPS, TILE, N), lambda i: (0, i, 0))],
        out_specs=[block] * 4,
        out_shape=[plane] * 4,
        compiler_params=params(),
        name="coefficients",
    )(moduli, mobility, rates, grain, label, strain)


def planar_sum(ref, start):
    center = ref[pl.ds(start, STRIP), :]
    before = ref[pl.ds(pl.multiple_of((start + N - 8) & (N - 1), 8), 8), :]
    after = ref[pl.ds(pl.multiple_of((start + STRIP) & (N - 1), 8), 8), :]
    tall = jnp.concatenate([before, center, after], axis=0)
    height = STRIP + 16
    above = pltpu.roll(tall, 1, 0)[8 : 8 + STRIP]
    below = pltpu.roll(tall, height - 1, 0)[8 : 8 + STRIP]
    sides = pltpu.roll(center, 1, 1) + pltpu.roll(center, N - 1, 1)
    return center, (above + below) + sides


def step_body(p_ref, c_ref, pu_ref, pd_ref, cu_ref, cd_ref, kin_ref, dec_ref, p_out, c_out):
    base = pl.program_id(0) * TILE

    def strip(step, carry):
        local = pl.multiple_of(step * STRIP, STRIP)
        where = pl.ds(local, STRIP)
        start = pl.multiple_of(base + local, STRIP)
        order_now, order_sum = planar_sum(p_ref, start)
        conc_now, conc_sum = planar_sum(c_ref, start)
        lap_order = order_sum + (pu_ref[where, :] + pd_ref[where, :]) - 6.0 * order_now
        lap_conc = conc_sum + (cu_ref[where, :] + cd_ref[where, :]) - 6.0 * conc_now
        slope = order_now * (1.0 - order_now)
        well_grad = 2.0 * slope * (1.0 - 2.0 * order_now)
        force = (
            grad_coef * lap_order
            - well_height * well_grad
            + drive_coef * 6.0 * slope * (conc_now - conc_eq)
        )
        order_new = order_now + kin_ref[where, :] * force - dec_ref[where, :] * order_now
        p_out[where, :] = order_new
        c_out[where, :] = (
            conc_now + time_step * diffusivity * lap_conc + release_coef * (order_now - order_new)
        )
        return carry

    lax.fori_loop(0, TILE // STRIP, strip, 0)


def substep(order_now, conc_now, halos, kinetic, decay):
    plane = jax.ShapeDtypeStruct((N, N), f32)
    whole = pl.BlockSpec((N, N), lambda i: (0, 0))
    block = pl.BlockSpec((TILE, N), lambda i: (i, 0))
    return pl.pallas_call(
        step_body,
        grid=(N // TILE,),
        in_specs=[whole, whole] + [block] * 6,
        out_specs=[block] * 2,
        out_shape=[plane] * 2,
        compiler_params=params(),
        name="substep",
    )(order_now, conc_now, *halos, kinetic, decay)


def forward_y(scratch, mq_ref, out_ref, pair):
    first = pair * 2
    mixed = []
    for comp in (0, 1):
        blocks_r = [scratch[first + comp, pl.ds(128 * j, 128), pl.ds(0, 128)] for j in range(4)]
        blocks_i = [scratch[first + comp, pl.ds(128 * j, 128), pl.ds(128, 128)] for j in range(4)]
        er0, er1 = blocks_r[0] + blocks_r[2], blocks_r[0] - blocks_r[2]
        or0, or1 = blocks_r[1] + blocks_r[3], blocks_r[1] - blocks_r[3]
        ei0, ei1 = blocks_i[0] + blocks_i[2], blocks_i[0] - blocks_i[2]
        oi0, oi1 = blocks_i[1] + blocks_i[3], blocks_i[1] - blocks_i[3]
        mixed.append(
            (
                (er0 + or0, ei0 + oi0),
                (er1 + oi1, ei1 - or1),
                (er0 - or0, ei0 - oi0),
                (er1 - oi1, ei1 + or1),
            )
        )
    for rest in range(RADIX):
        real = jnp.concatenate([mixed[0][rest][0], mixed[1][rest][0]], axis=1)
        imag = jnp.concatenate([mixed[0][rest][1], mixed[1][rest][1]], axis=1)
        value = jnp.concatenate([real, imag], axis=0)
        result = table_times((mq_ref[rest, 0], mq_ref[rest, 1]), value)
        for comp in (0, 1):
            row = ((first + comp) * RADIX + rest) * 2
            lanes = slice(128 * comp, 128 * comp + 128)
            out_ref[pl.ds(row, 128, stride=ROWS), :] = result[:128, lanes]
            out_ref[pl.ds(row + 1, 128, stride=ROWS), :] = result[128:, lanes]


XTILES = N // TILE


def even_body(p_ref, lame_in, shear_in, strain_ref, txf_ref, mq_ref, out_ref, odd_ref, scratch):
    step = pl.program_id(0)

    @pl.when(step < XTILES)
    def _():
        order = p_ref[...]
        scale = order * order * (3.0 - 2.0 * order) + residual_stiff
        shear_now = 2.0 * (scale * shear_in[...])
        lame_now = scale * lame_in[...]
        spread = lame_now * (strain_ref[0] + strain_ref[1] + strain_ref[2])
        where = pl.ds(pl.multiple_of(step * TILE, TILE), TILE)
        for comp in range(COMPS):
            part = shear_now * strain_ref[comp]
            if comp < 3:
                part = part + spread
            odd_ref[comp] = part[:, :HALF] - part[:, HALF:]
            folded = part[:, :HALF] + part[:, HALF:]
            scratch[comp, where, :] = times_table(folded, (txf_ref[0, 0], txf_ref[0, 1]))

    @pl.when(step == XTILES)
    def _():
        for pair in range(3):
            forward_y(scratch, mq_ref, out_ref, pair)


def forward_even(order, lame, shear, strain, txf, mq):
    last = XTILES - 1
    block = pl.BlockSpec((TILE, N), lambda i: (jnp.minimum(i, last), 0))
    return pl.pallas_call(
        even_body,
        grid=(XTILES + 1,),
        in_specs=[
            block,
            block,
            block,
            pl.BlockSpec((COMPS, TILE, N), lambda i: (0, jnp.minimum(i, last), 0)),
            pl.BlockSpec((1, 2, HALF, HALF), lambda i: (0, 0, 0, 0)),
            pl.BlockSpec((4, 2, HALF, HALF), lambda i: (0, 0, 0, 0)),
        ],
        out_specs=[
            pl.BlockSpec((BLOCK, LANE), lambda i: (0, 0)),
            pl.BlockSpec((COMPS, TILE, HALF), lambda i: (0, jnp.minimum(i, last), 0)),
        ],
        out_shape=[
            jax.ShapeDtypeStruct((BLOCK, LANE), f32),
            jax.ShapeDtypeStruct((COMPS, N, HALF), f32),
        ],
        scratch_shapes=[pltpu.VMEM((COMPS, N, HALF), f32)],
        compiler_params=params(),
        name="forward_even",
    )(order, lame, shear, strain, txf, mq)


def odd_body(odd_ref, txf_ref, mq_ref, out_ref, scratch):
    for comp in (0, 1):
        scratch[comp] = times_table(odd_ref[comp], (txf_ref[0, 0], txf_ref[0, 1]))
    pair = pl.program_id(0)
    first = pair * 2
    mixed = []
    for comp in (0, 1):
        blocks_r = [scratch[comp, pl.ds(128 * j, 128), pl.ds(0, 128)] for j in range(4)]
        blocks_i = [scratch[comp, pl.ds(128 * j, 128), pl.ds(128, 128)] for j in range(4)]
        er0, er1 = blocks_r[0] + blocks_r[2], blocks_r[0] - blocks_r[2]
        or0, or1 = blocks_r[1] + blocks_r[3], blocks_r[1] - blocks_r[3]
        ei0, ei1 = blocks_i[0] + blocks_i[2], blocks_i[0] - blocks_i[2]
        oi0, oi1 = blocks_i[1] + blocks_i[3], blocks_i[1] - blocks_i[3]
        mixed.append(
            (
                (er0 + or0, ei0 + oi0),
                (er1 + oi1, ei1 - or1),
                (er0 - or0, ei0 - oi0),
                (er1 - oi1, ei1 + or1),
            )
        )
    for rest in range(RADIX):
        real = jnp.concatenate([mixed[0][rest][0], mixed[1][rest][0]], axis=1)
        imag = jnp.concatenate([mixed[0][rest][1], mixed[1][rest][1]], axis=1)
        value = jnp.concatenate([real, imag], axis=0)
        result = table_times((mq_ref[rest, 0], mq_ref[rest, 1]), value)
        for comp in (0, 1):
            row = ((first + comp) * RADIX + rest) * 2
            lanes = slice(128 * comp, 128 * comp + 128)
            out_ref[pl.ds(row, 128, stride=ROWS), :] = result[:128, lanes]
            out_ref[pl.ds(row + 1, 128, stride=ROWS), :] = result[128:, lanes]


def forward_odd(odd, txf, mq):
    return pl.pallas_call(
        odd_body,
        grid=(3,),
        in_specs=[
            pl.BlockSpec((2, N, HALF), lambda i: (i, 0, 0)),
            pl.BlockSpec((1, 2, HALF, HALF), lambda i: (1, 0, 0, 0)),
            pl.BlockSpec((4, 2, HALF, HALF), lambda i: (0, 0, 0, 0)),
        ],
        out_specs=pl.BlockSpec((BLOCK, LANE), lambda i: (0, 0)),
        out_shape=jax.ShapeDtypeStruct((BLOCK, LANE), f32),
        scratch_shapes=[pltpu.VMEM((2, N, HALF), f32)],
        compiler_params=params(),
        name="forward_odd",
    )(odd, txf, mq)


def middle_body(band_ref, in_ref, mz_ref, out_ref, *, parity):
    rest = pl.program_id(0)
    forward = (mz_ref[0, 0], mz_ref[0, 1])
    backward = (mz_ref[1, 0], mz_ref[1, 1])
    tau_r, tau_i = [], []
    for pair in range(3):
        reals, imags = [], []
        for comp in (0, 1):
            row = (pair * 2 + comp) * RADIX * 2 + rest * 2
            reals.append(in_ref[pl.ds(row, 128, stride=ROWS), :])
            imags.append(in_ref[pl.ds(row + 1, 128, stride=ROWS), :])
        value = jnp.concatenate(
            [jnp.concatenate(reals, axis=1), jnp.concatenate(imags, axis=1)], axis=0
        )
        result = table_times(forward, value)
        for comp in (0, 1):
            lanes = slice(128 * comp, 128 * comp + 128)
            tau_r.append(result[:128, lanes])
            tau_i.append(result[128:, lanes])
    shape = (DEPTH, LANE)
    depth_index = lax.broadcasted_iota(jnp.int32, shape, 0)
    xi_z = jnp.where(depth_index < DEPTH // 2, depth_index, depth_index - DEPTH).astype(f32)
    xi_x = (2 * lax.broadcasted_iota(jnp.int32, shape, 1) + parity).astype(f32)
    wave_y = band_ref[0] * RADIX + rest
    xi_y = jnp.where(wave_y < N // 2, wave_y, wave_y - N).astype(f32)
    wave_sq = xi_x * xi_x + xi_y * xi_y + xi_z * xi_z
    live = (wave_sq > 0.5) & (xi_x < float(HALF))
    safe = jnp.where(live, wave_sq, 1.0)
    inverse = 1.0 / safe
    first = jnp.where(live, (0.5 / shear_ref) * inverse, 0.0)
    second = jnp.where(live, (0.5 * coupling) * (inverse * inverse), 0.0)
    grids = []
    for tau in (tau_r, tau_i):
        t_xx, t_yy, t_zz, t_yz, t_xz, t_xy = tau
        v_x = t_xx * xi_x + t_xy * xi_y + t_xz * xi_z
        v_y = t_xy * xi_x + t_yy * xi_y + t_yz * xi_z
        v_z = t_xz * xi_x + t_yz * xi_y + t_zz * xi_z
        inner = (xi_x * v_x + xi_y * v_y + xi_z * v_z) * second
        h_x = v_x * first - xi_x * inner
        h_y = v_y * first - xi_y * inner
        h_z = v_z * first - xi_z * inner
        grids.append(
            (
                2.0 * xi_x * h_x,
                2.0 * xi_y * h_y,
                2.0 * xi_z * h_z,
                xi_z * h_y + xi_y * h_z,
                xi_z * h_x + xi_x * h_z,
                xi_y * h_x + xi_x * h_y,
            )
        )
    for pair in range(3):
        real = jnp.concatenate([grids[0][pair * 2], grids[0][pair * 2 + 1]], axis=1)
        imag = jnp.concatenate([grids[1][pair * 2], grids[1][pair * 2 + 1]], axis=1)
        result = table_times(backward, jnp.concatenate([real, imag], axis=0))
        for comp in (0, 1):
            row = (pair * 2 + comp) * RADIX * 2 + rest * 2
            lanes = slice(128 * comp, 128 * comp + 128)
            out_ref[pl.ds(row, 128, stride=ROWS), :] = result[:128, lanes]
            out_ref[pl.ds(row + 1, 128, stride=ROWS), :] = result[128:, lanes]


def middle(band, received, mz, parity):
    return pl.pallas_call(
        functools.partial(middle_body, parity=parity),
        grid=(RADIX,),
        in_specs=[
            pl.BlockSpec(memory_space=pltpu.SMEM),
            pl.BlockSpec((BLOCK, LANE), lambda i: (0, 0)),
            pl.BlockSpec((2, 2, HALF, HALF), lambda i: (0, 0, 0, 0)),
        ],
        out_specs=pl.BlockSpec((BLOCK, LANE), lambda i: (0, 0)),
        out_shape=jax.ShapeDtypeStruct((BLOCK, LANE), f32),
        compiler_params=params(),
        name="middle_even" if parity == 0 else "middle_odd",
    )(band, received, mz)


def inverse_y(in_ref, mqi_ref, pair):
    blocks = []
    for rest in range(RADIX):
        reals, imags = [], []
        for comp in (0, 1):
            row = (pair * 2 + comp) * RADIX * 2 + rest * 2
            reals.append(in_ref[pl.ds(row, 128, stride=ROWS), :])
            imags.append(in_ref[pl.ds(row + 1, 128, stride=ROWS), :])
        value = jnp.concatenate(
            [jnp.concatenate(reals, axis=1), jnp.concatenate(imags, axis=1)], axis=0
        )
        result = table_times((mqi_ref[rest, 0], mqi_ref[rest, 1]), value)
        blocks.append((result[:128], result[128:]))
    er0, er1 = blocks[0][0] + blocks[2][0], blocks[0][0] - blocks[2][0]
    ei0, ei1 = blocks[0][1] + blocks[2][1], blocks[0][1] - blocks[2][1]
    or0, or1 = blocks[1][0] + blocks[3][0], blocks[1][0] - blocks[3][0]
    oi0, oi1 = blocks[1][1] + blocks[3][1], blocks[1][1] - blocks[3][1]
    return (
        (er0 + or0, ei0 + oi0),
        (er1 - oi1, ei1 + or1),
        (er0 - or0, ei0 - oi0),
        (er1 + oi1, ei1 - or1),
    )


def inverse_even_body(in_ref, mqi_ref, txi_ref, out_ref):
    table = (txi_ref[0, 0], txi_ref[0, 1])
    planes = inverse_y(in_ref, mqi_ref, pl.program_id(0))
    for comp in (0, 1):
        lanes = slice(128 * comp, 128 * comp + 128)
        for j in range(RADIX):
            value = jnp.concatenate([planes[j][0][:, lanes], planes[j][1][:, lanes]], axis=1)
            out_ref[comp, pl.ds(128 * j, 128), :] = times_table(value, table)


def inverse_odd_body(in_ref, even_ref, strain_ref, mqi_ref, txi_ref, out_ref):
    table = (txi_ref[0, 0], txi_ref[0, 1])
    planes = inverse_y(in_ref, mqi_ref, pl.program_id(0))
    for comp in (0, 1):
        lanes = slice(128 * comp, 128 * comp + 128)
        for j in range(RADIX):
            value = jnp.concatenate([planes[j][0][:, lanes], planes[j][1][:, lanes]], axis=1)
            odd = times_table(value, table)
            where = pl.ds(128 * j, 128)
            even = even_ref[comp, where, :]
            left = pl.ds(0, HALF)
            right = pl.ds(HALF, HALF)
            out_ref[comp, where, left] = strain_ref[comp, where, left] - (even + odd)
            out_ref[comp, where, right] = strain_ref[comp, where, right] - (even - odd)


def inverse_even(returned, mqi, txi):
    return pl.pallas_call(
        inverse_even_body,
        grid=(3,),
        in_specs=[
            pl.BlockSpec((BLOCK, LANE), lambda i: (0, 0)),
            pl.BlockSpec((4, 2, HALF, HALF), lambda i: (0, 0, 0, 0)),
            pl.BlockSpec((1, 2, HALF, HALF), lambda i: (0, 0, 0, 0)),
        ],
        out_specs=pl.BlockSpec((2, N, HALF), lambda i: (i, 0, 0)),
        out_shape=jax.ShapeDtypeStruct((COMPS, N, HALF), f32),
        compiler_params=params(),
        name="inverse_even",
    )(returned, mqi, txi)


def inverse_odd(returned, even, strain, mqi, txi):
    return pl.pallas_call(
        inverse_odd_body,
        grid=(3,),
        in_specs=[
            pl.BlockSpec((BLOCK, LANE), lambda i: (0, 0)),
            pl.BlockSpec((2, N, HALF), lambda i: (i, 0, 0)),
            pl.BlockSpec((2, N, N), lambda i: (i, 0, 0)),
            pl.BlockSpec((4, 2, HALF, HALF), lambda i: (0, 0, 0, 0)),
            pl.BlockSpec((1, 2, HALF, HALF), lambda i: (1, 0, 0, 0)),
        ],
        out_specs=pl.BlockSpec((2, N, N), lambda i: (i, 0, 0)),
        out_shape=jax.ShapeDtypeStruct((COMPS, N, N), f32),
        compiler_params=params(),
        name="inverse_odd",
    )(returned, even, strain, mqi, txi)


def exchange(block):
    packed = block.reshape(DEPTH, ROWS, LANE)
    moved = lax.all_to_all(packed, "gz", split_axis=0, concat_axis=0, tiled=True)
    return moved.reshape(BLOCK, LANE)


def neighbours(plane, count):
    ahead = [(i, (i + 1) % count) for i in range(count)]
    behind = [((i + 1) % count, i) for i in range(count)]
    return lax.ppermute(plane, "gz", ahead), lax.ppermute(plane, "gz", behind)


def shards(
    order_param,
    concentration,
    strain,
    grain_ids,
    seed_labels,
    grain_moduli,
    grain_mobility,
    seed_rate,
):
    count = lax.axis_size("gz")
    order_now = order_param.reshape(N, N)
    conc_now = concentration.reshape(N, N)
    planes = strain.reshape(COMPS, N, N)
    txf, mq, mz, mqi, txi = make_tables()
    lame, shear, kinetic, decay = coefficients(
        grain_moduli,
        grain_mobility,
        seed_rate,
        grain_ids.reshape(N, N),
        seed_labels.reshape(N, N),
        planes,
    )
    for _ in range(SUBSTEPS):
        halos = neighbours(order_now, count) + neighbours(conc_now, count)
        order_now, conc_now = substep(order_now, conc_now, halos, kinetic, decay)
    band = lax.axis_index("gz").astype(jnp.int32).reshape(1)
    even, odd = forward_even(order_now, lame, shear, planes, txf, mq)
    even = exchange(even)
    odd = exchange(forward_odd(odd, txf, mq))
    even = exchange(middle(band, even, mz, 0))
    odd = exchange(middle(band, odd, mz, 1))
    partial = inverse_even(even, mqi, txi)
    strain_next = inverse_odd(odd, partial, planes, mqi, txi)
    return (
        order_now.reshape(1, N, N),
        conc_now.reshape(1, N, N),
        strain_next.reshape(COMPS, 1, N, N),
    )


def solution(mesh):
    return jax.shard_map(
        shards,
        mesh=mesh,
        in_specs=(
            P("gz", None, None),
            P("gz", None, None),
            P(None, "gz", None, None),
            P("gz", None, None),
            P("gz", None, None),
            P(),
            P(),
            P(),
        ),
        out_specs=(P("gz", None, None), P("gz", None, None), P(None, "gz", None, None)),
        check_vma=False,
    )
```

time: 463 us -> 290 us (0.63); the launches traced: 455 us -> 289 us
  matrix products: 145 us -> 0 us
  Pallas kernels: 0 us -> 51.9 us
  waiting for transfers between devices: 185 us -> 141 us
  starting transfers between devices: 21.7 us -> 54.5 us
  other arithmetic: 32.6 us -> 0 us
  local copies, waits for them, and re-layouts: 67.8 us -> 39.9 us
    dot_general x20 -> x0, matrix products: 145 us -> none  [product(): return jnp.einsum(form, left, right, precision=lax.Precision.HIGHEST)]
    pallas_call x0 -> x10, Pallas kernels: none -> 51.9 us  [the longest x2 13.2 us: middle(): pl.pallas_call(functools.partial(middle_body, parity=parity), grid=(RADIX...]
    ppermute x4 -> x8, waiting for transfers between devices: 46.1 us -> 13.8 us  [neighbours(): return (lax.ppermute(plane, 'gz', ahead), lax.ppermute(plane, 'gz', behind))]
    unnamed x88 -> x66, local copies, waits for them, and re-layouts: 8.68 us -> 39.9 us
    another operation x6 -> x0, local copies, waits for them, and re-layouts: 27.4 us -> none  [the longest x1 10.3 us: plane_spectra(): return jnp.stack([real_y, imag_y])]
    slice x8 -> x0, local copies, waits for them, and re-layouts: 23.4 us -> none  [the longest x1 12.7 us: shards(): spectral[0]]
    ppermute x4 -> x8, starting transfers between devices: 9.04 us -> 30.1 us  [neighbours(): return (lax.ppermute(plane, 'gz', ahead), lax.ppermute(plane, 'gz', behind))]
    add x4 -> x0, other arithmetic: 11.8 us -> none  [the longest x2 11.7 us: advance(): conc_now + time_step * diffusivity * lap_conc]
  transfers between devices with their start and end apart: 6 -> 12, of which waited for: 6 -> 6; matrix products, arithmetic and copies ran while one was open for 5% -> 0% of each run, Pallas kernels for 0% -> 11%
where the time goes in v1:
time: 290 us; the launch traced here: 289 us
  waiting for transfers between devices  141 us (49%)
  starting transfers between devices  54.5 us (19%)
  Pallas kernels  51.9 us (18%)
  local copies, waits for them, and re-layouts  39.9 us (14%)
    all_to_all x4, waiting for transfers between devices, exchange(): lax.all_to_all(packed, 'gz', split_axis=0, concat_axis=0, tiled=True)  127 us
    unnamed x66, local copies, waits for them, and re-layouts  39.9 us
    ppermute x8, starting transfers between devices, neighbours(): return (lax.ppermute(plane, 'gz', ahead), lax.ppermute(plane, 'gz', behind))  30.1 us
    all_to_all x4, starting transfers between devices, exchange(): lax.all_to_all(packed, 'gz', split_axis=0, concat_axis=0, tiled=True)  24.4 us
    ppermute x8, waiting for transfers between devices, neighbours(): return (lax.ppermute(plane, 'gz', ahead), lax.ppermute(plane, 'gz', behind))  13.8 us
    pallas_call x2, Pallas kernels, middle(): pl.pallas_call(functools.partial(middle_body, parity=parity), grid=(RADIX...  13.2 us
    pallas_call x2, Pallas kernels, substep(): pl.pallas_call(step_body, grid=(N // TILE,), in_specs=[whole, whole] + [b...  8.1 us
    pallas_call x1, Pallas kernels, forward_even(): pl.pallas_call(even_body, grid=(XTILES + 1,), in_specs=[block, block, blo...  7.27 us
  transfers between devices with their start and end apart: 12, of which 6 were waited for; matrix products, arithmetic and copies ran while one was open for 0% of the time, Pallas kernels for 11%

profile of v1, /device:TPU:0, one launch (start us, length us, event | category | flops | bytes accessed | tf_op | source)
XLA Modules:
  0.0 288.5 jit_solution(12362295657927948201)
XLA Ops:
  0.7 8.3 %collective-permute-start.1 = (f32[512,512]{1,0:T(8,128)}, f32[512,512]{1,0:T(8,128)S(1)}, u32[]{:S(2)}, u32[]{:S(2)}) collective-permute-start(f32[512,512]{1,0:T(8,128)} %bitcast.32), channel_id=1, source_target_pairs={{1,0},{2,1},{3,2},{4,3},{5,4},{6,5},{7,6},{8,7},{9,8},{10,9},{11,1... | collective-permute-start | bytes 3145736 | tf_op jit(solution)/shard_map/ppermute | solution.py:531
  9.0 7.2 %collective-permute-start.3 = (f32[512,512]{1,0:T(8,128)}, f32[512,512]{1,0:T(8,128)S(1)}, u32[]{:S(2)}, u32[]{:S(2)}) collective-permute-start(f32[512,512]{1,0:T(8,128)} %bitcast.35), channel_id=1, source_target_pairs={{1,0},{2,1},{3,2},{4,3},{5,4},{6,5},{7,6},{8,7},{9,8},{10,9},{11,1... | collective-permute-start | bytes 3145736 | tf_op jit(solution)/shard_map/ppermute | solution.py:531
  16.2 2.8 copy-done
  23.4 6.0 %coefficients.1 = (f32[512,512]{1,0:T(8,128)S(1)}, f32[512,512]{1,0:T(8,128)S(1)}, f32[512,512]{1,0:T(8,128)S(1)}, f32[512,512]{1,0:T(8,128)S(1)}) custom-call(f32[2,16]{1,0:T(2,128)S(1)} %copy-done.30, f32[16]{0:T(128)S(1)} %copy-done.31, f32[8]{0:T(128)S(1)} %copy-done.32, s32[512,512]{1,0:T(8,128)S(1)} %bitcast.29, s32[512,512]{1,0:T(8,128)S(1)} %bitcast.30, ...), custom_call_target="tpu_custom_call" | custom-call | tf_op jit(solution)/shard_map/coefficients/pallas_call | solution.py:157
  29.5 3.4 %collective-permute-done.2.cu_ref = f32[512,512]{1,0:T(8,128)S(1)} collective-permute-done((f32[512,512]{1,0:T(8,128)}, f32[512,512]{1,0:T(8,128)S(1)}, u32[]{:S(2)}, u32[]{:S(2)}) %collective-permute-start.2) | collective-permute-done | bytes 1048608 | tf_op jit(solution)/shard_map/ppermute | solution.py:531
  32.9 3.6 %substep.2 = (f32[512,512]{1,0:T(8,128)S(1)}, f32[512,512]{1,0:T(8,128)S(1)}) custom-call(f32[512,512]{1,0:T(8,128)S(1)} %bitcast.33, f32[512,512]{1,0:T(8,128)S(1)} %bitcast.36, f32[512,512]{1,0:T(8,128)S(1)} %collective-permute-done.pu_ref, f32[512,512]{1,0:T(8,128)S(1)} %collective-permute-done.1.pd_ref, f32[512,512]{1,0:T(8,128)S(1)} %collective-permute-done.2.cu_ref, ...), custom_call_target="tpu_custom_call" | custom-call | tf_op jit(solution)/shard_map/substep/pallas_call | solution.py:212
  36.6 7.3 %collective-permute-start.5 = (f32[512,512]{1,0:T(8,128)S(1)}, f32[512,512]{1,0:T(8,128)S(1)}, u32[]{:S(2)}, u32[]{:S(2)}) collective-permute-start(f32[512,512]{1,0:T(8,128)S(1)} %get-tuple-element.20.p_ref), channel_id=1, source_target_pairs={{1,0},{2,1},{3,2},{4,3},{5,4},{6,5},{7,6},{8,7},{9,8},{10,9},{11,1... | collective-permute-start | bytes 3145736 | tf_op jit(solution)/shard_map/ppermute | solution.py:531
  43.9 7.2 %collective-permute-start.7 = (f32[512,512]{1,0:T(8,128)S(1)}, f32[512,512]{1,0:T(8,128)S(1)}, u32[]{:S(2)}, u32[]{:S(2)}) collective-permute-start(f32[512,512]{1,0:T(8,128)S(1)} %get-tuple-element.21.c_ref), channel_id=1, source_target_pairs={{1,0},{2,1},{3,2},{4,3},{5,4},{6,5},{7,6},{8,7},{9,8},{10,9},{11,1... | collective-permute-start | bytes 3145736 | tf_op jit(solution)/shard_map/ppermute | solution.py:531
  51.1 3.3 %tables.1 = (bf16[2,2,256,256]{3,2,1,0:T(8,128)(2,1)S(1)}, bf16[4,2,256,256]{3,2,1,0:T(8,128)(2,1)S(1)}, bf16[2,2,256,256]{3,2,1,0:T(8,128)(2,1)S(1)}, bf16[4,2,...) custom-call(), custom_call_target="tpu_custom_call" | custom-call | tf_op jit(solution)/shard_map/tables/pallas_call | solution.py:106
  57.1 10.4 %collective-permute-done.6.cu_ref = f32[512,512]{1,0:T(8,128)S(1)} collective-permute-done((f32[512,512]{1,0:T(8,128)S(1)}, f32[512,512]{1,0:T(8,128)S(1)}, u32[]{:S(2)}, u32[]{:S(2)}) %collective-permute-start.6) | collective-permute-done | bytes 1048608 | tf_op jit(solution)/shard_map/ppermute | solution.py:531
  67.5 4.5 %substep.3 = (f32[512,512]{1,0:T(8,128)}, f32[512,512]{1,0:T(8,128)}) custom-call(f32[512,512]{1,0:T(8,128)S(1)} %get-tuple-element.20.p_ref, f32[512,512]{1,0:T(8,128)S(1)} %get-tuple-element.21.c_ref, f32[512,512]{1,0:T(8,128)S(1)} %collective-permute-done.4.pu_ref, f32[512,512]{1,0:T(8,128)S(1)} %collective-permute-done.5.pd_ref, ...), custom_call_target="tpu_custom_call" | custom-call | tf_op jit(solution)/shard_map/substep/pallas_call | solution.py:212
  73.2 7.3 %forward_even.1 = (f32[6144,128]{1,0:T(8,128)S(1)}, f32[6,512,256]{2,1,0:T(8,128)S(1)}) custom-call(f32[512,512]{1,0:T(8,128)S(1)} %copy-done.29, f32[512,512]{1,0:T(8,128)S(1)} %get-tuple-element.24.lame_in, f32[512,512]{1,0:T(8,128)S(1)} %get-tuple-element.25.shear_in, f32[6,512,512]{2,1,0:T(8,128)} %bitcast.19, ...), custom_call_target="tpu_custom_call" | custom-call | tf_op jit(solution)/shard_map/forward_even/pallas_call | solution.py:284
  82.1 1.7 copy-done.15
  83.8 9.2 %all-to-all-start.2 = ((f32[128,48,128]{2,1,0:T(8,128)}), f32[128,48,128]{2,1,0:T(8,128)S(1)}, u32[]{:S(2)}, u32[]{:S(2)}) async-start(f32[128,48,128]{2,1,0:T(8,128)} %bitcast.28), calls=%async_computation.2 | async-start | bytes 6291456 | tf_op jit(solution)/shard_map/all_to_all | solution.py:524
  94.2 1.9 copy-done.16
  97.1 4.3 %forward_odd.1 = f32[6144,128]{1,0:T(8,128)S(1)} custom-call(f32[6,512,256]{2,1,0:T(8,128)S(1)} %copy-done.16, bf16[2,2,256,256]{3,2,1,0:T(8,128)(2,1)S(1)} %copy-done.24, bf16[4,2,256,256]{3,2,1,0:T(8,128)(2,1)S(1)} %copy-done.13), custom_call_target="tpu_custom_call" | custom-call | tf_op jit(solution)/shard_map/forward_odd/pallas_call | solution.py:343
  101.4 1.7 copy-done.6
  103.1 31.5 %all-to-all-done.2 = f32[128,48,128]{2,1,0:T(8,128)S(1)} async-done(((f32[128,48,128]{2,1,0:T(8,128)}), f32[128,48,128]{2,1,0:T(8,128)S(1)}, u32[]{:S(2)}, u32[]{:S(2)}) %all-to-all-start.2) | async-done | bytes 3145760 | tf_op jit(solution)/shard_map/all_to_all | solution.py:524
  134.6 5.9 %all-to-all-start = ((f32[128,48,128]{2,1,0:T(8,128)}), f32[128,48,128]{2,1,0:T(8,128)}, u32[]{:S(2)}, u32[]{:S(2)}) async-start(f32[128,48,128]{2,1,0:T(8,128)} %bitcast.26), calls=%async_computation | async-start | bytes 6291456 | tf_op jit(solution)/shard_map/all_to_all | solution.py:524
  141.6 5.7 %middle_even.1 = f32[6144,128]{1,0:T(8,128)S(1)} custom-call(s32[1]{0:T(128)} %bitcast.7.band_ref, f32[6144,128]{1,0:T(8,128)S(1)} %bitcast.23, bf16[2,2,256,256]{3,2,1,0:T(8,128)(2,1)S(1)} %copy-done.21), custom_call_target="tpu_custom_call" | custom-call | tf_op jit(solution)/shard_map/middle_even/pallas_call | solution.py:422
  147.3 1.7 copy-done.3
  148.9 32.9 %all-to-all-done = f32[128,48,128]{2,1,0:T(8,128)} async-done(((f32[128,48,128]{2,1,0:T(8,128)}), f32[128,48,128]{2,1,0:T(8,128)}, u32[]{:S(2)}, u32[]{:S(2)}) %all-to-all-start) | async-done | bytes 3145760 | tf_op jit(solution)/shard_map/all_to_all | solution.py:524
  181.8 4.7 %all-to-all-start.3 = ((f32[128,48,128]{2,1,0:T(8,128)}), f32[128,48,128]{2,1,0:T(8,128)S(1)}, u32[]{:S(2)}, u32[]{:S(2)}) async-start(f32[128,48,128]{2,1,0:T(8,128)} %bitcast.25), calls=%async_computation.3 | async-start | bytes 6291456 | tf_op jit(solution)/shard_map/all_to_all | solution.py:524
  187.5 7.6 %middle_odd.1 = f32[6144,128]{1,0:T(8,128)S(1)} custom-call(s32[1]{0:T(128)} %bitcast.7.band_ref, f32[6144,128]{1,0:T(8,128)} %bitcast.9.in_ref, bf16[2,2,256,256]{3,2,1,0:T(8,128)(2,1)S(1)} %copy-done.22), custom_call_target="tpu_custom_call" | custom-call | tf_op jit(solution)/shard_map/middle_odd/pallas_call | solution.py:422
  196.7 31.3 %all-to-all-done.3 = f32[128,48,128]{2,1,0:T(8,128)S(1)} async-done(((f32[128,48,128]{2,1,0:T(8,128)}), f32[128,48,128]{2,1,0:T(8,128)S(1)}, u32[]{:S(2)}, u32[]{:S(2)}) %all-to-all-start.3) | async-done | bytes 3145760 | tf_op jit(solution)/shard_map/all_to_all | solution.py:524
  229.7 4.7 %all-to-all-start.1 = ((f32[128,48,128]{2,1,0:T(8,128)}), f32[128,48,128]{2,1,0:T(8,128)S(1)}, u32[]{:S(2)}, u32[]{:S(2)}) async-start(f32[128,48,128]{2,1,0:T(8,128)} %bitcast.24), calls=%async_computation.1 | async-start | bytes 6291456 | tf_op jit(solution)/shard_map/all_to_all | solution.py:524
  234.4 1.9 copy-done.8
  238.5 4.1 %inverse_even.1.even_ref = f32[6,512,256]{2,1,0:T(8,128)S(1)} custom-call(f32[6144,128]{1,0:T(8,128)S(1)} %bitcast.27, bf16[4,2,256,256]{3,2,1,0:T(8,128)(2,1)S(1)} %copy-done.10, bf16[2,2,256,256]{3,2,1,0:T(8,128)(2,1)S(1)} %copy-done.18), custom_call_target="tpu_custom_call" | custom-call | tf_op jit(solution)/shard_map/inverse_even/pallas_call | solution.py:489
  244.3 31.7 %all-to-all-done.1 = f32[128,48,128]{2,1,0:T(8,128)S(1)} async-done(((f32[128,48,128]{2,1,0:T(8,128)}), f32[128,48,128]{2,1,0:T(8,128)S(1)}, u32[]{:S(2)}, u32[]{:S(2)}) %all-to-all-start.1) | async-done | bytes 3145760 | tf_op jit(solution)/shard_map/all_to_all | solution.py:524
  276.0 2.8 copy-done.1
  278.8 1.9 copy-done.5
  282.9 5.6 %inverse_odd.1 = f32[6,512,512]{2,1,0:T(8,128)} custom-call(f32[6144,128]{1,0:T(8,128)S(1)} %bitcast.22, f32[6,512,256]{2,1,0:T(8,128)S(1)} %copy-done.5, f32[6,512,512]{2,1,0:T(8,128)S(1)} %bitcast.21, bf16[4,2,256,256]{3,2,1,0:T(8,128)(2,1)S(1)} %copy-done.11, bf16[2,2,256,256]{3,2,1,0:T(8,128)(2,1)S(1)} %copy-done.19), custom_call_target="tpu_custom_call" | custom-call | tf_op jit(solution)/shard_map/inverse_odd/pallas_call | solution.py:505
  (68 shorter events, 23.9 us)
Async XLA Ops:
  0.6 28.8 %collective-permute-start = (f32[512,512]{1,0:T(8,128)}, f32[512,512]{1,0:T(8,128)S(1)}, u32[]{:S(2)}, u32[]{:S(2)}) collective-permute-start(f32[512,512]{1,0:T(8,128)} %bitcast.31), channel_id=1, source_target_pairs={{0,1},{1,2},{2,3},{3,4},{4,5},{5,6},{6,7},{7,8},{8,9},{9,10},{10,1... | collective-permute-start | bytes 3145736 | tf_op jit(solution)/shard_map/ppermute | solution.py:531
  0.7 28.7 %collective-permute-start.1 = (f32[512,512]{1,0:T(8,128)}, f32[512,512]{1,0:T(8,128)S(1)}, u32[]{:S(2)}, u32[]{:S(2)}) collective-permute-start(f32[512,512]{1,0:T(8,128)} %bitcast.32), channel_id=1, source_target_pairs={{1,0},{2,1},{3,2},{4,3},{5,4},{6,5},{7,6},{8,7},{9,8},{10,9},{11,1... | collective-permute-start | bytes 3145736 | tf_op jit(solution)/shard_map/ppermute | solution.py:531
  9.0 23.8 %collective-permute-start.2 = (f32[512,512]{1,0:T(8,128)}, f32[512,512]{1,0:T(8,128)S(1)}, u32[]{:S(2)}, u32[]{:S(2)}) collective-permute-start(f32[512,512]{1,0:T(8,128)} %bitcast.34), channel_id=1, source_target_pairs={{0,1},{1,2},{2,3},{3,4},{4,5},{5,6},{6,7},{7,8},{8,9},{9,10},{10,1... | collective-permute-start | bytes 3145736 | tf_op jit(solution)/shard_map/ppermute | solution.py:531
  9.0 23.9 %collective-permute-start.3 = (f32[512,512]{1,0:T(8,128)}, f32[512,512]{1,0:T(8,128)S(1)}, u32[]{:S(2)}, u32[]{:S(2)}) collective-permute-start(f32[512,512]{1,0:T(8,128)} %bitcast.35), channel_id=1, source_target_pairs={{1,0},{2,1},{3,2},{4,3},{5,4},{6,5},{7,6},{8,7},{9,8},{10,9},{11,1... | collective-permute-start | bytes 3145736 | tf_op jit(solution)/shard_map/ppermute | solution.py:531
  16.2 2.8 copy-start
  18.9 1.2 copy-start.25
  23.4 9.5 %copy-start.27 = (f32[1,512,512]{2,1,0:T(8,128)S(1)}, f32[1,512,512]{2,1,0:T(8,128)}, u32[]{:S(2)}) copy-start(f32[1,512,512]{2,1,0:T(8,128)} %param.8) | copy-start | bytes 3145732
  23.4 9.5 %copy-start.28 = (f32[1,512,512]{2,1,0:T(8,128)S(1)}, f32[1,512,512]{2,1,0:T(8,128)}, u32[]{:S(2)}) copy-start(f32[1,512,512]{2,1,0:T(8,128)} %param.9) | copy-start | bytes 3145732
  36.5 20.6 %collective-permute-start.4 = (f32[512,512]{1,0:T(8,128)S(1)}, f32[512,512]{1,0:T(8,128)S(1)}, u32[]{:S(2)}, u32[]{:S(2)}) collective-permute-start(f32[512,512]{1,0:T(8,128)S(1)} %get-tuple-element.20.p_ref), channel_id=1, source_target_pairs={{0,1},{1,2},{2,3},{3,4},{4,5},{5,6},{6,7},{7,8},{8,9},{9,10},{10,1... | collective-permute-start | bytes 3145736 | tf_op jit(solution)/shard_map/ppermute | solution.py:531
  36.6 20.5 %collective-permute-start.5 = (f32[512,512]{1,0:T(8,128)S(1)}, f32[512,512]{1,0:T(8,128)S(1)}, u32[]{:S(2)}, u32[]{:S(2)}) collective-permute-start(f32[512,512]{1,0:T(8,128)S(1)} %get-tuple-element.20.p_ref), channel_id=1, source_target_pairs={{1,0},{2,1},{3,2},{4,3},{5,4},{6,5},{7,6},{8,7},{9,8},{10,9},{11,1... | collective-permute-start | bytes 3145736 | tf_op jit(solution)/shard_map/ppermute | solution.py:531
  43.9 23.6 %collective-permute-start.6 = (f32[512,512]{1,0:T(8,128)S(1)}, f32[512,512]{1,0:T(8,128)S(1)}, u32[]{:S(2)}, u32[]{:S(2)}) collective-permute-start(f32[512,512]{1,0:T(8,128)S(1)} %get-tuple-element.21.c_ref), channel_id=1, source_target_pairs={{0,1},{1,2},{2,3},{3,4},{4,5},{5,6},{6,7},{7,8},{8,9},{9,10},{10,1... | collective-permute-start | bytes 3145736 | tf_op jit(solution)/shard_map/ppermute | solution.py:531
  43.9 23.6 %collective-permute-start.7 = (f32[512,512]{1,0:T(8,128)S(1)}, f32[512,512]{1,0:T(8,128)S(1)}, u32[]{:S(2)}, u32[]{:S(2)}) collective-permute-start(f32[512,512]{1,0:T(8,128)S(1)} %get-tuple-element.21.c_ref), channel_id=1, source_target_pairs={{1,0},{2,1},{3,2},{4,3},{5,4},{6,5},{7,6},{8,7},{9,8},{10,9},{11,1... | collective-permute-start | bytes 3145736 | tf_op jit(solution)/shard_map/ppermute | solution.py:531
  57.1 14.9 %copy-start.12 = (bf16[4,2,256,256]{3,2,1,0:T(8,128)(2,1)}, bf16[4,2,256,256]{3,2,1,0:T(8,128)(2,1)S(1)}, u32[]{:S(2)}) copy-start(bf16[4,2,256,256]{3,2,1,0:T(8,128)(2,1)S(1)} %get-tuple-element.27.mq_ref) | copy-start | bytes 3145732
  57.1 14.9 %copy-start.23 = (bf16[2,2,256,256]{3,2,1,0:T(8,128)(2,1)}, bf16[2,2,256,256]{3,2,1,0:T(8,128)(2,1)S(1)}, u32[]{:S(2)}) copy-start(bf16[2,2,256,256]{3,2,1,0:T(8,128)(2,1)S(1)} %get-tuple-element.26.txf_ref) | copy-start | bytes 1572868
  72.0 1.2 copy-start.29
  80.5 1.6 copy-start.14
  82.1 1.7 copy-start.15
  83.8 50.8 %all-to-all-start.2 = ((f32[128,48,128]{2,1,0:T(8,128)}), f32[128,48,128]{2,1,0:T(8,128)S(1)}, u32[]{:S(2)}, u32[]{:S(2)}) async-start(f32[128,48,128]{2,1,0:T(8,128)} %bitcast.28), calls=%async_computation.2 | async-start | bytes 6291456 | tf_op jit(solution)/shard_map/all_to_all | solution.py:524
  93.0 1.2 copy-start.13
  94.2 1.9 copy-start.16
  101.4 1.7 copy-start.6
  134.6 47.2 %all-to-all-start = ((f32[128,48,128]{2,1,0:T(8,128)}), f32[128,48,128]{2,1,0:T(8,128)}, u32[]{:S(2)}, u32[]{:S(2)}) async-start(f32[128,48,128]{2,1,0:T(8,128)} %bitcast.26), calls=%async_computation | async-start | bytes 6291456 | tf_op jit(solution)/shard_map/all_to_all | solution.py:524
  147.3 1.7 copy-start.3
  181.8 46.3 %all-to-all-start.3 = ((f32[128,48,128]{2,1,0:T(8,128)}), f32[128,48,128]{2,1,0:T(8,128)S(1)}, u32[]{:S(2)}, u32[]{:S(2)}) async-start(f32[128,48,128]{2,1,0:T(8,128)} %bitcast.25), calls=%async_computation.3 | async-start | bytes 6291456 | tf_op jit(solution)/shard_map/all_to_all | solution.py:524
  195.1 1.7 copy-start.2
  228.1 1.6 copy-start.7
  229.7 46.3 %all-to-all-start.1 = ((f32[128,48,128]{2,1,0:T(8,128)}), f32[128,48,128]{2,1,0:T(8,128)S(1)}, u32[]{:S(2)}, u32[]{:S(2)}) async-start(f32[128,48,128]{2,1,0:T(8,128)} %bitcast.24), calls=%async_computation.1 | async-start | bytes 6291456 | tf_op jit(solution)/shard_map/all_to_all | solution.py:524
  234.4 1.9 copy-start.8
  236.3 1.2 copy-start.10
  242.7 1.6 copy-start.4
  276.0 2.8 copy-start.1
  278.8 1.9 copy-start.5
  (13 other events, 12.3 us)

commit v2 on v1

v2 whole, which is shorter than its diff:
```python
import functools
import math

import jax
import jax.numpy as jnp
from jax import lax
from jax.experimental import pallas as pl
from jax.experimental.pallas import tpu as pltpu
from jax.sharding import PartitionSpec as P

SUBSTEPS = 2
N = 512
HALF = 256
LANE = 128
DEPTH = 128
COMPS = 6
RADIX = 4
PAIRS = COMPS // 2
SUB = 8
QROWS = PAIRS * SUB
PROWS = RADIX * SUB
ROWS = PAIRS * RADIX * SUB

time_step = 0.05
grad_coef = 1.0
well_height = 1.0
drive_coef = 2.0
conc_eq = 0.5
mech_boost = 1.0
diffusivity = 1.0
release_coef = 1.0
residual_stiff = 0.1
lame_ref = 1.0
shear_ref = 1.0
coupling = (lame_ref + shear_ref) / (shear_ref * (lame_ref + 2.0 * shear_ref))

f32 = jnp.float32
bf16 = jnp.bfloat16
VMEM_LIMIT = 40 * 1024 * 1024


def params(dims=1):
    return pltpu.CompilerParams(
        dimension_semantics=("arbitrary",) * dims, vmem_limit_bytes=VMEM_LIMIT
    )


def split(value):
    high = value.astype(bf16)
    low = (value - high.astype(f32)).astype(bf16)
    return high, low


def mul(left, right):
    return lax.dot_general(
        left, right, (((1,), (0,)), ((), ())), preferred_element_type=f32
    )


def table_times(table, value):
    high, low = split(value)
    return mul(table[0], high) + mul(table[0], low) + mul(table[1], high)


def times_table(value, table):
    high, low = split(value)
    return mul(high, table[0]) + mul(low, table[0]) + mul(high, table[1])


def unit_cos(index):
    wrapped = ((index + 256) & 511) - 256
    angle = (128 - jnp.abs(wrapped)).astype(f32) * (2.0 * math.pi / 512.0)
    square = angle * angle
    poly = 1.0 / 6227020800.0
    for power in (39916800.0, 362880.0, 5040.0, 120.0, 6.0):
        poly = 1.0 / power - square * poly
    return angle * (1.0 - square * poly)


def table_body(txf_ref, mq_ref, mz_ref, mqi_ref, txi_ref):
    rows = lax.broadcasted_iota(jnp.int32, (HALF, HALF), 0)
    cols = lax.broadcasted_iota(jnp.int32, (HALF, HALF), 1)
    row_low = rows & 127
    row_top = rows >> 7
    col_low = cols & 127
    col_top = cols >> 7

    def put(ref, slot, value):
        high, low = split(value)
        ref[slot, 0] = high
        ref[slot, 1] = low

    turn = (row_top - col_top) * 128
    for parity in range(2):
        wave = 2 * col_low + parity
        put(txf_ref, parity, unit_cos(rows * wave + col_top * 128))
        wave = 2 * row_low + parity
        weight = jnp.where(wave == 0, 1.0, 2.0) * (1.0 / float(N * N * DEPTH))
        put(txi_ref, parity, unit_cos(wave * cols + row_top * 128) * weight)
    for rest in range(RADIX):
        put(mq_ref, rest, unit_cos((4 * row_low + rest) * col_low + turn))
        put(mqi_ref, rest, unit_cos((4 * col_low + rest) * row_low - turn))
    put(mz_ref, 0, unit_cos(4 * row_low * col_low + turn))
    put(mz_ref, 1, unit_cos(4 * row_low * col_low - turn))


def make_tables():
    shape = lambda count: jax.ShapeDtypeStruct((count, 2, HALF, HALF), bf16)
    return pl.pallas_call(
        table_body,
        out_shape=(shape(2), shape(4), shape(2), shape(4), shape(2)),
        compiler_params=pltpu.CompilerParams(vmem_limit_bytes=VMEM_LIMIT),
        name="tables",
    )()


TILE = 128
STRIP = 16


def strips(rows, body):
    def step(index, carry):
        body(pl.multiple_of(index * STRIP, STRIP))
        return carry

    lax.fori_loop(0, rows // STRIP, step, 0)


def lane_table(read, count):
    lanes = lax.broadcasted_iota(jnp.int32, (STRIP, LANE), 1)
    table = jnp.zeros((STRIP, LANE), f32)
    for index in range(count):
        table = jnp.where(lanes == index, read(index), table)
    return table


def pick(table, index):
    parts = [
        jnp.take_along_axis(table, index[:, LANE * k : LANE * (k + 1)], axis=1)
        for k in range(N // LANE)
    ]
    return jnp.concatenate(parts, axis=1)


def coef_body(moduli, mobility, rates, grain_ref, label_ref, strain_ref, lame_out, shear_out, kin_out, dec_out):
    grains = mobility.shape[0]
    lames = lane_table(lambda k: moduli[0, k], grains)
    shears = lane_table(lambda k: moduli[1, k], grains)
    mobs = lane_table(lambda k: mobility[k], grains)
    speeds = lane_table(lambda k: rates[k - 1] if k else 0.0, rates.shape[0] + 1)

    def strip(start):
        where = pl.ds(start, STRIP)
        grain = grain_ref[where, :]
        lame = pick(lames, grain)
        shear = pick(shears, grain)
        parts = [strain_ref[comp, where, :] for comp in range(COMPS)]
        trace = parts[0] + parts[1] + parts[2]
        square = (
            parts[0] * parts[0]
            + parts[1] * parts[1]
            + parts[2] * parts[2]
            + 2.0 * (parts[3] * parts[3] + parts[4] * parts[4] + parts[5] * parts[5])
        )
        energy = 0.5 * lame * trace * trace + shear * square
        mech = 1.0 + mech_boost * energy / (1.0 + energy)
        lame_out[where, :] = lame
        shear_out[where, :] = shear
        kin_out[where, :] = time_step * pick(mobs, grain) * mech
        dec_out[where, :] = time_step * pick(speeds, label_ref[where, :])

    strips(TILE, strip)


PLANE = jax.ShapeDtypeStruct((N, N), f32)
WHOLE = pl.BlockSpec((N, N), lambda i: (0, 0))
STRIPE = pl.BlockSpec((TILE, N), lambda i: (i, 0))


def coefficients(moduli, mobility, rates, grain, label, strain):
    smem = pl.BlockSpec(memory_space=pltpu.SMEM)
    return pl.pallas_call(
        coef_body,
        grid=(N // TILE,),
        in_specs=[smem, smem, smem, STRIPE, STRIPE, pl.BlockSpec((COMPS, TILE, N), lambda i: (0, i, 0))],
        out_specs=[STRIPE] * 4,
        out_shape=[PLANE] * 4,
        compiler_params=params(),
        name="coefficients",
    )(moduli, mobility, rates, grain, label, strain)


def planar_sum(ref, start):
    center = ref[pl.ds(start, STRIP), :]
    before = ref[pl.ds(pl.multiple_of((start + N - 8) & (N - 1), 8), 8), :]
    after = ref[pl.ds(pl.multiple_of((start + STRIP) & (N - 1), 8), 8), :]
    tall = jnp.concatenate([before, center, after], axis=0)
    height = STRIP + 16
    above = pltpu.roll(tall, 1, 0)[8 : 8 + STRIP]
    below = pltpu.roll(tall, height - 1, 0)[8 : 8 + STRIP]
    sides = pltpu.roll(center, 1, 1) + pltpu.roll(center, N - 1, 1)
    return center, (above + below) + sides


def next_order(p_ref, start, halo_sum, conc_now, kinetic, decay):
    order_now, order_sum = planar_sum(p_ref, start)
    lap_order = order_sum + halo_sum - 6.0 * order_now
    slope = order_now * (1.0 - order_now)
    well_grad = 2.0 * slope * (1.0 - 2.0 * order_now)
    force = (
        grad_coef * lap_order
        - well_height * well_grad
        + drive_coef * 6.0 * slope * (conc_now - conc_eq)
    )
    return order_now + kinetic * force - decay * order_now


def order_body(p_ref, c_ref, up_ref, down_ref, kin_ref, dec_ref, p_out):
    base = pl.program_id(0) * TILE

    def strip(local):
        where = pl.ds(local, STRIP)
        start = pl.multiple_of(base + local, STRIP)
        p_out[where, :] = next_order(
            p_ref,
            start,
            up_ref[where, :] + down_ref[where, :],
            c_ref[where, :],
            kin_ref[where, :],
            dec_ref[where, :],
        )

    strips(TILE, strip)


def order_step(order_now, conc_now, halos, kinetic, decay):
    return pl.pallas_call(
        order_body,
        grid=(N // TILE,),
        in_specs=[WHOLE] + [STRIPE] * 5,
        out_specs=STRIPE,
        out_shape=PLANE,
        compiler_params=params(),
        name="order_step",
    )(order_now, conc_now, *halos, kinetic, decay)


def conc_body(c_ref, p_ref, new_ref, up_ref, down_ref, c_out):
    base = pl.program_id(0) * TILE

    def strip(local):
        where = pl.ds(local, STRIP)
        conc_now, conc_sum = planar_sum(c_ref, pl.multiple_of(base + local, STRIP))
        lap_conc = conc_sum + (up_ref[where, :] + down_ref[where, :]) - 6.0 * conc_now
        c_out[where, :] = (
            conc_now
            + time_step * diffusivity * lap_conc
            + release_coef * (p_ref[where, :] - new_ref[where, :])
        )

    strips(TILE, strip)


def conc_step(conc_now, order_now, order_new, halos):
    return pl.pallas_call(
        conc_body,
        grid=(N // TILE,),
        in_specs=[WHOLE] + [STRIPE] * 4,
        out_specs=STRIPE,
        out_shape=PLANE,
        compiler_params=params(),
        name="conc_step",
    )(conc_now, order_now, order_new, *halos)


XTILES = N // TILE


def fold_blocks(scratch, comp, lanes_r, lanes_i, rest):
    reals = [scratch[comp, pl.ds(128 * j, 128), lanes_r] for j in range(RADIX)]
    imags = [scratch[comp, pl.ds(128 * j, 128), lanes_i] for j in range(RADIX)]
    if rest % 2 == 0:
        sign = 1.0 if rest == 0 else -1.0
        real = (reals[0] + reals[2]) + sign * (reals[1] + reals[3])
        imag = (imags[0] + imags[2]) + sign * (imags[1] + imags[3])
    elif rest == 1:
        real = (reals[0] - reals[2]) + (imags[1] - imags[3])
        imag = (imags[0] - imags[2]) - (reals[1] - reals[3])
    else:
        real = (reals[0] - reals[2]) - (imags[1] - imags[3])
        imag = (imags[0] - imags[2]) + (reals[1] - reals[3])
    return real, imag


def forward_body(
    p_ref, c_ref, up_ref, down_ref, kin_ref, dec_ref, lame_in, shear_in, strain_ref,
    txf_ref, mq_ref, out_ref, p_out, scratch,
):
    step = pl.program_id(0)

    @pl.when(step < XTILES)
    def _():
        base = step * TILE

        def strip(local):
            where = pl.ds(local, STRIP)
            p_out[where, :] = next_order(
                p_ref,
                pl.multiple_of(base + local, STRIP),
                up_ref[where, :] + down_ref[where, :],
                c_ref[where, :],
                kin_ref[where, :],
                dec_ref[where, :],
            )

        strips(TILE, strip)
        order = p_out[...]
        scale = order * order * (3.0 - 2.0 * order) + residual_stiff
        shear_now = 2.0 * (scale * shear_in[...])
        lame_now = scale * lame_in[...]
        spread = lame_now * (strain_ref[0] + strain_ref[1] + strain_ref[2])
        rows = pl.ds(pl.multiple_of(base, TILE), TILE)
        for comp in range(COMPS):
            part = shear_now * strain_ref[comp]
            if comp < 3:
                part = part + spread
            left = part[:, :HALF]
            right = part[:, HALF:]
            for parity, folded in ((0, left + right), (1, left - right)):
                table = (txf_ref[parity, 0], txf_ref[parity, 1])
                scratch[comp, rows, pl.ds(HALF * parity, HALF)] = times_table(folded, table)

    for rest in range(RADIX):

        @pl.when(step == XTILES + rest)
        def _():
            out = out_ref.reshape(LANE * QROWS, LANE)
            table = (mq_ref[rest, 0], mq_ref[rest, 1])
            for pair in range(PAIRS):
                for parity in range(2):
                    lanes_r = pl.ds(HALF * parity, LANE)
                    lanes_i = pl.ds(HALF * parity + LANE, LANE)
                    both = [
                        fold_blocks(scratch, 2 * pair + k, lanes_r, lanes_i, rest) for k in (0, 1)
                    ]
                    real = jnp.concatenate([both[0][0], both[1][0]], axis=1)
                    imag = jnp.concatenate([both[0][1], both[1][1]], axis=1)
                    result = table_times(table, jnp.concatenate([real, imag], axis=0))
                    row = pair * SUB + parity * 4
                    for k in (0, 1):
                        lanes = slice(LANE * k, LANE * (k + 1))
                        out[pl.ds(row + 2 * k, LANE, stride=QROWS), :] = result[:LANE, lanes]
                        out[pl.ds(row + 2 * k + 1, LANE, stride=QROWS), :] = result[LANE:, lanes]


BUFFER = jax.ShapeDtypeStruct((LANE, PAIRS, RADIX, SUB, LANE), f32)
REST_BLOCK = (LANE, PAIRS, None, SUB, LANE)
PAIR_BLOCK = (LANE, None, RADIX, SUB, LANE)


def full(*shape):
    return pl.BlockSpec(shape, lambda i: (0,) * len(shape))


def forward(order, conc, halos, kinetic, decay, lame, shear, strain, txf, mq):
    last = XTILES - 1
    stripe = pl.BlockSpec((TILE, N), lambda i: (jnp.minimum(i, last), 0))
    return pl.pallas_call(
        forward_body,
        grid=(XTILES + RADIX,),
        in_specs=[
            full(N, N),
            stripe,
            stripe,
            stripe,
            stripe,
            stripe,
            stripe,
            stripe,
            pl.BlockSpec((COMPS, TILE, N), lambda i: (0, jnp.minimum(i, last), 0)),
            full(2, 2, HALF, HALF),
            full(4, 2, HALF, HALF),
        ],
        out_specs=[
            pl.BlockSpec(REST_BLOCK, lambda i: (0, 0, jnp.maximum(i - XTILES, 0), 0, 0)),
            stripe,
        ],
        out_shape=[BUFFER, PLANE],
        scratch_shapes=[pltpu.VMEM((COMPS, N, N), f32)],
        compiler_params=params(),
        name="forward",
    )(order, conc, *halos, kinetic, decay, lame, shear, strain, txf, mq)


def take_pair(ref, row, stride):
    reals, imags = [], []
    for k in (0, 1):
        reals.append(ref[pl.ds(row + 2 * k, LANE, stride=stride), :])
        imags.append(ref[pl.ds(row + 2 * k + 1, LANE, stride=stride), :])
    return jnp.concatenate(
        [jnp.concatenate(reals, axis=1), jnp.concatenate(imags, axis=1)], axis=0
    )


def middle_body(band_ref, in_ref, mz_ref, out_ref):
    rest = pl.program_id(0)
    source = in_ref.reshape(LANE * QROWS, LANE)
    out = out_ref.reshape(LANE * QROWS, LANE)
    onward = (mz_ref[0, 0], mz_ref[0, 1])
    backward = (mz_ref[1, 0], mz_ref[1, 1])
    shape = (DEPTH, LANE)
    depth_index = lax.broadcasted_iota(jnp.int32, shape, 0)
    xi_z = jnp.where(depth_index < DEPTH // 2, depth_index, depth_index - DEPTH).astype(f32)
    wave_y = band_ref[0] * RADIX + rest
    xi_y = jnp.where(wave_y < N // 2, wave_y, wave_y - N).astype(f32)
    for parity in range(2):
        tau_r, tau_i = [], []
        for pair in range(PAIRS):
            result = table_times(onward, take_pair(source, pair * SUB + parity * 4, QROWS))
            for k in (0, 1):
                lanes = slice(LANE * k, LANE * (k + 1))
                tau_r.append(result[:LANE, lanes])
                tau_i.append(result[LANE:, lanes])
        xi_x = (2 * lax.broadcasted_iota(jnp.int32, shape, 1) + parity).astype(f32)
        wave_sq = xi_x * xi_x + xi_y * xi_y + xi_z * xi_z
        live = (wave_sq > 0.5) & (xi_x < float(HALF))
        safe = jnp.where(live, wave_sq, 1.0)
        inverse = 1.0 / safe
        first = jnp.where(live, (0.5 / shear_ref) * inverse, 0.0)
        second = jnp.where(live, (0.5 * coupling) * (inverse * inverse), 0.0)
        grids = []
        for tau in (tau_r, tau_i):
            t_xx, t_yy, t_zz, t_yz, t_xz, t_xy = tau
            v_x = t_xx * xi_x + t_xy * xi_y + t_xz * xi_z
            v_y = t_xy * xi_x + t_yy * xi_y + t_yz * xi_z
            v_z = t_xz * xi_x + t_yz * xi_y + t_zz * xi_z
            inner = (xi_x * v_x + xi_y * v_y + xi_z * v_z) * second
            h_x = v_x * first - xi_x * inner
            h_y = v_y * first - xi_y * inner
            h_z = v_z * first - xi_z * inner
            grids.append(
                (
                    2.0 * xi_x * h_x,
                    2.0 * xi_y * h_y,
                    2.0 * xi_z * h_z,
                    xi_z * h_y + xi_y * h_z,
                    xi_z * h_x + xi_x * h_z,
                    xi_y * h_x + xi_x * h_y,
                )
            )
        for pair in range(PAIRS):
            real = jnp.concatenate([grids[0][pair * 2], grids[0][pair * 2 + 1]], axis=1)
            imag = jnp.concatenate([grids[1][pair * 2], grids[1][pair * 2 + 1]], axis=1)
            result = table_times(backward, jnp.concatenate([real, imag], axis=0))
            row = pair * SUB + parity * 4
            for k in (0, 1):
                lanes = slice(LANE * k, LANE * (k + 1))
                out[pl.ds(row + 2 * k, LANE, stride=QROWS), :] = result[:LANE, lanes]
                out[pl.ds(row + 2 * k + 1, LANE, stride=QROWS), :] = result[LANE:, lanes]


def middle(band, received, mz):
    spec = pl.BlockSpec(REST_BLOCK, lambda i: (0, 0, i, 0, 0))
    return pl.pallas_call(
        middle_body,
        grid=(RADIX,),
        in_specs=[pl.BlockSpec(memory_space=pltpu.SMEM), spec, full(2, 2, HALF, HALF)],
        out_specs=spec,
        out_shape=BUFFER,
        compiler_params=params(),
        name="middle",
    )(band, received, mz)


def inverse_y(source, mqi_ref, parity):
    blocks = []
    for rest in range(RADIX):
        value = take_pair(source, rest * SUB + parity * 4, PROWS)
        result = table_times((mqi_ref[rest, 0], mqi_ref[rest, 1]), value)
        blocks.append((result[:LANE], result[LANE:]))
    er0, er1 = blocks[0][0] + blocks[2][0], blocks[0][0] - blocks[2][0]
    ei0, ei1 = blocks[0][1] + blocks[2][1], blocks[0][1] - blocks[2][1]
    or0, or1 = blocks[1][0] + blocks[3][0], blocks[1][0] - blocks[3][0]
    oi0, oi1 = blocks[1][1] + blocks[3][1], blocks[1][1] - blocks[3][1]
    return (
        (er0 + or0, ei0 + oi0),
        (er1 - oi1, ei1 + or1),
        (er0 - or0, ei0 - oi0),
        (er1 + oi1, ei1 - or1),
    )


def inverse_body(in_ref, strain_ref, mqi_ref, txi_ref, out_ref):
    source = in_ref.reshape(LANE * PROWS, LANE)
    planes = [inverse_y(source, mqi_ref, parity) for parity in range(2)]
    for k in (0, 1):
        lanes = slice(LANE * k, LANE * (k + 1))
        for j in range(RADIX):
            halves = []
            for parity in range(2):
                real, imag = planes[parity][j]
                value = jnp.concatenate([real[:, lanes], imag[:, lanes]], axis=1)
                halves.append(times_table(value, (txi_ref[parity, 0], txi_ref[parity, 1])))
            even, odd = halves
            where = pl.ds(LANE * j, LANE)
            left = pl.ds(0, HALF)
            right = pl.ds(HALF, HALF)
            out_ref[k, where, left] = strain_ref[k, where, left] - (even + odd)
            out_ref[k, where, right] = strain_ref[k, where, right] - (even - odd)


def inverse(returned, strain, mqi, txi):
    return pl.pallas_call(
        inverse_body,
        grid=(PAIRS,),
        in_specs=[
            pl.BlockSpec(PAIR_BLOCK, lambda i: (0, i, 0, 0, 0)),
            pl.BlockSpec((2, N, N), lambda i: (i, 0, 0)),
            full(4, 2, HALF, HALF),
            full(2, 2, HALF, HALF),
        ],
        out_specs=pl.BlockSpec((2, N, N), lambda i: (i, 0, 0)),
        out_shape=jax.ShapeDtypeStruct((COMPS, N, N), f32),
        compiler_params=params(),
        name="inverse",
    )(returned, strain, mqi, txi)


def exchange(block):
    packed = block.reshape(DEPTH, ROWS, LANE)
    moved = lax.all_to_all(packed, "gz", split_axis=0, concat_axis=0, tiled=True)
    return moved.reshape(BUFFER.shape)


def neighbours(plane, count):
    ahead = [(i, (i + 1) % count) for i in range(count)]
    behind = [((i + 1) % count, i) for i in range(count)]
    return lax.ppermute(plane, "gz", ahead), lax.ppermute(plane, "gz", behind)


def shards(
    order_param,
    concentration,
    strain,
    grain_ids,
    seed_labels,
    grain_moduli,
    grain_mobility,
    seed_rate,
):
    count = lax.axis_size("gz")
    order_now = order_param.reshape(N, N)
    conc_now = concentration.reshape(N, N)
    planes = strain.reshape(COMPS, N, N)
    order_halos = neighbours(order_now, count)
    conc_halos = neighbours(conc_now, count)
    lame, shear, kinetic, decay = coefficients(
        grain_moduli,
        grain_mobility,
        seed_rate,
        grain_ids.reshape(N, N),
        seed_labels.reshape(N, N),
        planes,
    )
    txf, mq, mz, mqi, txi = make_tables()
    for _ in range(SUBSTEPS - 1):
        order_new = order_step(order_now, conc_now, order_halos, kinetic, decay)
        order_halos = neighbours(order_new, count)
        conc_new = conc_step(conc_now, order_now, order_new, conc_halos)
        conc_halos = neighbours(conc_new, count)
        order_now, conc_now = order_new, conc_new
    spectra, order_next = forward(
        order_now, conc_now, order_halos, kinetic, decay, lame, shear, planes, txf, mq
    )
    conc_next = conc_step(conc_now, order_now, order_next, conc_halos)
    band = lax.axis_index("gz").astype(jnp.int32).reshape(1)
    returned = exchange(middle(band, exchange(spectra), mz))
    strain_next = inverse(returned, planes, mqi, txi)
    return (
        order_next.reshape(1, N, N),
        conc_next.reshape(1, N, N),
        strain_next.reshape(COMPS, 1, N, N),
    )


def solution(mesh):
    return jax.shard_map(
        shards,
        mesh=mesh,
        in_specs=(
            P("gz", None, None),
            P("gz", None, None),
            P(None, "gz", None, None),
            P("gz", None, None),
            P("gz", None, None),
            P(),
            P(),
            P(),
        ),
        out_specs=(P("gz", None, None), P("gz", None, None), P(None, "gz", None, None)),
        check_vma=False,
    )
```

time: 290 us -> 280 us (0.966)
  local copies, waits for them, and re-layouts: 39.9 us -> 17.6 us
  waiting for transfers between devices: 141 us -> 158 us
  starting transfers between devices: 54.5 us -> 46.1 us
  Pallas kernels: 51.9 us -> 56.6 us
    ppermute x8, waiting for transfers between devices: 13.8 us -> 83.2 us  [neighbours(): return (lax.ppermute(plane, 'gz', ahead), lax.ppermute(plane, 'gz', behind))]
    all_to_all x4 -> x2, waiting for transfers between devices: 127 us -> 74.8 us  [exchange(): lax.all_to_all(packed, 'gz', split_axis=0, concat_axis=0, tiled=True)]
    unnamed x66 -> x30, local copies, waits for them, and re-layouts: 39.9 us -> 17.6 us
    all_to_all x4 -> x2, starting transfers between devices: 24.4 us -> 16.1 us  [exchange(): lax.all_to_all(packed, 'gz', split_axis=0, concat_axis=0, tiled=True)]
    pallas_call x8 -> x6, Pallas kernels: 42.6 us -> 47.2 us  [the longest x1 14.3 us: forward(): pl.pallas_call(forward_body, grid=(XTILES + RADIX,), in_specs=[full(N, N)...]
  transfers between devices with their start and end apart: 12 -> 10, of which waited for: 6 -> 3; matrix products, arithmetic and copies ran while one was open for 0% -> 0% of each run, Pallas kernels for 11% -> 7%
where the time goes in v2:
time: 280 us; the launch traced here: 279 us
  waiting for transfers between devices  158 us (56%)
  Pallas kernels  56.6 us (20%)
  starting transfers between devices  46.1 us (16%)
  local copies, waits for them, and re-layouts  17.6 us (6%)
    ppermute x8, waiting for transfers between devices, neighbours(): return (lax.ppermute(plane, 'gz', ahead), lax.ppermute(plane, 'gz', behind))  83.2 us
    all_to_all x2, waiting for transfers between devices, exchange(): lax.all_to_all(packed, 'gz', split_axis=0, concat_axis=0, tiled=True)  74.8 us
    ppermute x8, starting transfers between devices, neighbours(): return (lax.ppermute(plane, 'gz', ahead), lax.ppermute(plane, 'gz', behind))  30 us
    unnamed x30, local copies, waits for them, and re-layouts  17.6 us
    all_to_all x2, starting transfers between devices, exchange(): lax.all_to_all(packed, 'gz', split_axis=0, concat_axis=0, tiled=True)  16.1 us
    pallas_call x1, Pallas kernels, forward(): pl.pallas_call(forward_body, grid=(XTILES + RADIX,), in_specs=[full(N, N)...  14.3 us
    pallas_call x1, Pallas kernels, inverse(): pl.pallas_call(inverse_body, grid=(PAIRS,), in_specs=[pl.BlockSpec(PAIR_B...  11.7 us
    pallas_call x1, Pallas kernels, middle(): pl.pallas_call(middle_body, grid=(RADIX,), in_specs=[pl.BlockSpec(memory_...  11.2 us
  transfers between devices with their start and end apart: 10, of which 3 were waited for; matrix products, arithmetic and copies ran while one was open for 0% of the time, Pallas kernels for 7%

profile of v2, /device:TPU:0, one launch (start us, length us, event | category | flops | bytes accessed | tf_op | source)
XLA Modules:
  0.0 279.0 jit_solution(6595686791876645104)
XLA Ops:
  0.7 8.3 %collective-permute-start.1 = (f32[512,512]{1,0:T(8,128)}, f32[512,512]{1,0:T(8,128)S(1)}, u32[]{:S(2)}, u32[]{:S(2)}) collective-permute-start(f32[512,512]{1,0:T(8,128)} %bitcast.20), channel_id=1, source_target_pairs={{1,0},{2,1},{3,2},{4,3},{5,4},{6,5},{7,6},{8,7},{9,8},{10,9},{11,1... | collective-permute-start | bytes 3145736 | tf_op jit(solution)/shard_map/ppermute | solution.py:538
  9.0 7.2 %collective-permute-start.3 = (f32[512,512]{1,0:T(8,128)}, f32[512,512]{1,0:T(8,128)S(1)}, u32[]{:S(2)}, u32[]{:S(2)}) collective-permute-start(f32[512,512]{1,0:T(8,128)} %bitcast.24), channel_id=1, source_target_pairs={{1,0},{2,1},{3,2},{4,3},{5,4},{6,5},{7,6},{8,7},{9,8},{10,9},{11,1... | collective-permute-start | bytes 3145736 | tf_op jit(solution)/shard_map/ppermute | solution.py:538
  16.2 2.8 copy-done
  19.0 1.2 copy-done.5
  20.2 1.2 copy-done.6
  21.4 0.7 copy-done.12
  22.1 0.7 copy-done.13
  22.7 0.7 copy-done.14
  23.4 6.1 %coefficients.1 = (f32[512,512]{1,0:T(8,128)S(1)}, f32[512,512]{1,0:T(8,128)S(1)}, f32[512,512]{1,0:T(8,128)S(1)}, f32[512,512]{1,0:T(8,128)S(1)}) custom-call(f32[2,16]{1,0:T(2,128)S(1)} %copy-done.12, f32[16]{0:T(128)S(1)} %copy-done.13, f32[8]{0:T(128)S(1)} %copy-done.14, s32[512,512]{1,0:T(8,128)S(1)} %bitcast.27, s32[512,512]{1,0:T(8,128)S(1)} %bitcast.28, ...), custom_call_target="tpu_custom_call" | custom-call | tf_op jit(solution)/shard_map/coefficients/pallas_call | solution.py:182
  29.5 3.1 %order_step.1.new_ref.p_ref = f32[512,512]{1,0:T(8,128)S(1)} custom-call(f32[512,512]{1,0:T(8,128)S(1)} %bitcast.21, f32[512,512]{1,0:T(8,128)S(1)} %bitcast.25, f32[512,512]{1,0:T(8,128)S(1)} %collective-permute-done.up_ref, f32[512,512]{1,0:T(8,128)S(1)} %collective-permute-done.1.down_ref, f32[512,512]{1,0:T(8,128)S(1)} %get-tuple-element.14.kin_ref, ...), custom_call_target="tpu_custom_call" | custom-call | tf_op jit(solution)/shard_map/order_step/pallas_call | solution.py:237
  32.7 0.1 collective-permute-start.4
  32.7 7.2 %collective-permute-start.5 = (f32[512,512]{1,0:T(8,128)S(1)}, f32[512,512]{1,0:T(8,128)S(1)}, u32[]{:S(2)}, u32[]{:S(2)}) collective-permute-start(f32[512,512]{1,0:T(8,128)S(1)} %order_step.1.new_ref.p_ref), channel_id=1, source_target_pairs={{1,0},{2,1},{3,2},{4,3},{5,4},{6,5},{7,6},{8,7},{9,8},{10,9},{11,1... | collective-permute-start | bytes 3145736 | tf_op jit(solution)/shard_map/ppermute | solution.py:538
  39.9 3.3 %tables.1 = (bf16[2,2,256,256]{3,2,1,0:T(8,128)(2,1)S(1)}, bf16[4,2,256,256]{3,2,1,0:T(8,128)(2,1)S(1)}, bf16[2,2,256,256]{3,2,1,0:T(8,128)(2,1)S(1)}, bf16[4,2,...) custom-call(), custom_call_target="tpu_custom_call" | custom-call | tf_op jit(solution)/shard_map/tables/pallas_call | solution.py:109
  43.2 0.8 copy-done.8
  44.0 0.8 copy-done.10
  44.8 3.1 %conc_step.2.c_ref = f32[512,512]{1,0:T(8,128)S(1)} custom-call(f32[512,512]{1,0:T(8,128)S(1)} %bitcast.26, f32[512,512]{1,0:T(8,128)S(1)} %bitcast.22, f32[512,512]{1,0:T(8,128)S(1)} %order_step.1.new_ref.p_ref, f32[512,512]{1,0:T(8,128)S(1)} %collective-permute-done.2.up_ref, f32[512,512]{1,0:T(8,128)S(1)} %collective-permute-done.3.down_ref), custom_call_target="tpu_custom_call" | custom-call | tf_op jit(solution)/shard_map/conc_step/pallas_call | solution.py:265
  47.9 4.5 %collective-permute-done.4.up_ref = f32[512,512]{1,0:T(8,128)S(1)} collective-permute-done((f32[512,512]{1,0:T(8,128)S(1)}, f32[512,512]{1,0:T(8,128)S(1)}, u32[]{:S(2)}, u32[]{:S(2)}) %collective-permute-start.4) | collective-permute-done | bytes 1048608 | tf_op jit(solution)/shard_map/ppermute | solution.py:538
  52.4 14.3 %forward.1 = (f32[128,3,4,8,128]{4,3,2,1,0:T(8,128)}, f32[512,512]{1,0:T(8,128)}) custom-call(f32[512,512]{1,0:T(8,128)S(1)} %order_step.1.new_ref.p_ref, f32[512,512]{1,0:T(8,128)S(1)} %conc_step.2.c_ref, f32[512,512]{1,0:T(8,128)S(1)} %collective-permute-done.4.up_ref, f32[512,512]{1,0:T(8,128)S(1)} %collective-permute-done.5.down_ref, ...), custom_call_target="tpu_custom_call" | custom-call | tf_op jit(solution)/shard_map/forward/pallas_call | solution.py:368
  66.7 9.8 %all-to-all-start = ((f32[128,96,128]{2,1,0:T(8,128)}), f32[128,96,128]{2,1,0:T(8,128)}, u32[]{:S(2)}, u32[]{:S(2)}) async-start(f32[128,96,128]{2,1,0:T(8,128)} %bitcast.30), calls=%async_computation | async-start | bytes 12582912 | tf_op jit(solution)/shard_map/all_to_all | solution.py:531
  76.5 74.8 %all-to-all-done = f32[128,96,128]{2,1,0:T(8,128)} async-done(((f32[128,96,128]{2,1,0:T(8,128)}), f32[128,96,128]{2,1,0:T(8,128)}, u32[]{:S(2)}, u32[]{:S(2)}) %all-to-all-start) | async-done | bytes 6291488 | tf_op jit(solution)/shard_map/all_to_all | solution.py:531
  151.2 1.0 copy-done.11
  152.3 11.2 %middle.1 = f32[128,3,4,8,128]{4,3,2,1,0:T(8,128)S(1)} custom-call(s32[1]{0:T(128)} %bitcast.7.band_ref, f32[128,3,4,8,128]{4,3,2,1,0:T(8,128)} %bitcast.9.in_ref, bf16[2,2,256,256]{3,2,1,0:T(8,128)(2,1)S(1)} %copy-done.11), custom_call_target="tpu_custom_call" | custom-call | tf_op jit(solution)/shard_map/middle/pallas_call | solution.py:464
  163.5 2.7 copy-done.2
  166.2 6.3 %all-to-all-start.1 = ((f32[128,96,128]{2,1,0:T(8,128)}), f32[128,96,128]{2,1,0:T(8,128)}, u32[]{:S(2)}, u32[]{:S(2)}) async-start(f32[128,96,128]{2,1,0:T(8,128)} %bitcast.18), calls=%async_computation.1 | async-start | bytes 12582912 | tf_op jit(solution)/shard_map/all_to_all | solution.py:531
  172.5 0.1 collective-permute-start.6
  172.6 7.2 %collective-permute-start.7 = (f32[512,512]{1,0:T(8,128)S(1)}, f32[512,512]{1,0:T(8,128)S(1)}, u32[]{:S(2)}, u32[]{:S(2)}) collective-permute-start(f32[512,512]{1,0:T(8,128)S(1)} %conc_step.2.c_ref), channel_id=1, source_target_pairs={{1,0},{2,1},{3,2},{4,3},{5,4},{6,5},{7,6},{8,7},{9,8},{10,9},{11,1... | collective-permute-start | bytes 3145736 | tf_op jit(solution)/shard_map/ppermute | solution.py:538
  179.8 78.7 %collective-permute-done.6.up_ref = f32[512,512]{1,0:T(8,128)S(1)} collective-permute-done((f32[512,512]{1,0:T(8,128)S(1)}, f32[512,512]{1,0:T(8,128)S(1)}, u32[]{:S(2)}, u32[]{:S(2)}) %collective-permute-start.6) | collective-permute-done | bytes 1048608 | tf_op jit(solution)/shard_map/ppermute | solution.py:538
  258.5 1.2 copy-done.7
  259.7 3.8 %conc_step.3 = f32[512,512]{1,0:T(8,128)} custom-call(f32[512,512]{1,0:T(8,128)S(1)} %conc_step.2.c_ref, f32[512,512]{1,0:T(8,128)S(1)} %order_step.1.new_ref.p_ref, f32[512,512]{1,0:T(8,128)S(1)} %copy-done.7, f32[512,512]{1,0:T(8,128)S(1)} %collective-permute-done.6.up_ref, f32[512,512]{1,0:T(8,128)S(1)} %collective-permute-done.7.down_ref), custom_call_target="tpu_custom_call" | custom-call | tf_op jit(solution)/shard_map/conc_step/pallas_call | solution.py:265
  263.4 2.8 copy-done.1
  266.2 1.0 copy-done.9
  267.3 11.7 %inverse.1 = f32[6,512,512]{2,1,0:T(8,128)} custom-call(f32[128,3,4,8,128]{4,3,2,1,0:T(8,128)} %bitcast.11.in_ref, f32[6,512,512]{2,1,0:T(8,128)S(1)} %bitcast.17, bf16[4,2,256,256]{3,2,1,0:T(8,128)(2,1)S(1)} %get-tuple-element.23.mqi_ref, bf16[2,2,256,256]{3,2,1,0:T(8,128)(2,1)S(1)} %copy-done.9), custom_call_target="tpu_custom_call" | custom-call | tf_op jit(solution)/shard_map/inverse/pallas_call | solution.py:513
  (26 shorter events, 0.1 us)
Async XLA Ops:
  0.6 28.8 %collective-permute-start = (f32[512,512]{1,0:T(8,128)}, f32[512,512]{1,0:T(8,128)S(1)}, u32[]{:S(2)}, u32[]{:S(2)}) collective-permute-start(f32[512,512]{1,0:T(8,128)} %bitcast.19), channel_id=1, source_target_pairs={{0,1},{1,2},{2,3},{3,4},{4,5},{5,6},{6,7},{7,8},{8,9},{9,10},{10,1... | collective-permute-start | bytes 3145736 | tf_op jit(solution)/shard_map/ppermute | solution.py:538
  0.7 28.8 %collective-permute-start.1 = (f32[512,512]{1,0:T(8,128)}, f32[512,512]{1,0:T(8,128)S(1)}, u32[]{:S(2)}, u32[]{:S(2)}) collective-permute-start(f32[512,512]{1,0:T(8,128)} %bitcast.20), channel_id=1, source_target_pairs={{1,0},{2,1},{3,2},{4,3},{5,4},{6,5},{7,6},{8,7},{9,8},{10,9},{11,1... | collective-permute-start | bytes 3145736 | tf_op jit(solution)/shard_map/ppermute | solution.py:538
  9.0 35.9 %collective-permute-start.2 = (f32[512,512]{1,0:T(8,128)}, f32[512,512]{1,0:T(8,128)S(1)}, u32[]{:S(2)}, u32[]{:S(2)}) collective-permute-start(f32[512,512]{1,0:T(8,128)} %bitcast.23), channel_id=1, source_target_pairs={{0,1},{1,2},{2,3},{3,4},{4,5},{5,6},{6,7},{7,8},{8,9},{9,10},{10,1... | collective-permute-start | bytes 3145736 | tf_op jit(solution)/shard_map/ppermute | solution.py:538
  9.0 35.9 %collective-permute-start.3 = (f32[512,512]{1,0:T(8,128)}, f32[512,512]{1,0:T(8,128)S(1)}, u32[]{:S(2)}, u32[]{:S(2)}) collective-permute-start(f32[512,512]{1,0:T(8,128)} %bitcast.24), channel_id=1, source_target_pairs={{1,0},{2,1},{3,2},{4,3},{5,4},{6,5},{7,6},{8,7},{9,8},{10,9},{11,1... | collective-permute-start | bytes 3145736 | tf_op jit(solution)/shard_map/ppermute | solution.py:538
  16.2 2.8 copy-start
  18.9 1.2 copy-start.5
  20.2 1.2 copy-start.6
  21.4 0.7 copy-start.12
  22.1 0.7 copy-start.13
  22.7 0.7 copy-start.14
  23.4 6.1 %copy-start.3 = (f32[1,512,512]{2,1,0:T(8,128)S(1)}, f32[1,512,512]{2,1,0:T(8,128)}, u32[]{:S(2)}) copy-start(f32[1,512,512]{2,1,0:T(8,128)} %param.8) | copy-start | bytes 3145732
  23.4 6.1 %copy-start.4 = (f32[1,512,512]{2,1,0:T(8,128)S(1)}, f32[1,512,512]{2,1,0:T(8,128)}, u32[]{:S(2)}) copy-start(f32[1,512,512]{2,1,0:T(8,128)} %param.9) | copy-start | bytes 3145732
  32.7 19.7 %collective-permute-start.4 = (f32[512,512]{1,0:T(8,128)S(1)}, f32[512,512]{1,0:T(8,128)S(1)}, u32[]{:S(2)}, u32[]{:S(2)}) collective-permute-start(f32[512,512]{1,0:T(8,128)S(1)} %order_step.1.new_ref.p_ref), channel_id=1, source_target_pairs={{0,1},{1,2},{2,3},{3,4},{4,5},{5,6},{6,7},{7,8},{8,9},{9,10},{10,1... | collective-permute-start | bytes 3145736 | tf_op jit(solution)/shard_map/ppermute | solution.py:538
  32.7 19.6 %collective-permute-start.5 = (f32[512,512]{1,0:T(8,128)S(1)}, f32[512,512]{1,0:T(8,128)S(1)}, u32[]{:S(2)}, u32[]{:S(2)}) collective-permute-start(f32[512,512]{1,0:T(8,128)S(1)} %order_step.1.new_ref.p_ref), channel_id=1, source_target_pairs={{1,0},{2,1},{3,2},{4,3},{5,4},{6,5},{7,6},{8,7},{9,8},{10,9},{11,1... | collective-permute-start | bytes 3145736 | tf_op jit(solution)/shard_map/ppermute | solution.py:538
  43.2 0.8 copy-start.8
  44.0 0.8 copy-start.10
  66.7 84.5 %all-to-all-start = ((f32[128,96,128]{2,1,0:T(8,128)}), f32[128,96,128]{2,1,0:T(8,128)}, u32[]{:S(2)}, u32[]{:S(2)}) async-start(f32[128,96,128]{2,1,0:T(8,128)} %bitcast.30), calls=%async_computation | async-start | bytes 12582912 | tf_op jit(solution)/shard_map/all_to_all | solution.py:531
  151.2 1.0 copy-start.11
  163.5 2.7 copy-start.2
  166.2 97.2 %all-to-all-start.1 = ((f32[128,96,128]{2,1,0:T(8,128)}), f32[128,96,128]{2,1,0:T(8,128)}, u32[]{:S(2)}, u32[]{:S(2)}) async-start(f32[128,96,128]{2,1,0:T(8,128)} %bitcast.18), calls=%async_computation.1 | async-start | bytes 12582912 | tf_op jit(solution)/shard_map/all_to_all | solution.py:531
  172.5 85.9 %collective-permute-start.6 = (f32[512,512]{1,0:T(8,128)S(1)}, f32[512,512]{1,0:T(8,128)S(1)}, u32[]{:S(2)}, u32[]{:S(2)}) collective-permute-start(f32[512,512]{1,0:T(8,128)S(1)} %conc_step.2.c_ref), channel_id=1, source_target_pairs={{0,1},{1,2},{2,3},{3,4},{4,5},{5,6},{6,7},{7,8},{8,9},{9,10},{10,1... | collective-permute-start | bytes 3145736 | tf_op jit(solution)/shard_map/ppermute | solution.py:538
  172.6 85.8 %collective-permute-start.7 = (f32[512,512]{1,0:T(8,128)S(1)}, f32[512,512]{1,0:T(8,128)S(1)}, u32[]{:S(2)}, u32[]{:S(2)}) collective-permute-start(f32[512,512]{1,0:T(8,128)S(1)} %conc_step.2.c_ref), channel_id=1, source_target_pairs={{1,0},{2,1},{3,2},{4,3},{5,4},{6,5},{7,6},{8,7},{9,8},{10,9},{11,1... | collective-permute-start | bytes 3145736 | tf_op jit(solution)/shard_map/ppermute | solution.py:538
  258.5 1.2 copy-start.7
  263.4 2.8 copy-start.1
  266.2 1.0 copy-start.9

commit v3 on v2

v3 whole, which is shorter than its diff:
```python
import functools
import math

import jax
import jax.numpy as jnp
from jax import lax
from jax.experimental import pallas as pl
from jax.experimental.pallas import tpu as pltpu
from jax.sharding import PartitionSpec as P

SUBSTEPS = 2
N = 512
HALF = 256
LANE = 128
DEPTH = 128
COMPS = 6
RADIX = 4
PAIRS = COMPS // 2
SUB = 8
BLOCKS = PAIRS * RADIX
ROWS = BLOCKS * SUB
PITCH = (BLOCKS + 1) * SUB

time_step = 0.05
grad_coef = 1.0
well_height = 1.0
drive_coef = 2.0
conc_eq = 0.5
mech_boost = 1.0
diffusivity = 1.0
release_coef = 1.0
residual_stiff = 0.1
lame_ref = 1.0
shear_ref = 1.0
coupling = (lame_ref + shear_ref) / (shear_ref * (lame_ref + 2.0 * shear_ref))

f32 = jnp.float32
bf16 = jnp.bfloat16
MIB = 1024 * 1024


def params(mib, dims=0):
    semantics = ("arbitrary",) * dims if dims else None
    return pltpu.CompilerParams(dimension_semantics=semantics, vmem_limit_bytes=mib * MIB)


def in_hbm(value):
    return pltpu.with_memory_space_constraint(value, pltpu.HBM)


RESIDENT = pl.BlockSpec(memory_space=pltpu.VMEM)
REMAIN = pl.BlockSpec(memory_space=pl.ANY)
SCALAR = pl.BlockSpec(memory_space=pltpu.SMEM)


def split(value):
    high = value.astype(bf16)
    low = (value - high.astype(f32)).astype(bf16)
    return high, low


def mul(left, right):
    return lax.dot_general(
        left, right, (((1,), (0,)), ((), ())), preferred_element_type=f32
    )


def table_times(table, value):
    high, low = split(value)
    return mul(table[0], high) + mul(table[0], low) + mul(table[1], high)


def times_table(value, table):
    high, low = split(value)
    return mul(high, table[0]) + mul(low, table[0]) + mul(high, table[1])


def unit_cos(index):
    wrapped = ((index + 256) & 511) - 256
    angle = (128 - jnp.abs(wrapped)).astype(f32) * (2.0 * math.pi / 512.0)
    square = angle * angle
    poly = 1.0 / 6227020800.0
    for power in (39916800.0, 362880.0, 5040.0, 120.0, 6.0):
        poly = 1.0 / power - square * poly
    return angle * (1.0 - square * poly)


def table_grid():
    rows = lax.broadcasted_iota(jnp.int32, (HALF, HALF), 0)
    cols = lax.broadcasted_iota(jnp.int32, (HALF, HALF), 1)
    turn = ((rows >> 7) - (cols >> 7)) * 128
    return rows, cols, rows & 127, cols & 127, turn


def put(ref, slot, value):
    high, low = split(value)
    ref[slot, 0] = high
    ref[slot, 1] = low


def onward_body(order_ref, txf_ref, mq_ref):
    rows, cols, row_low, col_low, turn = table_grid()
    for parity in range(2):
        wave = 2 * col_low + parity
        put(txf_ref, parity, unit_cos(rows * wave + (cols >> 7) * 128))
    for rest in range(RADIX):
        put(mq_ref, rest, unit_cos((4 * row_low + rest) * col_low + turn))


def backward_body(order_ref, mz_ref, mqi_ref, txi_ref):
    rows, cols, row_low, col_low, turn = table_grid()
    for parity in range(2):
        wave = 2 * row_low + parity
        weight = jnp.where(wave == 0, 1.0, 2.0) * (1.0 / float(N * N * DEPTH))
        put(txi_ref, parity, unit_cos(wave * cols + (rows >> 7) * 128) * weight)
    for rest in range(RADIX):
        put(mqi_ref, rest, unit_cos((4 * col_low + rest) * row_low - turn))
    put(mz_ref, 0, unit_cos(4 * row_low * col_low + turn))
    put(mz_ref, 1, unit_cos(4 * row_low * col_low - turn))


def tables_of(count):
    return (count, 2, HALF, HALF)


def table_call(body, counts, name, operand, spec):
    return pl.pallas_call(
        body,
        in_specs=[spec],
        out_shape=tuple(pltpu.HBM(tables_of(count), bf16) for count in counts),
        out_specs=tuple(RESIDENT for _ in counts),
        compiler_params=params(8),
        name=name,
    )(operand)


def onward_tables(ready):
    return table_call(onward_body, (2, 4), "onward_tables", ready, REMAIN)


def backward_tables(ready):
    return table_call(backward_body, (2, 4, 2), "backward_tables", ready, SCALAR)


TILE = 128
STRIP = 16


def strips(rows, body):
    def step(index, carry):
        body(pl.multiple_of(index * STRIP, STRIP))
        return carry

    lax.fori_loop(0, rows // STRIP, step, 0, unroll=True)


def lane_table(read, count):
    lanes = lax.broadcasted_iota(jnp.int32, (STRIP, LANE), 1)
    table = jnp.zeros((STRIP, LANE), f32)
    for index in range(count):
        table = jnp.where(lanes == index, read(index), table)
    return table


def pick(table, index):
    parts = [
        jnp.take_along_axis(table, index[:, LANE * k : LANE * (k + 1)], axis=1)
        for k in range(N // LANE)
    ]
    return jnp.concatenate(parts, axis=1)


def rows_of(index):
    return pl.ds(pl.multiple_of(index * TILE, TILE), TILE)


def stream(fetch, work, count=N // TILE):
    first = fetch(0)
    for copy in first:
        copy.start()
    for copy in first:
        copy.wait()
    for index in range(1, count):
        for copy in fetch(index):
            copy.start()

    def step(index, carry):
        @pl.when(index > 0)
        def _():
            for copy in fetch(index):
                copy.wait()

        work(index)
        return carry

    lax.fori_loop(0, count, step, 0)


def planes_of(source, target, rows, sems, index, base):
    return tuple(
        pltpu.make_async_copy(source.at[k, rows], target.at[k, rows], sems.at[index, base + k])
        for k in range(COMPS)
    )


def coef_body(
    moduli_hbm, mobility_hbm, rates_hbm, grain_ref, label_ref, strain_ref,
    unit_out, kin_out, dec_out, moduli, mobility, rates, lookup, sems,
):
    grains = mobility.shape[0]

    @pl.when(pl.program_id(0) == 0)
    def _():
        copies = [
            pltpu.make_async_copy(source, target, sems.at[k])
            for k, (source, target) in enumerate(
                ((moduli_hbm, moduli), (mobility_hbm, mobility), (rates_hbm, rates))
            )
        ]
        for copy in copies:
            copy.start()
        for copy in copies:
            copy.wait()
        lookup[0] = lane_table(lambda k: moduli[0, k], grains)
        lookup[1] = lane_table(lambda k: moduli[1, k], grains)
        lookup[2] = lane_table(lambda k: mobility[k], grains)
        lookup[3] = lane_table(lambda k: rates[k - 1] if k else 0.0, rates.shape[0] + 1)

    lames, shears, mobs, speeds = (lookup[k] for k in range(4))

    def strip(start):
        where = pl.ds(start, STRIP)
        grain = grain_ref[where, :]
        lame = pick(lames, grain)
        shear = pick(shears, grain)
        parts = [strain_ref[comp, where, :] for comp in range(COMPS)]
        trace = parts[0] + parts[1] + parts[2]
        square = (
            parts[0] * parts[0]
            + parts[1] * parts[1]
            + parts[2] * parts[2]
            + 2.0 * (parts[3] * parts[3] + parts[4] * parts[4] + parts[5] * parts[5])
        )
        energy = 0.5 * lame * trace * trace + shear * square
        mech = 1.0 + mech_boost * energy / (1.0 + energy)
        kin_out[where, :] = time_step * pick(mobs, grain) * mech
        dec_out[where, :] = time_step * pick(speeds, label_ref[where, :])
        spread = lame * trace
        double = 2.0 * shear
        for comp in range(COMPS):
            part = double * parts[comp]
            unit_out[comp, where, :] = part + spread if comp < 3 else part

    strips(TILE, strip)


PLANE = jax.ShapeDtypeStruct((N, N), f32)
TILES = N // TILE


def coefficients(moduli, mobility, rates, grain, label, strain):
    stripe = pl.BlockSpec((TILE, N), lambda i: (i, 0))
    stack = pl.BlockSpec((COMPS, TILE, N), lambda i: (0, i, 0))
    operands = (moduli, mobility, rates, grain, label, strain)
    return pl.pallas_call(
        coef_body,
        grid=(TILES,),
        in_specs=[REMAIN, REMAIN, REMAIN, stripe, stripe, stack],
        out_specs=[stack, stripe, stripe],
        out_shape=[pltpu.VMEM((COMPS, N, N), f32), pltpu.VMEM((N, N), f32), pltpu.VMEM((N, N), f32)],
        scratch_shapes=[
            pltpu.SMEM(moduli.shape, f32),
            pltpu.SMEM(mobility.shape, f32),
            pltpu.SMEM(rates.shape, f32),
            pltpu.VMEM((4, STRIP, LANE), f32),
            pltpu.SemaphoreType.DMA((3,)),
        ],
        compiler_params=params(16, 1),
        name="coefficients",
    )(*map(in_hbm, operands))


def planar_sum(ref, start):
    center = ref[pl.ds(start, STRIP), :]
    before = ref[pl.ds(pl.multiple_of((start + N - 8) & (N - 1), 8), 8), :]
    after = ref[pl.ds(pl.multiple_of((start + STRIP) & (N - 1), 8), 8), :]
    tall = jnp.concatenate([before, center, after], axis=0)
    height = STRIP + 16
    above = pltpu.roll(tall, 1, 0)[8 : 8 + STRIP]
    below = pltpu.roll(tall, height - 1, 0)[8 : 8 + STRIP]
    sides = pltpu.roll(center, 1, 1) + pltpu.roll(center, N - 1, 1)
    return center, (above + below) + sides


def next_order(p_ref, start, halo_sum, conc_now, kinetic, decay):
    order_now, order_sum = planar_sum(p_ref, start)
    lap_order = order_sum + halo_sum - 6.0 * order_now
    slope = order_now * (1.0 - order_now)
    well_grad = 2.0 * slope * (1.0 - 2.0 * order_now)
    force = (
        grad_coef * lap_order
        - well_height * well_grad
        + drive_coef * 6.0 * slope * (conc_now - conc_eq)
    )
    return order_now + kinetic * force - decay * order_now


def tiles(body):
    def step(index, carry):
        base = pl.multiple_of(index * TILE, TILE)
        strips(TILE, lambda local: body(pl.multiple_of(base + local, STRIP)))
        return carry

    lax.fori_loop(0, N // TILE, step, 0)


def order_body(p_ref, c_ref, up_ref, down_ref, kin_ref, dec_ref, p_out):
    def strip(start):
        where = pl.ds(start, STRIP)
        p_out[where, :] = next_order(
            p_ref,
            start,
            up_ref[where, :] + down_ref[where, :],
            c_ref[where, :],
            kin_ref[where, :],
            dec_ref[where, :],
        )

    tiles(strip)


def order_step(order_now, conc_now, halos, kinetic, decay):
    planes = (order_now, conc_now, *halos, kinetic, decay)
    return pl.pallas_call(
        order_body,
        in_specs=[RESIDENT] * 6,
        out_specs=RESIDENT,
        out_shape=PLANE,
        compiler_params=params(8),
        name="order_step",
    )(*planes)


def next_conc(c_ref, start, halo_sum, order_now, order_new):
    conc_now, conc_sum = planar_sum(c_ref, start)
    lap_conc = conc_sum + halo_sum - 6.0 * conc_now
    return (
        conc_now + time_step * diffusivity * lap_conc + release_coef * (order_now - order_new)
    )


def conc_body(c_ref, p_ref, new_ref, up_ref, down_ref, *refs):
    c_out = refs[-1]

    def strip(start):
        where = pl.ds(start, STRIP)
        halo_sum = up_ref[where, :] + down_ref[where, :]
        c_out[where, :] = next_conc(c_ref, start, halo_sum, p_ref[where, :], new_ref[where, :])

    tiles(strip)


def conc_step(conc_now, order_now, order_new, halos, after=()):
    planes = (conc_now, order_now, order_new, *halos)
    return pl.pallas_call(
        conc_body,
        in_specs=[RESIDENT] * 5 + [REMAIN] * len(after),
        out_specs=RESIDENT,
        out_shape=PLANE,
        compiler_params=params(8),
        name="conc_step",
    )(*planes, *map(in_hbm, after))


def butterflies(spectra, comp, lanes_r, lanes_i, odd):
    reals = [spectra[comp, pl.ds(LANE * j, LANE), lanes_r] for j in range(RADIX)]
    imags = [spectra[comp, pl.ds(LANE * j, LANE), lanes_i] for j in range(RADIX)]
    if odd:
        er, ei = reals[0] - reals[2], imags[0] - imags[2]
        turned_r, turned_i = imags[1] - imags[3], reals[3] - reals[1]
    else:
        er, ei = reals[0] + reals[2], imags[0] + imags[2]
        turned_r, turned_i = reals[1] + reals[3], imags[1] + imags[3]
    return (er + turned_r, ei + turned_i), (er - turned_r, ei - turned_i)


def forward_body(
    p_ref, c_ref, up_hbm, down_hbm, kin_hbm, dec_hbm, unit_hbm, txf_hbm, mq_hbm,
    out_ref, p_hbm, up_ref, down_ref, kin_ref, dec_ref, unit_ref, txf_ref, mq_ref, p_out, spectra, packed, highs, lows,
    in_sems, table_sems, order_sems, sems,
):
    def fetch(index):
        rows = rows_of(index)
        singles = (
            (up_hbm, up_ref),
            (down_hbm, down_ref),
            (kin_hbm, kin_ref),
            (dec_hbm, dec_ref),
        )
        return (
            *(
                pltpu.make_async_copy(source.at[rows], target.at[rows], in_sems.at[index, COMPS + k])
                for k, (source, target) in enumerate(singles)
            ),
            *planes_of(unit_hbm, unit_ref, rows, in_sems, index, 0),
        )

    def keep(index):
        rows = rows_of(index)
        return pltpu.make_async_copy(p_out.at[rows], p_hbm.at[rows], order_sems.at[index])

    txf_copy = pltpu.make_async_copy(txf_hbm, txf_ref, table_sems.at[0])
    mq_copy = pltpu.make_async_copy(mq_hbm, mq_ref, table_sems.at[1])
    txf_copy.start()

    def tile(index):
        base = pl.multiple_of(index * TILE, TILE)

        def strip(local):
            start = pl.multiple_of(base + local, STRIP)
            where = pl.ds(start, STRIP)
            order = next_order(
                p_ref,
                start,
                up_ref[where, :] + down_ref[where, :],
                c_ref[where, :],
                kin_ref[where, :],
                dec_ref[where, :],
            )
            p_out[where, :] = order
            scale = order * order * (3.0 - 2.0 * order) + residual_stiff
            for comp in range(COMPS):
                part = scale * unit_ref[comp, where, :]
                left = part[:, :HALF]
                right = part[:, HALF:]
                here = pl.ds(pl.multiple_of(comp * TILE + local, STRIP), STRIP)
                for parity, folded in ((0, left + right), (1, left - right)):
                    highs[parity, here, :], lows[parity, here, :] = split(folded)

        strips(TILE, strip)
        keep(index).start()

        @pl.when(index == 0)
        def _():
            mq_copy.start()
            txf_copy.wait()

        for parity in range(2):
            high = highs[parity]
            result = (
                mul(high, txf_ref[parity, 0])
                + mul(lows[parity], txf_ref[parity, 0])
                + mul(high, txf_ref[parity, 1])
            )
            for comp in range(COMPS):
                spectra[comp, pl.ds(base, TILE), pl.ds(HALF * parity, HALF)] = result[
                    comp * TILE : (comp + 1) * TILE
                ]

    stream(fetch, tile)
    mq_copy.wait()

    flat = packed.reshape(LANE * PITCH, LANE)
    copies = []
    for odd in range(2):
        for pair in range(PAIRS):
            for parity in range(2):
                lanes_r = pl.ds(HALF * parity, LANE)
                lanes_i = pl.ds(HALF * parity + LANE, LANE)
                both = [butterflies(spectra, 2 * pair + k, lanes_r, lanes_i, odd) for k in (0, 1)]
                for half in range(2):
                    rest = odd + 2 * half
                    real = jnp.concatenate([both[0][half][0], both[1][half][0]], axis=1)
                    imag = jnp.concatenate([both[0][half][1], both[1][half][1]], axis=1)
                    value = jnp.concatenate([real, imag], axis=0)
                    result = table_times((mq_ref[rest, 0], mq_ref[rest, 1]), value)
                    give_pair(flat, (pair * RADIX + rest) * SUB + parity * 4, result)
            for rest in (odd, odd + 2):
                block = pair * RADIX + rest
                copy = pltpu.make_async_copy(packed.at[:, block], out_ref.at[:, block], sems.at[block])
                copy.start()
                copies.append(copy)
    for copy in copies:
        copy.wait()
    for index in range(N // TILE):
        keep(index).wait()


def give_pair(flat, row, result):
    for k in (0, 1):
        lanes = slice(LANE * k, LANE * (k + 1))
        flat[pl.ds(row + 2 * k, LANE, stride=PITCH), :] = result[:LANE, lanes]
        flat[pl.ds(row + 2 * k + 1, LANE, stride=PITCH), :] = result[LANE:, lanes]


def take_pair(flat, row):
    reals, imags = [], []
    for k in (0, 1):
        reals.append(flat[pl.ds(row + 2 * k, LANE, stride=PITCH), :])
        imags.append(flat[pl.ds(row + 2 * k + 1, LANE, stride=PITCH), :])
    return jnp.concatenate(
        [jnp.concatenate(reals, axis=1), jnp.concatenate(imags, axis=1)], axis=0
    )


SHAPE = (LANE, BLOCKS, SUB, LANE)
SPACED = (LANE, BLOCKS + 1, SUB, LANE)
BUFFER = pltpu.HBM(SHAPE, f32)


def forward(order, conc, halos, kinetic, decay, unit, txf, mq):
    return pl.pallas_call(
        forward_body,
        in_specs=[RESIDENT] * 2 + [REMAIN] * 7,
        out_specs=(REMAIN, REMAIN),
        out_shape=(BUFFER, pltpu.HBM((N, N), f32)),
        scratch_shapes=[
            *[pltpu.VMEM((N, N), f32)] * 4,
            pltpu.VMEM((COMPS, N, N), f32),
            pltpu.VMEM(tables_of(2), bf16),
            pltpu.VMEM(tables_of(4), bf16),
            pltpu.VMEM((N, N), f32),
            pltpu.VMEM((COMPS, N, N), f32),
            pltpu.VMEM(SPACED, f32),
            pltpu.VMEM((2, COMPS * TILE, HALF), bf16),
            pltpu.VMEM((2, COMPS * TILE, HALF), bf16),
            pltpu.SemaphoreType.DMA((N // TILE, COMPS + 4)),
            pltpu.SemaphoreType.DMA((2,)),
            pltpu.SemaphoreType.DMA((N // TILE,)),
            pltpu.SemaphoreType.DMA((BLOCKS,)),
        ],
        compiler_params=params(40),
        name="forward",
    )(order, conc, *map(in_hbm, (*halos, kinetic, decay, unit, txf, mq)))


def middle_body(
    band_ref, in_ref, mz_hbm, out_ref, received, mz_ref, packed, in_sems, out_sems, table_sem
):
    source = received.reshape(LANE * PITCH, LANE)
    flat = packed.reshape(LANE * PITCH, LANE)

    def fetch(pair, rest):
        block = pair * RADIX + rest
        return pltpu.make_async_copy(in_ref.at[:, block], received.at[:, block], in_sems.at[block])

    def send(pair, rest):
        block = pair * RADIX + rest
        return pltpu.make_async_copy(packed.at[:, block], out_ref.at[:, block], out_sems.at[block])

    mz_copy = pltpu.make_async_copy(mz_hbm, mz_ref, table_sem)
    for pair in range(PAIRS):
        fetch(pair, 0).start()
    mz_copy.start()
    for pair in range(PAIRS):
        fetch(pair, 0).wait()
    for rest in range(1, RADIX):
        for pair in range(PAIRS):
            fetch(pair, rest).start()
    mz_copy.wait()

    def step(rest, carry):
        @pl.when(rest > 0)
        def _():
            for pair in range(PAIRS):
                fetch(pair, rest).wait()

        middle_step(band_ref, source, mz_ref, flat, rest)
        for pair in range(PAIRS):
            send(pair, rest).start()
        return carry

    lax.fori_loop(0, RADIX, step, 0)
    for rest in range(RADIX):
        for pair in range(PAIRS):
            send(pair, rest).wait()


def middle_step(band_ref, source, mz_ref, flat, rest):
    onward = (mz_ref[0, 0], mz_ref[0, 1])
    backward = (mz_ref[1, 0], mz_ref[1, 1])
    shape = (DEPTH, LANE)
    depth_index = lax.broadcasted_iota(jnp.int32, shape, 0)
    xi_z = jnp.where(depth_index < DEPTH // 2, depth_index, depth_index - DEPTH).astype(f32)
    wave_y = band_ref[0] * RADIX + rest
    xi_y = jnp.where(wave_y < N // 2, wave_y, wave_y - N).astype(f32)
    for parity in range(2):
        tau_r, tau_i = [], []
        for pair in range(PAIRS):
            result = table_times(onward, take_pair(source, (pair * RADIX + rest) * SUB + parity * 4))
            for k in (0, 1):
                lanes = slice(LANE * k, LANE * (k + 1))
                tau_r.append(result[:LANE, lanes])
                tau_i.append(result[LANE:, lanes])
        xi_x = (2 * lax.broadcasted_iota(jnp.int32, shape, 1) + parity).astype(f32)
        wave_sq = xi_x * xi_x + xi_y * xi_y + xi_z * xi_z
        live = (wave_sq > 0.5) & (xi_x < float(HALF))
        safe = jnp.where(live, wave_sq, 1.0)
        inverse = 1.0 / safe
        first = jnp.where(live, (0.5 / shear_ref) * inverse, 0.0)
        second = jnp.where(live, (0.5 * coupling) * (inverse * inverse), 0.0)
        grids = []
        for tau in (tau_r, tau_i):
            t_xx, t_yy, t_zz, t_yz, t_xz, t_xy = tau
            v_x = t_xx * xi_x + t_xy * xi_y + t_xz * xi_z
            v_y = t_xy * xi_x + t_yy * xi_y + t_yz * xi_z
            v_z = t_xz * xi_x + t_yz * xi_y + t_zz * xi_z
            inner = (xi_x * v_x + xi_y * v_y + xi_z * v_z) * second
            h_x = v_x * first - xi_x * inner
            h_y = v_y * first - xi_y * inner
            h_z = v_z * first - xi_z * inner
            grids.append(
                (
                    2.0 * xi_x * h_x,
                    2.0 * xi_y * h_y,
                    2.0 * xi_z * h_z,
                    xi_z * h_y + xi_y * h_z,
                    xi_z * h_x + xi_x * h_z,
                    xi_y * h_x + xi_x * h_y,
                )
            )
        for pair in range(PAIRS):
            real = jnp.concatenate([grids[0][pair * 2], grids[0][pair * 2 + 1]], axis=1)
            imag = jnp.concatenate([grids[1][pair * 2], grids[1][pair * 2 + 1]], axis=1)
            result = table_times(backward, jnp.concatenate([real, imag], axis=0))
            give_pair(flat, (pair * RADIX + rest) * SUB + parity * 4, result)


def middle(band, received, mz):
    return pl.pallas_call(
        middle_body,
        in_specs=[SCALAR, REMAIN, REMAIN],
        out_specs=REMAIN,
        out_shape=BUFFER,
        scratch_shapes=[
            pltpu.VMEM(SPACED, f32),
            pltpu.VMEM(tables_of(2), bf16),
            pltpu.VMEM(SPACED, f32),
            pltpu.SemaphoreType.DMA((BLOCKS,)),
            pltpu.SemaphoreType.DMA((BLOCKS,)),
            pltpu.SemaphoreType.DMA(()),
        ],
        compiler_params=params(24),
        name="middle",
    )(band, in_hbm(received), in_hbm(mz))


def inverse_y(source, mqi_ref, pair, parity):
    blocks = []
    for rest in range(RADIX):
        value = take_pair(source, (pair * RADIX + rest) * SUB + parity * 4)
        result = table_times((mqi_ref[rest, 0], mqi_ref[rest, 1]), value)
        blocks.append((result[:LANE], result[LANE:]))
    er0, er1 = blocks[0][0] + blocks[2][0], blocks[0][0] - blocks[2][0]
    ei0, ei1 = blocks[0][1] + blocks[2][1], blocks[0][1] - blocks[2][1]
    or0, or1 = blocks[1][0] + blocks[3][0], blocks[1][0] - blocks[3][0]
    oi0, oi1 = blocks[1][1] + blocks[3][1], blocks[1][1] - blocks[3][1]
    return (
        (er0 + or0, ei0 + oi0),
        (er1 - oi1, ei1 + or1),
        (er0 - or0, ei0 - oi0),
        (er1 + oi1, ei1 - or1),
    )


def inverse_body(
    in_ref, strain_hbm, mqi_hbm, txi_hbm, out_ref, received, strain_ref, mqi_ref, txi_ref, moved,
    in_sems, strain_sems, table_sems, sems,
):
    source = received.reshape(LANE * PITCH, LANE)

    def fetch(pair, rest):
        block = pair * RADIX + rest
        return pltpu.make_async_copy(in_ref.at[:, block], received.at[:, block], in_sems.at[block])

    def fetch_strain(comp):
        return pltpu.make_async_copy(strain_hbm.at[comp], strain_ref.at[comp], strain_sems.at[comp])

    mqi_copy = pltpu.make_async_copy(mqi_hbm, mqi_ref, table_sems.at[0])
    txi_copy = pltpu.make_async_copy(txi_hbm, txi_ref, table_sems.at[1])
    def copy_of(comp):
        return pltpu.make_async_copy(moved.at[comp], out_ref.at[comp], sems.at[comp])

    for rest in range(RADIX):
        fetch(0, rest).start()
    mqi_copy.start()
    txi_copy.start()
    for rest in range(RADIX):
        fetch(0, rest).wait()
    mqi_copy.wait()
    txi_copy.wait()
    for pair in range(PAIRS):
        for k in (0, 1):
            fetch_strain(2 * pair + k).start()
        if pair + 1 < PAIRS:
            for rest in range(RADIX):
                fetch(pair + 1, rest).start()

    def step(pair, carry):
        @pl.when(pair > 0)
        def _():
            for rest in range(RADIX):
                fetch(pair, rest).wait()

        planes = [inverse_y(source, mqi_ref, pair, parity) for parity in range(2)]
        for k in (0, 1):
            fetch_strain(2 * pair + k).wait()
        for k in (0, 1):
            comp = pair * 2 + k
            lanes = slice(LANE * k, LANE * (k + 1))
            halves = []
            for parity in range(2):
                value = jnp.concatenate(
                    [
                        jnp.concatenate([real[:, lanes], imag[:, lanes]], axis=1)
                        for real, imag in planes[parity]
                    ],
                    axis=0,
                )
                halves.append(times_table(value, (txi_ref[parity, 0], txi_ref[parity, 1])))
            even, odd = halves
            left = pl.ds(0, HALF)
            right = pl.ds(HALF, HALF)
            moved[comp, :, left] = strain_ref[comp, :, left] - (even + odd)
            moved[comp, :, right] = strain_ref[comp, :, right] - (even - odd)
            copy_of(comp).start()
        return carry

    lax.fori_loop(0, PAIRS, step, 0)
    for comp in range(COMPS):
        copy_of(comp).wait()


def inverse(returned, strain, mqi, txi):
    return pl.pallas_call(
        inverse_body,
        in_specs=[REMAIN] * 4,
        out_specs=REMAIN,
        out_shape=pltpu.HBM((COMPS, N, N), f32),
        scratch_shapes=[
            pltpu.VMEM(SPACED, f32),
            pltpu.VMEM((COMPS, N, N), f32),
            pltpu.VMEM(tables_of(4), bf16),
            pltpu.VMEM(tables_of(2), bf16),
            pltpu.VMEM((COMPS, N, N), f32),
            pltpu.SemaphoreType.DMA((BLOCKS,)),
            pltpu.SemaphoreType.DMA((COMPS,)),
            pltpu.SemaphoreType.DMA((2,)),
            pltpu.SemaphoreType.DMA((COMPS,)),
        ],
        compiler_params=params(32),
        name="inverse",
    )(in_hbm(returned), in_hbm(strain), in_hbm(mqi), in_hbm(txi))


def exchange(block):
    packed = block.reshape(DEPTH, ROWS, LANE)
    moved = lax.all_to_all(packed, "gz", split_axis=0, concat_axis=0, tiled=True)
    return moved.reshape(SHAPE)


def neighbours(plane, count):
    ahead = [(i, (i + 1) % count) for i in range(count)]
    behind = [((i + 1) % count, i) for i in range(count)]
    return lax.ppermute(plane, "gz", ahead), lax.ppermute(plane, "gz", behind)


def shards(
    order_param,
    concentration,
    strain,
    grain_ids,
    seed_labels,
    grain_moduli,
    grain_mobility,
    seed_rate,
):
    count = lax.axis_size("gz")
    order_now = order_param.reshape(N, N)
    conc_now = concentration.reshape(N, N)
    planes = strain.reshape(COMPS, N, N)
    order_halos = neighbours(order_now, count)
    conc_halos = neighbours(conc_now, count)
    unit, kinetic, decay = coefficients(
        grain_moduli,
        grain_mobility,
        seed_rate,
        grain_ids.reshape(N, N),
        seed_labels.reshape(N, N),
        planes,
    )
    for _ in range(SUBSTEPS - 1):
        order_new = order_step(order_now, conc_now, order_halos, kinetic, decay)
        order_halos = neighbours(order_new, count)
        txf, mq = onward_tables(conc_halos[0])
        conc_new = conc_step(conc_now, order_now, order_new, conc_halos, (txf,))
        conc_halos = neighbours(conc_new, count)
        order_now, conc_now = order_new, conc_new
    spectra, order_next = forward(
        order_now, conc_now, order_halos, kinetic, decay, unit, txf, mq
    )
    band = lax.axis_index("gz").astype(jnp.int32).reshape(1)
    spectra, band, conc_halos = lax.optimization_barrier((spectra, band, conc_halos))
    received = exchange(spectra)
    mz, mqi, txi = backward_tables(band)
    conc_next = conc_step(conc_now, order_now, order_next, conc_halos)
    returned = exchange(middle(band, received, mz))
    strain_next = inverse(returned, planes, mqi, txi)
    return (
        order_next.reshape(1, N, N),
        conc_next.reshape(1, N, N),
        strain_next.reshape(COMPS, 1, N, N),
    )


def solution(mesh):
    return jax.shard_map(
        shards,
        mesh=mesh,
        in_specs=(
            P("gz", None, None),
            P("gz", None, None),
            P(None, "gz", None, None),
            P("gz", None, None),
            P("gz", None, None),
            P(),
            P(),
            P(),
        ),
        out_specs=(P("gz", None, None), P("gz", None, None), P(None, "gz", None, None)),
        check_vma=False,
    )
```

time: 280 us -> 248 us (0.89)
  local copies, waits for them, and re-layouts: 17.6 us -> 2.21 us
  waiting for transfers between devices: 158 us -> 145 us
  Pallas kernels: 56.6 us -> 52.7 us
    ppermute x8, waiting for transfers between devices: 83.2 us -> 2.06 us  [neighbours(): return (lax.ppermute(plane, 'gz', ahead), lax.ppermute(plane, 'gz', behind))]
    all_to_all x2, waiting for transfers between devices: 74.8 us -> 143 us  [exchange(): lax.all_to_all(packed, 'gz', split_axis=0, concat_axis=0, tiled=True)]
    unnamed x30 -> x16, local copies, waits for them, and re-layouts: 17.6 us -> 2.21 us
    pallas_call x8 -> x9, Pallas kernels: 56.6 us -> 52.7 us  [the longest x1 12.9 us: forward(): pl.pallas_call(forward_body, in_specs=[RESIDENT] * 2 + [REMAIN] * 7, out_...]
  transfers between devices with their start and end apart: 10 -> 10, of which waited for: 3 -> 4; matrix products, arithmetic and copies ran while one was open for 0% -> 0% of each run, Pallas kernels for 7% -> 12%
where the time goes in v3:
time: 248 us; the launch traced here: 247 us
  waiting for transfers between devices  145 us (58%)
  Pallas kernels  52.7 us (21%)
  starting transfers between devices  46.2 us (19%)
    all_to_all x2, waiting for transfers between devices, exchange(): lax.all_to_all(packed, 'gz', split_axis=0, concat_axis=0, tiled=True)  143 us
    ppermute x8, starting transfers between devices, neighbours(): return (lax.ppermute(plane, 'gz', ahead), lax.ppermute(plane, 'gz', behind))  30 us
    all_to_all x2, starting transfers between devices, exchange(): lax.all_to_all(packed, 'gz', split_axis=0, concat_axis=0, tiled=True)  16.2 us
    pallas_call x1, Pallas kernels, forward(): pl.pallas_call(forward_body, in_specs=[RESIDENT] * 2 + [REMAIN] * 7, out_...  12.9 us
    pallas_call x1, Pallas kernels, middle(): pl.pallas_call(middle_body, in_specs=[SCALAR, REMAIN, REMAIN], out_specs=...  11.8 us
    pallas_call x1, Pallas kernels, inverse(): pl.pallas_call(inverse_body, in_specs=[REMAIN] * 4, out_specs=REMAIN, out...  10.6 us
    pallas_call x1, Pallas kernels, coefficients(): pl.pallas_call(coef_body, grid=(TILES,), in_specs=[REMAIN, REMAIN, REMAIN...  6.82 us
    pallas_call x2, Pallas kernels, table_call(): pl.pallas_call(body, in_specs=[spec], out_shape=tuple((pltpu.HBM(tables_o...  5.38 us
  transfers between devices with their start and end apart: 10, of which 4 were waited for; matrix products, arithmetic and copies ran while one was open for 0% of the time, Pallas kernels for 12%

profile of v3, /device:TPU:0, one launch (start us, length us, event | category | flops | bytes accessed | tf_op | source)
XLA Modules:
  0.0 246.7 jit_solution(1809299018460106031)
XLA Ops:
  0.7 0.1 collective-permute-start
  0.7 8.3 %collective-permute-start.1 = (f32[512,512]{1,0:T(8,128)}, f32[512,512]{1,0:T(8,128)S(1)}, u32[]{:S(2)}, u32[]{:S(2)}) collective-permute-start(f32[512,512]{1,0:T(8,128)} %bitcast.16), channel_id=1, source_target_pairs={{1,0},{2,1},{3,2},{4,3},{5,4},{6,5},{7,6},{8,7},{9,8},{10,9},{11,1... | collective-permute-start | bytes 3145736 | tf_op jit(solution)/shard_map/ppermute | solution.py:765
  9.0 7.2 %collective-permute-start.3 = (f32[512,512]{1,0:T(8,128)}, f32[512,512]{1,0:T(8,128)S(1)}, u32[]{:S(2)}, u32[]{:S(2)}) collective-permute-start(f32[512,512]{1,0:T(8,128)} %bitcast.20), channel_id=1, source_target_pairs={{1,0},{2,1},{3,2},{4,3},{5,4},{6,5},{7,6},{8,7},{9,8},{10,9},{11,1... | collective-permute-start | bytes 3145736 | tf_op jit(solution)/shard_map/ppermute | solution.py:765
  16.2 6.8 %coefficients.1 = (f32[6,512,512]{2,1,0:T(8,128)S(1)}, f32[512,512]{1,0:T(8,128)S(1)}, f32[512,512]{1,0:T(8,128)S(1)}) custom-call(f32[2,16]{1,0:T(2,128)} %moduli_hbm.1, f32[16]{0:T(128)} %mobility_hbm.1, f32[8]{0:T(128)} %rates_hbm.1, s32[512,512]{1,0:T(8,128)} %bitcast.29, s32[512,512]{1,0:T(8,128)} %bitcast.30, f32[6,512,512]{2,1,0:T(8,128)} %bitcast.25), custom_call_target="tpu_custom_call" | custom-call | tf_op jit(solution)/shard_map/coefficients/pallas_call | solution.py:265
  23.0 0.0 copy-start
  23.0 0.0 collective-permute-done.up_ref
  23.1 0.0 collective-permute-done.1.down_ref
  23.1 1.1 order_step.1.new_ref.p_ref
  24.2 0.1 collective-permute-start.4
  24.3 7.2 %collective-permute-start.5 = (f32[512,512]{1,0:T(8,128)S(1)}, f32[512,512]{1,0:T(8,128)}, u32[]{:S(2)}, u32[]{:S(2)}) collective-permute-start(f32[512,512]{1,0:T(8,128)S(1)} %order_step.1.new_ref.p_ref), channel_id=1, source_target_pairs={{1,0},{2,1},{3,2},{4,3},{5,4},{6,5},{7,6},{8,7},{9,8},{10,9},{11,1... | collective-permute-start | bytes 3145736 | tf_op jit(solution)/shard_map/ppermute | solution.py:765
  31.4 1.4 collective-permute-done.2.order_ref.up_ref
  32.9 2.5 %onward_tables.1 = (bf16[2,2,256,256]{3,2,1,0:T(8,128)(2,1)}, bf16[4,2,256,256]{3,2,1,0:T(8,128)(2,1)}) custom-call(f32[512,512]{1,0:T(8,128)S(1)} %collective-permute-done.2.order_ref.up_ref), custom_call_target="tpu_custom_call" | custom-call | tf_op jit(solution)/shard_map/onward_tables/pallas_call | solution.py:127
  35.4 0.0 collective-permute-done.3.down_ref
  35.4 0.9 conc_step.2.c_ref
  36.3 0.1 collective-permute-start.6
  36.4 7.2 %collective-permute-start.7 = (f32[512,512]{1,0:T(8,128)S(1)}, f32[512,512]{1,0:T(8,128)S(1)}, u32[]{:S(2)}, u32[]{:S(2)}) collective-permute-start(f32[512,512]{1,0:T(8,128)S(1)} %conc_step.2.c_ref), channel_id=1, source_target_pairs={{1,0},{2,1},{3,2},{4,3},{5,4},{6,5},{7,6},{8,7},{9,8},{10,9},{11,1... | collective-permute-start | bytes 3145736 | tf_op jit(solution)/shard_map/ppermute | solution.py:765
  43.6 0.6 collective-permute-done.4.up_hbm
  44.2 12.9 %forward.1 = (f32[128,12,8,128]{3,2,1,0:T(8,128)}, f32[512,512]{1,0:T(8,128)}) custom-call(f32[512,512]{1,0:T(8,128)S(1)} %order_step.1.new_ref.p_ref, f32[512,512]{1,0:T(8,128)S(1)} %conc_step.2.c_ref, f32[512,512]{1,0:T(8,128)} %collective-permute-done.4.up_hbm, f32[512,512]{1,0:T(8,128)} %collective-permute-done.5.down_hbm, f32[512,512]{1,0:T(8,128)} %copy-done.1, ...), custom_call_target="tpu_custom_call" | custom-call | tf_op jit(solution)/shard_map/forward/pallas_call | solution.py:512
  57.1 0.0 collective-permute-done.6.up_ref
  57.1 0.0 copy-start.6
  57.2 1.0 copy-done.6
  58.1 9.8 %all-to-all-start = ((f32[128,96,128]{2,1,0:T(8,128)}), f32[128,96,128]{2,1,0:T(8,128)}, u32[]{:S(2)}, u32[]{:S(2)}) async-start(f32[128,96,128]{2,1,0:T(8,128)} %bitcast.27), calls=%async_computation | async-start | bytes 12582912 | tf_op jit(solution)/shard_map/all_to_all | solution.py:758
  68.0 2.9 %backward_tables.1 = (bf16[2,2,256,256]{3,2,1,0:T(8,128)(2,1)}, bf16[4,2,256,256]{3,2,1,0:T(8,128)(2,1)}, bf16[2,2,256,256]{3,2,1,0:T(8,128)(2,1)}) custom-call(s32[1]{0:T(128)} %bitcast.6.order_ref.band_ref), custom_call_target="tpu_custom_call" | custom-call | tf_op jit(solution)/shard_map/backward_tables/pallas_call | solution.py:127
  70.8 71.9 %all-to-all-done = f32[128,96,128]{2,1,0:T(8,128)} async-done(((f32[128,96,128]{2,1,0:T(8,128)}), f32[128,96,128]{2,1,0:T(8,128)}, u32[]{:S(2)}, u32[]{:S(2)}) %all-to-all-start) | async-done | bytes 6291488 | tf_op jit(solution)/shard_map/all_to_all | solution.py:758
  142.8 11.8 %middle.1 = f32[128,12,8,128]{3,2,1,0:T(8,128)} custom-call(s32[1]{0:T(128)} %bitcast.6.order_ref.band_ref, f32[128,12,8,128]{3,2,1,0:T(8,128)} %bitcast.9.in_ref, bf16[2,2,256,256]{3,2,1,0:T(8,128)(2,1)} %get-tuple-element.28.mz_hbm), custom_call_target="tpu_custom_call" | custom-call | tf_op jit(solution)/shard_map/middle/pallas_call | solution.py:630
  154.6 0.0 copy-start.5
  154.6 6.3 %all-to-all-start.1 = ((f32[128,96,128]{2,1,0:T(8,128)}), f32[128,96,128]{2,1,0:T(8,128)}, u32[]{:S(2)}, u32[]{:S(2)}) async-start(f32[128,96,128]{2,1,0:T(8,128)} %bitcast.24), calls=%async_computation.1 | async-start | bytes 12582912 | tf_op jit(solution)/shard_map/all_to_all | solution.py:758
  160.9 0.0 copy-start.7
  160.9 1.2 copy-done.7
  162.2 3.1 %conc_step.3 = f32[512,512]{1,0:T(8,128)} custom-call(f32[512,512]{1,0:T(8,128)S(1)} %conc_step.2.c_ref, f32[512,512]{1,0:T(8,128)S(1)} %order_step.1.new_ref.p_ref, f32[512,512]{1,0:T(8,128)S(1)} %copy-done.5, f32[512,512]{1,0:T(8,128)} %collective-permute-done.6.up_ref, f32[512,512]{1,0:T(8,128)S(1)} %copy-done.7), custom_call_target="tpu_custom_call" | custom-call | tf_op jit(solution)/shard_map/conc_step/pallas_call | solution.py:365
  165.3 70.6 %all-to-all-done.1 = f32[128,96,128]{2,1,0:T(8,128)} async-done(((f32[128,96,128]{2,1,0:T(8,128)}), f32[128,96,128]{2,1,0:T(8,128)}, u32[]{:S(2)}, u32[]{:S(2)}) %all-to-all-start.1) | async-done | bytes 6291488 | tf_op jit(solution)/shard_map/all_to_all | solution.py:758
  235.9 10.6 %inverse.1 = f32[6,512,512]{2,1,0:T(8,128)} custom-call(f32[128,12,8,128]{3,2,1,0:T(8,128)} %bitcast.11.in_ref, f32[6,512,512]{2,1,0:T(8,128)} %bitcast.26, bf16[4,2,256,256]{3,2,1,0:T(8,128)(2,1)} %get-tuple-element.29.mqi_hbm, bf16[2,2,256,256]{3,2,1,0:T(8,128)(2,1)} %get-tuple-element.30.txi_hbm), custom_call_target="tpu_custom_call" | custom-call | tf_op jit(solution)/shard_map/inverse/pallas_call | solution.py:735
  (13 shorter events, 0.0 us)
Async XLA Ops:
  0.6 22.4 %copy-start.3 = (f32[1,512,512]{2,1,0:T(8,128)S(1)}, f32[1,512,512]{2,1,0:T(8,128)}, u32[]{:S(2)}) copy-start(f32[1,512,512]{2,1,0:T(8,128)} %param.8) | copy-start | bytes 3145732
  0.6 22.4 %copy-start.4 = (f32[1,512,512]{2,1,0:T(8,128)S(1)}, f32[1,512,512]{2,1,0:T(8,128)}, u32[]{:S(2)}) copy-start(f32[1,512,512]{2,1,0:T(8,128)} %param.9) | copy-start | bytes 3145732
  0.7 22.4 %collective-permute-start = (f32[512,512]{1,0:T(8,128)}, f32[512,512]{1,0:T(8,128)S(1)}, u32[]{:S(2)}, u32[]{:S(2)}) collective-permute-start(f32[512,512]{1,0:T(8,128)} %bitcast.15), channel_id=1, source_target_pairs={{0,1},{1,2},{2,3},{3,4},{4,5},{5,6},{6,7},{7,8},{8,9},{9,10},{10,1... | collective-permute-start | bytes 3145736 | tf_op jit(solution)/shard_map/ppermute | solution.py:765
  0.7 22.3 %collective-permute-start.1 = (f32[512,512]{1,0:T(8,128)}, f32[512,512]{1,0:T(8,128)S(1)}, u32[]{:S(2)}, u32[]{:S(2)}) collective-permute-start(f32[512,512]{1,0:T(8,128)} %bitcast.16), channel_id=1, source_target_pairs={{1,0},{2,1},{3,2},{4,3},{5,4},{6,5},{7,6},{8,7},{9,8},{10,9},{11,1... | collective-permute-start | bytes 3145736 | tf_op jit(solution)/shard_map/ppermute | solution.py:765
  9.0 23.8 %collective-permute-start.2 = (f32[512,512]{1,0:T(8,128)}, f32[512,512]{1,0:T(8,128)S(1)}, u32[]{:S(2)}, u32[]{:S(2)}) collective-permute-start(f32[512,512]{1,0:T(8,128)} %bitcast.19), channel_id=1, source_target_pairs={{0,1},{1,2},{2,3},{3,4},{4,5},{5,6},{6,7},{7,8},{8,9},{9,10},{10,1... | collective-permute-start | bytes 3145736 | tf_op jit(solution)/shard_map/ppermute | solution.py:765
  9.0 26.4 %collective-permute-start.3 = (f32[512,512]{1,0:T(8,128)}, f32[512,512]{1,0:T(8,128)S(1)}, u32[]{:S(2)}, u32[]{:S(2)}) collective-permute-start(f32[512,512]{1,0:T(8,128)} %bitcast.20), channel_id=1, source_target_pairs={{1,0},{2,1},{3,2},{4,3},{5,4},{6,5},{7,6},{8,7},{9,8},{10,9},{11,1... | collective-permute-start | bytes 3145736 | tf_op jit(solution)/shard_map/ppermute | solution.py:765
  23.0 12.4 %copy-start.2 = (f32[512,512]{1,0:T(8,128)}, f32[512,512]{1,0:T(8,128)S(1)}, u32[]{:S(2)}) copy-start(f32[512,512]{1,0:T(8,128)S(1)} %get-tuple-element.18.dec_ref.dec_hbm) | copy-start | bytes 3145732
  23.0 13.3 %copy-start = (f32[6,512,512]{2,1,0:T(8,128)}, f32[6,512,512]{2,1,0:T(8,128)S(1)}, u32[]{:S(2)}) copy-start(f32[6,512,512]{2,1,0:T(8,128)S(1)} %get-tuple-element.20.unit_hbm) | copy-start | bytes 18874372
  23.0 13.3 %copy-start.1 = (f32[512,512]{1,0:T(8,128)}, f32[512,512]{1,0:T(8,128)S(1)}, u32[]{:S(2)}) copy-start(f32[512,512]{1,0:T(8,128)S(1)} %get-tuple-element.17.kin_ref.kin_hbm) | copy-start | bytes 3145732
  24.2 20.0 %collective-permute-start.4 = (f32[512,512]{1,0:T(8,128)S(1)}, f32[512,512]{1,0:T(8,128)}, u32[]{:S(2)}, u32[]{:S(2)}) collective-permute-start(f32[512,512]{1,0:T(8,128)S(1)} %order_step.1.new_ref.p_ref), channel_id=1, source_target_pairs={{0,1},{1,2},{2,3},{3,4},{4,5},{5,6},{6,7},{7,8},{8,9},{9,10},{10,1... | collective-permute-start | bytes 3145736 | tf_op jit(solution)/shard_map/ppermute | solution.py:765
  24.3 19.9 %collective-permute-start.5 = (f32[512,512]{1,0:T(8,128)S(1)}, f32[512,512]{1,0:T(8,128)}, u32[]{:S(2)}, u32[]{:S(2)}) collective-permute-start(f32[512,512]{1,0:T(8,128)S(1)} %order_step.1.new_ref.p_ref), channel_id=1, source_target_pairs={{1,0},{2,1},{3,2},{4,3},{5,4},{6,5},{7,6},{8,7},{9,8},{10,9},{11,1... | collective-permute-start | bytes 3145736 | tf_op jit(solution)/shard_map/ppermute | solution.py:765
  36.3 20.8 %collective-permute-start.6 = (f32[512,512]{1,0:T(8,128)S(1)}, f32[512,512]{1,0:T(8,128)}, u32[]{:S(2)}, u32[]{:S(2)}) collective-permute-start(f32[512,512]{1,0:T(8,128)S(1)} %conc_step.2.c_ref), channel_id=1, source_target_pairs={{0,1},{1,2},{2,3},{3,4},{4,5},{5,6},{6,7},{7,8},{8,9},{9,10},{10,1... | collective-permute-start | bytes 3145736 | tf_op jit(solution)/shard_map/ppermute | solution.py:765
  36.4 20.7 %collective-permute-start.7 = (f32[512,512]{1,0:T(8,128)S(1)}, f32[512,512]{1,0:T(8,128)S(1)}, u32[]{:S(2)}, u32[]{:S(2)}) collective-permute-start(f32[512,512]{1,0:T(8,128)S(1)} %conc_step.2.c_ref), channel_id=1, source_target_pairs={{1,0},{2,1},{3,2},{4,3},{5,4},{6,5},{7,6},{8,7},{9,8},{10,9},{11,1... | collective-permute-start | bytes 3145736 | tf_op jit(solution)/shard_map/ppermute | solution.py:765
  57.1 1.0 copy-start.6
  58.1 84.6 %all-to-all-start = ((f32[128,96,128]{2,1,0:T(8,128)}), f32[128,96,128]{2,1,0:T(8,128)}, u32[]{:S(2)}, u32[]{:S(2)}) async-start(f32[128,96,128]{2,1,0:T(8,128)} %bitcast.27), calls=%async_computation | async-start | bytes 12582912 | tf_op jit(solution)/shard_map/all_to_all | solution.py:758
  154.6 6.3 %copy-start.5 = (f32[512,512]{1,0:T(8,128)S(1)}, f32[512,512]{1,0:T(8,128)}, u32[]{:S(2)}) copy-start(f32[512,512]{1,0:T(8,128)} %get-tuple-element.22.new_ref) | copy-start | bytes 3145732
  154.6 81.3 %all-to-all-start.1 = ((f32[128,96,128]{2,1,0:T(8,128)}), f32[128,96,128]{2,1,0:T(8,128)}, u32[]{:S(2)}, u32[]{:S(2)}) async-start(f32[128,96,128]{2,1,0:T(8,128)} %bitcast.24), calls=%async_computation.1 | async-start | bytes 12582912 | tf_op jit(solution)/shard_map/all_to_all | solution.py:758
  160.9 1.2 copy-start.7

commit v4 on v3

--- a/solution.py
+++ b/solution.py
@@ -15,9 +15,9 @@
 DEPTH = 128
 COMPS = 6
 RADIX = 4
-PAIRS = COMPS // 2
+FIELDS = 5
 SUB = 8
-BLOCKS = PAIRS * RADIX
+BLOCKS = 2 * FIELDS
 ROWS = BLOCKS * SUB
 PITCH = (BLOCKS + 1) * SUB
 
@@ -372,16 +372,56 @@
     )(*planes, *map(in_hbm, after))
 
 
-def butterflies(spectra, comp, lanes_r, lanes_i, odd):
-    reals = [spectra[comp, pl.ds(LANE * j, LANE), lanes_r] for j in range(RADIX)]
-    imags = [spectra[comp, pl.ds(LANE * j, LANE), lanes_i] for j in range(RADIX)]
+def waves_x(rows):
+    lanes = lax.broadcasted_iota(jnp.int32, (rows, HALF), 1)
+    return (2 * (lanes & (LANE - 1)) + (lanes >> 7)).astype(f32)
+
+
+def waves_y(rows, rest):
+    index = RADIX * (lax.broadcasted_iota(jnp.int32, (rows, HALF), 0) & (LANE - 1)) + rest
+    return jnp.where(index < N // 2, index, index - N).astype(f32)
+
+
+def give(flat, block, half, value):
+    row = block * SUB + half * 4
+    for parity in range(2):
+        lanes = slice(LANE * parity, LANE * (parity + 1))
+        flat[pl.ds(row + 2 * parity, LANE, stride=PITCH), :] = value[:LANE, lanes]
+        flat[pl.ds(row + 2 * parity + 1, LANE, stride=PITCH), :] = value[LANE:, lanes]
+
+
+def take(flat, block, half):
+    row = block * SUB + half * 4
+    parts = [
+        jnp.concatenate(
+            [flat[pl.ds(row + 2 * parity + k, LANE, stride=PITCH), :] for parity in range(2)],
+            axis=1,
+        )
+        for k in range(2)
+    ]
+    return jnp.concatenate(parts, axis=0)
+
+
+def both_parities(spectra, comp, j, shift):
+    rows = pl.ds(LANE * j, LANE)
+    return jnp.concatenate(
+        [spectra[comp, rows, pl.ds(HALF * parity + shift, LANE)] for parity in range(2)], axis=1
+    )
+
+
+def butterflies(spectra, comp, odd):
+    reals = [both_parities(spectra, comp, j, 0) for j in range(RADIX)]
+    imags = [both_parities(spectra, comp, j, LANE) for j in range(RADIX)]
     if odd:
         er, ei = reals[0] - reals[2], imags[0] - imags[2]
         turned_r, turned_i = imags[1] - imags[3], reals[3] - reals[1]
     else:
         er, ei = reals[0] + reals[2], imags[0] + imags[2]
         turned_r, turned_i = reals[1] + reals[3], imags[1] + imags[3]
-    return (er + turned_r, ei + turned_i), (er - turned_r, ei - turned_i)
+    return (
+        jnp.concatenate([er + turned_r, ei + turned_i], axis=0),
+        jnp.concatenate([er - turned_r, ei - turned_i], axis=0),
+    )
 
 
 def forward_body(
@@ -462,45 +502,36 @@
 
     flat = packed.reshape(LANE * PITCH, LANE)
     copies = []
+
+    def send(block):
+        copy = pltpu.make_async_copy(packed.at[:, block], out_ref.at[:, block], sems.at[block])
+        copy.start()
+        copies.append(copy)
+
+    xi_x = waves_x(HALF)
     for odd in range(2):
-        for pair in range(PAIRS):
-            for parity in range(2):
-                lanes_r = pl.ds(HALF * parity, LANE)
-                lanes_i = pl.ds(HALF * parity + LANE, LANE)
-                both = [butterflies(spectra, 2 * pair + k, lanes_r, lanes_i, odd) for k in (0, 1)]
-                for half in range(2):
-                    rest = odd + 2 * half
-                    real = jnp.concatenate([both[0][half][0], both[1][half][0]], axis=1)
-                    imag = jnp.concatenate([both[0][half][1], both[1][half][1]], axis=1)
-                    value = jnp.concatenate([real, imag], axis=0)
-                    result = table_times((mq_ref[rest, 0], mq_ref[rest, 1]), value)
-                    give_pair(flat, (pair * RADIX + rest) * SUB + parity * 4, result)
-            for rest in (odd, odd + 2):
-                block = pair * RADIX + rest
-                copy = pltpu.make_async_copy(packed.at[:, block], out_ref.at[:, block], sems.at[block])
-                copy.start()
-                copies.append(copy)
+
+        def spectrum(comp):
+            return [
+                table_times((mq_ref[odd + 2 * half, 0], mq_ref[odd + 2 * half, 1]), value)
+                for half, value in enumerate(butterflies(spectra, comp, odd))
+            ]
+
+        for field, comp in ((2, 4), (3, 3), (4, 2)):
+            for half, value in enumerate(spectrum(comp)):
+                give(flat, odd * FIELDS + field, half, value)
+            send(odd * FIELDS + field)
+        t_xx, t_xy, t_yy = spectrum(0), spectrum(5), spectrum(1)
+        for half in range(2):
+            xi_y = waves_y(HALF, odd + 2 * half)
+            give(flat, odd * FIELDS, half, xi_x * t_xx[half] + xi_y * t_xy[half])
+            give(flat, odd * FIELDS + 1, half, xi_x * t_xy[half] + xi_y * t_yy[half])
+        send(odd * FIELDS)
+        send(odd * FIELDS + 1)
     for copy in copies:
         copy.wait()
     for index in range(N // TILE):
         keep(index).wait()
-
-
-def give_pair(flat, row, result):
-    for k in (0, 1):
-        lanes = slice(LANE * k, LANE * (k + 1))
-        flat[pl.ds(row + 2 * k, LANE, stride=PITCH), :] = result[:LANE, lanes]
-        flat[pl.ds(row + 2 * k + 1, LANE, stride=PITCH), :] = result[LANE:, lanes]
-
-
-def take_pair(flat, row):
-    reals, imags = [], []
-    for k in (0, 1):
-        reals.append(flat[pl.ds(row + 2 * k, LANE, stride=PITCH), :])
-        imags.append(flat[pl.ds(row + 2 * k + 1, LANE, stride=PITCH), :])
-    return jnp.concatenate(
-        [jnp.concatenate(reals, axis=1), jnp.concatenate(imags, axis=1)], axis=0
-    )
 
 
 SHAPE = (LANE, BLOCKS, SUB, LANE)
@@ -540,90 +571,82 @@
     source = received.reshape(LANE * PITCH, LANE)
     flat = packed.reshape(LANE * PITCH, LANE)
 
-    def fetch(pair, rest):
-        block = pair * RADIX + rest
+    def fetch(block):
         return pltpu.make_async_copy(in_ref.at[:, block], received.at[:, block], in_sems.at[block])
 
-    def send(pair, rest):
-        block = pair * RADIX + rest
+    def send(block):
         return pltpu.make_async_copy(packed.at[:, block], out_ref.at[:, block], out_sems.at[block])
 
     mz_copy = pltpu.make_async_copy(mz_hbm, mz_ref, table_sem)
-    for pair in range(PAIRS):
-        fetch(pair, 0).start()
+    for field in range(FIELDS):
+        fetch(field).start()
     mz_copy.start()
-    for pair in range(PAIRS):
-        fetch(pair, 0).wait()
-    for rest in range(1, RADIX):
-        for pair in range(PAIRS):
-            fetch(pair, rest).start()
+    for field in range(FIELDS):
+        fetch(field).wait()
+    for field in range(FIELDS):
+        fetch(FIELDS + field).start()
     mz_copy.wait()
 
-    def step(rest, carry):
-        @pl.when(rest > 0)
+    def step(odd, carry):
+        @pl.when(odd > 0)
         def _():
-            for pair in range(PAIRS):
-                fetch(pair, rest).wait()
-
-        middle_step(band_ref, source, mz_ref, flat, rest)
-        for pair in range(PAIRS):
-            send(pair, rest).start()
+            for field in range(FIELDS):
+                fetch(FIELDS + field).wait()
+
+        middle_step(band_ref[0], source, mz_ref, flat, odd)
+        for field in range(FIELDS):
+            send(odd * FIELDS + field).start()
         return carry
 
-    lax.fori_loop(0, RADIX, step, 0)
-    for rest in range(RADIX):
-        for pair in range(PAIRS):
-            send(pair, rest).wait()
-
-
-def middle_step(band_ref, source, mz_ref, flat, rest):
+    lax.fori_loop(0, 2, step, 0)
+    for block in range(BLOCKS):
+        send(block).wait()
+
+
+def middle_step(band, source, mz_ref, flat, odd):
     onward = (mz_ref[0, 0], mz_ref[0, 1])
     backward = (mz_ref[1, 0], mz_ref[1, 1])
-    shape = (DEPTH, LANE)
-    depth_index = lax.broadcasted_iota(jnp.int32, shape, 0)
+    fields = [
+        [
+            table_times(onward, take(source, odd * FIELDS + field, half))
+            for field in range(FIELDS)
+        ]
+        for half in range(2)
+    ]
+    xi_x = waves_x(DEPTH)
+    depth_index = lax.broadcasted_iota(jnp.int32, (DEPTH, HALF), 0)
     xi_z = jnp.where(depth_index < DEPTH // 2, depth_index, depth_index - DEPTH).astype(f32)
-    wave_y = band_ref[0] * RADIX + rest
-    xi_y = jnp.where(wave_y < N // 2, wave_y, wave_y - N).astype(f32)
-    for parity in range(2):
-        tau_r, tau_i = [], []
-        for pair in range(PAIRS):
-            result = table_times(onward, take_pair(source, (pair * RADIX + rest) * SUB + parity * 4))
-            for k in (0, 1):
-                lanes = slice(LANE * k, LANE * (k + 1))
-                tau_r.append(result[:LANE, lanes])
-                tau_i.append(result[LANE:, lanes])
-        xi_x = (2 * lax.broadcasted_iota(jnp.int32, shape, 1) + parity).astype(f32)
+    for half in range(2):
+        wave_y = band * RADIX + odd + 2 * half
+        xi_y = jnp.where(wave_y < N // 2, wave_y, wave_y - N).astype(f32)
         wave_sq = xi_x * xi_x + xi_y * xi_y + xi_z * xi_z
         live = (wave_sq > 0.5) & (xi_x < float(HALF))
         safe = jnp.where(live, wave_sq, 1.0)
         inverse = 1.0 / safe
         first = jnp.where(live, (0.5 / shear_ref) * inverse, 0.0)
         second = jnp.where(live, (0.5 * coupling) * (inverse * inverse), 0.0)
-        grids = []
-        for tau in (tau_r, tau_i):
-            t_xx, t_yy, t_zz, t_yz, t_xz, t_xy = tau
-            v_x = t_xx * xi_x + t_xy * xi_y + t_xz * xi_z
-            v_y = t_xy * xi_x + t_yy * xi_y + t_yz * xi_z
+        parts = []
+        for rows in (slice(0, DEPTH), slice(DEPTH, 2 * DEPTH)):
+            a_x, a_y, t_xz, t_yz, t_zz = (field[rows] for field in fields[half])
+            v_x = a_x + t_xz * xi_z
+            v_y = a_y + t_yz * xi_z
             v_z = t_xz * xi_x + t_yz * xi_y + t_zz * xi_z
             inner = (xi_x * v_x + xi_y * v_y + xi_z * v_z) * second
             h_x = v_x * first - xi_x * inner
             h_y = v_y * first - xi_y * inner
             h_z = v_z * first - xi_z * inner
-            grids.append(
+            parts.append(
                 (
-                    2.0 * xi_x * h_x,
-                    2.0 * xi_y * h_y,
+                    h_x,
+                    h_y,
+                    xi_z * h_x + xi_x * h_z,
+                    xi_z * h_y + xi_y * h_z,
                     2.0 * xi_z * h_z,
-                    xi_z * h_y + xi_y * h_z,
-                    xi_z * h_x + xi_x * h_z,
-                    xi_y * h_x + xi_x * h_y,
                 )
             )
-        for pair in range(PAIRS):
-            real = jnp.concatenate([grids[0][pair * 2], grids[0][pair * 2 + 1]], axis=1)
-            imag = jnp.concatenate([grids[1][pair * 2], grids[1][pair * 2 + 1]], axis=1)
-            result = table_times(backward, jnp.concatenate([real, imag], axis=0))
-            give_pair(flat, (pair * RADIX + rest) * SUB + parity * 4, result)
+        for field in range(FIELDS):
+            value = jnp.concatenate([parts[0][field], parts[1][field]], axis=0)
+            give(flat, odd * FIELDS + field, half, table_times(backward, value))
 
 
 def middle(band, received, mz):
@@ -645,10 +668,22 @@
     )(band, in_hbm(received), in_hbm(mz))
 
 
-def inverse_y(source, mqi_ref, pair, parity):
+def inverse_y(source, mqi_ref, comp):
     blocks = []
     for rest in range(RADIX):
-        value = take_pair(source, (pair * RADIX + rest) * SUB + parity * 4)
+        odd, half = rest % 2, rest // 2
+
+        def field(index):
+            return take(source, odd * FIELDS + index, half)
+
+        if comp == 0:
+            value = 2.0 * waves_x(HALF) * field(0)
+        elif comp == 1:
+            value = 2.0 * waves_y(HALF, rest) * field(1)
+        elif comp == 5:
+            value = waves_y(HALF, rest) * field(0) + waves_x(HALF) * field(1)
+        else:
+            value = field(6 - comp)
         result = table_times((mqi_ref[rest, 0], mqi_ref[rest, 1]), value)
         blocks.append((result[:LANE], result[LANE:]))
     er0, er1 = blocks[0][0] + blocks[2][0], blocks[0][0] - blocks[2][0]
@@ -669,64 +704,66 @@
 ):
     source = received.reshape(LANE * PITCH, LANE)
 
-    def fetch(pair, rest):
-        block = pair * RADIX + rest
-        return pltpu.make_async_copy(in_ref.at[:, block], received.at[:, block], in_sems.at[block])
+    def fetch(field):
+        return [
+            pltpu.make_async_copy(in_ref.at[:, block], received.at[:, block], in_sems.at[block])
+            for block in (field, FIELDS + field)
+        ]
 
     def fetch_strain(comp):
-        return pltpu.make_async_copy(strain_hbm.at[comp], strain_ref.at[comp], strain_sems.at[comp])
-
-    mqi_copy = pltpu.make_async_copy(mqi_hbm, mqi_ref, table_sems.at[0])
-    txi_copy = pltpu.make_async_copy(txi_hbm, txi_ref, table_sems.at[1])
+        return [
+            pltpu.make_async_copy(strain_hbm.at[comp], strain_ref.at[comp], strain_sems.at[comp])
+        ]
+
     def copy_of(comp):
         return pltpu.make_async_copy(moved.at[comp], out_ref.at[comp], sems.at[comp])
 
-    for rest in range(RADIX):
-        fetch(0, rest).start()
-    mqi_copy.start()
-    txi_copy.start()
-    for rest in range(RADIX):
-        fetch(0, rest).wait()
-    mqi_copy.wait()
-    txi_copy.wait()
-    for pair in range(PAIRS):
-        for k in (0, 1):
-            fetch_strain(2 * pair + k).start()
-        if pair + 1 < PAIRS:
-            for rest in range(RADIX):
-                fetch(pair + 1, rest).start()
-
-    def step(pair, carry):
-        @pl.when(pair > 0)
-        def _():
-            for rest in range(RADIX):
-                fetch(pair, rest).wait()
-
-        planes = [inverse_y(source, mqi_ref, pair, parity) for parity in range(2)]
-        for k in (0, 1):
-            fetch_strain(2 * pair + k).wait()
-        for k in (0, 1):
-            comp = pair * 2 + k
-            lanes = slice(LANE * k, LANE * (k + 1))
-            halves = []
-            for parity in range(2):
-                value = jnp.concatenate(
-                    [
-                        jnp.concatenate([real[:, lanes], imag[:, lanes]], axis=1)
-                        for real, imag in planes[parity]
-                    ],
-                    axis=0,
-                )
-                halves.append(times_table(value, (txi_ref[parity, 0], txi_ref[parity, 1])))
-            even, odd = halves
-            left = pl.ds(0, HALF)
-            right = pl.ds(HALF, HALF)
-            moved[comp, :, left] = strain_ref[comp, :, left] - (even + odd)
-            moved[comp, :, right] = strain_ref[comp, :, right] - (even - odd)
-            copy_of(comp).start()
-        return carry
-
-    lax.fori_loop(0, PAIRS, step, 0)
+    def start(copies):
+        for copy in copies:
+            copy.start()
+
+    def wait(copies):
+        for copy in copies:
+            copy.wait()
+
+    tables = [
+        pltpu.make_async_copy(mqi_hbm, mqi_ref, table_sems.at[0]),
+        pltpu.make_async_copy(txi_hbm, txi_ref, table_sems.at[1]),
+    ]
+    order = (4, 3, 2, 0, 1, 5)
+    needs = ((2,), (3,), (4,), (0,), (1,), ())
+    start(fetch(2))
+    start(tables)
+    wait(fetch(2))
+    wait(tables)
+    for comp, fields in zip(order, needs):
+        start(fetch_strain(comp))
+        for field in fields:
+            if field != 2:
+                start(fetch(field))
+
+    planes = inverse_y(source, mqi_ref, order[0])
+    for place, comp in enumerate(order):
+        wait(fetch_strain(comp))
+        if place + 1 < COMPS:
+            for field in needs[place + 1]:
+                wait(fetch(field))
+            following = inverse_y(source, mqi_ref, order[place + 1])
+        halves = []
+        for parity in range(2):
+            lanes = slice(LANE * parity, LANE * (parity + 1))
+            value = jnp.concatenate(
+                [jnp.concatenate([real[:, lanes], imag[:, lanes]], axis=1) for real, imag in planes],
+                axis=0,
+            )
+            halves.append(times_table(value, (txi_ref[parity, 0], txi_ref[parity, 1])))
+        even, odd = halves
+        left = pl.ds(0, HALF)
+        right = pl.ds(HALF, HALF)
+        moved[comp, :, left] = strain_ref[comp, :, left] - (even + odd)
+        moved[comp, :, right] = strain_ref[comp, :, right] - (even - odd)
+        copy_of(comp).start()
+        planes = following
     for comp in range(COMPS):
         copy_of(comp).wait()
 

time: 248 us -> 223 us (0.90)
  waiting for transfers between devices: 145 us -> 122 us
    all_to_all x2, waiting for transfers between devices: 143 us -> 120 us  [exchange(): lax.all_to_all(packed, 'gz', split_axis=0, concat_axis=0, tiled=True)]
    pallas_call x1, Pallas kernels: 11.8 us -> 9.21 us  [middle(): pl.pallas_call(middle_body, in_specs=[SCALAR, REMAIN, REMAIN], out_specs=...]
  transfers between devices with their start and end apart: 10 -> 10, of which waited for: 4 -> 4; matrix products, arithmetic and copies ran while one was open for 0% -> 0% of each run, Pallas kernels for 12% -> 13%
where the time goes in v4:
time: 223 us; the launch traced here: 222 us
  waiting for transfers between devices  122 us (55%)
  Pallas kernels  51 us (23%)
  starting transfers between devices  45.8 us (21%)
    all_to_all x2, waiting for transfers between devices, exchange(): lax.all_to_all(packed, 'gz', split_axis=0, concat_axis=0, tiled=True)  120 us
    ppermute x8, starting transfers between devices, neighbours(): return (lax.ppermute(plane, 'gz', ahead), lax.ppermute(plane, 'gz', behind))  30 us
    all_to_all x2, starting transfers between devices, exchange(): lax.all_to_all(packed, 'gz', split_axis=0, concat_axis=0, tiled=True)  15.8 us
    pallas_call x1, Pallas kernels, forward(): pl.pallas_call(forward_body, in_specs=[RESIDENT] * 2 + [REMAIN] * 7, out_...  12.6 us
    pallas_call x1, Pallas kernels, inverse(): pl.pallas_call(inverse_body, in_specs=[REMAIN] * 4, out_specs=REMAIN, out...  11.9 us
    pallas_call x1, Pallas kernels, middle(): pl.pallas_call(middle_body, in_specs=[SCALAR, REMAIN, REMAIN], out_specs=...  9.21 us
    pallas_call x1, Pallas kernels, coefficients(): pl.pallas_call(coef_body, grid=(TILES,), in_specs=[REMAIN, REMAIN, REMAIN...  6.82 us
    pallas_call x2, Pallas kernels, table_call(): pl.pallas_call(body, in_specs=[spec], out_shape=tuple((pltpu.HBM(tables_o...  5.35 us
  transfers between devices with their start and end apart: 10, of which 4 were waited for; matrix products, arithmetic and copies ran while one was open for 0% of the time, Pallas kernels for 13%

profile of v4, /device:TPU:0, one launch (start us, length us, event | category | flops | bytes accessed | tf_op | source)
XLA Modules:
  0.0 222.2 jit_solution(17710529779101841297)
XLA Ops:
  0.7 0.1 collective-permute-start
  0.7 8.3 %collective-permute-start.1 = (f32[512,512]{1,0:T(8,128)}, f32[512,512]{1,0:T(8,128)S(1)}, u32[]{:S(2)}, u32[]{:S(2)}) collective-permute-start(f32[512,512]{1,0:T(8,128)} %bitcast.16), channel_id=1, source_target_pairs={{1,0},{2,1},{3,2},{4,3},{5,4},{6,5},{7,6},{8,7},{9,8},{10,9},{11,1... | collective-permute-start | bytes 3145736 | tf_op jit(solution)/shard_map/ppermute | solution.py:802
  9.0 0.0 collective-permute-start.2
  9.0 7.2 %collective-permute-start.3 = (f32[512,512]{1,0:T(8,128)}, f32[512,512]{1,0:T(8,128)S(1)}, u32[]{:S(2)}, u32[]{:S(2)}) collective-permute-start(f32[512,512]{1,0:T(8,128)} %bitcast.20), channel_id=1, source_target_pairs={{1,0},{2,1},{3,2},{4,3},{5,4},{6,5},{7,6},{8,7},{9,8},{10,9},{11,1... | collective-permute-start | bytes 3145736 | tf_op jit(solution)/shard_map/ppermute | solution.py:802
  16.2 6.8 %coefficients.1 = (f32[6,512,512]{2,1,0:T(8,128)S(1)}, f32[512,512]{1,0:T(8,128)S(1)}, f32[512,512]{1,0:T(8,128)S(1)}) custom-call(f32[2,16]{1,0:T(2,128)} %moduli_hbm.1, f32[16]{0:T(128)} %mobility_hbm.1, f32[8]{0:T(128)} %rates_hbm.1, s32[512,512]{1,0:T(8,128)} %bitcast.29, s32[512,512]{1,0:T(8,128)} %bitcast.30, f32[6,512,512]{2,1,0:T(8,128)} %bitcast.24), custom_call_target="tpu_custom_call" | custom-call | tf_op jit(solution)/shard_map/coefficients/pallas_call | solution.py:265
  23.0 0.0 copy-start
  23.0 0.0 collective-permute-done.up_ref
  23.1 1.1 order_step.1.new_ref.p_ref
  24.2 0.1 collective-permute-start.4
  24.3 7.2 %collective-permute-start.5 = (f32[512,512]{1,0:T(8,128)S(1)}, f32[512,512]{1,0:T(8,128)}, u32[]{:S(2)}, u32[]{:S(2)}) collective-permute-start(f32[512,512]{1,0:T(8,128)S(1)} %order_step.1.new_ref.p_ref), channel_id=1, source_target_pairs={{1,0},{2,1},{3,2},{4,3},{5,4},{6,5},{7,6},{8,7},{9,8},{10,9},{11,1... | collective-permute-start | bytes 3145736 | tf_op jit(solution)/shard_map/ppermute | solution.py:802
  31.4 1.4 collective-permute-done.2.order_ref.up_ref
  32.9 2.5 %onward_tables.1 = (bf16[2,2,256,256]{3,2,1,0:T(8,128)(2,1)}, bf16[4,2,256,256]{3,2,1,0:T(8,128)(2,1)}) custom-call(f32[512,512]{1,0:T(8,128)S(1)} %collective-permute-done.2.order_ref.up_ref), custom_call_target="tpu_custom_call" | custom-call | tf_op jit(solution)/shard_map/onward_tables/pallas_call | solution.py:127
  35.4 0.0 collective-permute-done.3.down_ref
  35.4 0.9 conc_step.2.c_ref
  36.3 0.1 collective-permute-start.6
  36.4 7.2 %collective-permute-start.7 = (f32[512,512]{1,0:T(8,128)S(1)}, f32[512,512]{1,0:T(8,128)S(1)}, u32[]{:S(2)}, u32[]{:S(2)}) collective-permute-start(f32[512,512]{1,0:T(8,128)S(1)} %conc_step.2.c_ref), channel_id=1, source_target_pairs={{1,0},{2,1},{3,2},{4,3},{5,4},{6,5},{7,6},{8,7},{9,8},{10,9},{11,1... | collective-permute-start | bytes 3145736 | tf_op jit(solution)/shard_map/ppermute | solution.py:802
  43.6 0.6 collective-permute-done.4.up_hbm
  44.2 0.0 collective-permute-done.5.down_hbm
  44.2 12.6 %forward.1 = (f32[128,10,8,128]{3,2,1,0:T(8,128)}, f32[512,512]{1,0:T(8,128)}) custom-call(f32[512,512]{1,0:T(8,128)S(1)} %order_step.1.new_ref.p_ref, f32[512,512]{1,0:T(8,128)S(1)} %conc_step.2.c_ref, f32[512,512]{1,0:T(8,128)} %collective-permute-done.4.up_hbm, f32[512,512]{1,0:T(8,128)} %collective-permute-done.5.down_hbm, f32[512,512]{1,0:T(8,128)} %copy-done.1, ...), custom_call_target="tpu_custom_call" | custom-call | tf_op jit(solution)/shard_map/forward/pallas_call | solution.py:543
  56.9 0.0 copy-start.6
  56.9 1.0 copy-done.6
  57.8 9.9 %all-to-all-start = ((f32[128,80,128]{2,1,0:T(8,128)}), f32[128,80,128]{2,1,0:T(8,128)}, u32[]{:S(2)}, u32[]{:S(2)}) async-start(f32[128,80,128]{2,1,0:T(8,128)} %bitcast.28), calls=%async_computation | async-start | bytes 10485760 | tf_op jit(solution)/shard_map/all_to_all | solution.py:795
  67.7 2.8 %backward_tables.1 = (bf16[2,2,256,256]{3,2,1,0:T(8,128)(2,1)}, bf16[4,2,256,256]{3,2,1,0:T(8,128)(2,1)}, bf16[2,2,256,256]{3,2,1,0:T(8,128)(2,1)}) custom-call(s32[1]{0:T(128)} %bitcast.6.order_ref.band_ref), custom_call_target="tpu_custom_call" | custom-call | tf_op jit(solution)/shard_map/backward_tables/pallas_call | solution.py:127
  70.5 60.7 %all-to-all-done = f32[128,80,128]{2,1,0:T(8,128)} async-done(((f32[128,80,128]{2,1,0:T(8,128)}), f32[128,80,128]{2,1,0:T(8,128)}, u32[]{:S(2)}, u32[]{:S(2)}) %all-to-all-start) | async-done | bytes 5242912 | tf_op jit(solution)/shard_map/all_to_all | solution.py:795
  131.2 9.2 %middle.1 = f32[128,10,8,128]{3,2,1,0:T(8,128)} custom-call(s32[1]{0:T(128)} %bitcast.6.order_ref.band_ref, f32[128,10,8,128]{3,2,1,0:T(8,128)} %bitcast.9.in_ref, bf16[2,2,256,256]{3,2,1,0:T(8,128)(2,1)} %get-tuple-element.28.mz_hbm), custom_call_target="tpu_custom_call" | custom-call | tf_op jit(solution)/shard_map/middle/pallas_call | solution.py:653
  140.5 0.0 copy-start.5
  140.5 5.9 %all-to-all-start.1 = ((f32[128,80,128]{2,1,0:T(8,128)}), f32[128,80,128]{2,1,0:T(8,128)}, u32[]{:S(2)}, u32[]{:S(2)}) async-start(f32[128,80,128]{2,1,0:T(8,128)} %bitcast.26), calls=%async_computation.1 | async-start | bytes 10485760 | tf_op jit(solution)/shard_map/all_to_all | solution.py:795
  146.4 0.0 copy-start.7
  146.5 1.2 copy-done.7
  147.7 3.1 %conc_step.3 = f32[512,512]{1,0:T(8,128)} custom-call(f32[512,512]{1,0:T(8,128)S(1)} %conc_step.2.c_ref, f32[512,512]{1,0:T(8,128)S(1)} %order_step.1.new_ref.p_ref, f32[512,512]{1,0:T(8,128)S(1)} %copy-done.5, f32[512,512]{1,0:T(8,128)} %collective-permute-done.6.up_ref, f32[512,512]{1,0:T(8,128)S(1)} %copy-done.7), custom_call_target="tpu_custom_call" | custom-call | tf_op jit(solution)/shard_map/conc_step/pallas_call | solution.py:365
  150.8 59.4 %all-to-all-done.1 = f32[128,80,128]{2,1,0:T(8,128)} async-done(((f32[128,80,128]{2,1,0:T(8,128)}), f32[128,80,128]{2,1,0:T(8,128)}, u32[]{:S(2)}, u32[]{:S(2)}) %all-to-all-start.1) | async-done | bytes 5242912 | tf_op jit(solution)/shard_map/all_to_all | solution.py:795
  210.2 11.9 %inverse.1 = f32[6,512,512]{2,1,0:T(8,128)} custom-call(f32[128,10,8,128]{3,2,1,0:T(8,128)} %bitcast.11.in_ref, f32[6,512,512]{2,1,0:T(8,128)} %bitcast.25, bf16[4,2,256,256]{3,2,1,0:T(8,128)(2,1)} %get-tuple-element.29.mqi_hbm, bf16[2,2,256,256]{3,2,1,0:T(8,128)(2,1)} %get-tuple-element.30.txi_hbm), custom_call_target="tpu_custom_call" | custom-call | tf_op jit(solution)/shard_map/inverse/pallas_call | solution.py:772
  (13 shorter events, 0.0 us)
Async XLA Ops:
  0.6 22.4 %copy-start.3 = (f32[1,512,512]{2,1,0:T(8,128)S(1)}, f32[1,512,512]{2,1,0:T(8,128)}, u32[]{:S(2)}) copy-start(f32[1,512,512]{2,1,0:T(8,128)} %param.8) | copy-start | bytes 3145732
  0.6 22.4 %copy-start.4 = (f32[1,512,512]{2,1,0:T(8,128)S(1)}, f32[1,512,512]{2,1,0:T(8,128)}, u32[]{:S(2)}) copy-start(f32[1,512,512]{2,1,0:T(8,128)} %param.9) | copy-start | bytes 3145732
  0.7 22.4 %collective-permute-start = (f32[512,512]{1,0:T(8,128)}, f32[512,512]{1,0:T(8,128)S(1)}, u32[]{:S(2)}, u32[]{:S(2)}) collective-permute-start(f32[512,512]{1,0:T(8,128)} %bitcast.15), channel_id=1, source_target_pairs={{0,1},{1,2},{2,3},{3,4},{4,5},{5,6},{6,7},{7,8},{8,9},{9,10},{10,1... | collective-permute-start | bytes 3145736 | tf_op jit(solution)/shard_map/ppermute | solution.py:802
  0.7 22.3 %collective-permute-start.1 = (f32[512,512]{1,0:T(8,128)}, f32[512,512]{1,0:T(8,128)S(1)}, u32[]{:S(2)}, u32[]{:S(2)}) collective-permute-start(f32[512,512]{1,0:T(8,128)} %bitcast.16), channel_id=1, source_target_pairs={{1,0},{2,1},{3,2},{4,3},{5,4},{6,5},{7,6},{8,7},{9,8},{10,9},{11,1... | collective-permute-start | bytes 3145736 | tf_op jit(solution)/shard_map/ppermute | solution.py:802
  9.0 23.8 %collective-permute-start.2 = (f32[512,512]{1,0:T(8,128)}, f32[512,512]{1,0:T(8,128)S(1)}, u32[]{:S(2)}, u32[]{:S(2)}) collective-permute-start(f32[512,512]{1,0:T(8,128)} %bitcast.19), channel_id=1, source_target_pairs={{0,1},{1,2},{2,3},{3,4},{4,5},{5,6},{6,7},{7,8},{8,9},{9,10},{10,1... | collective-permute-start | bytes 3145736 | tf_op jit(solution)/shard_map/ppermute | solution.py:802
  9.0 26.4 %collective-permute-start.3 = (f32[512,512]{1,0:T(8,128)}, f32[512,512]{1,0:T(8,128)S(1)}, u32[]{:S(2)}, u32[]{:S(2)}) collective-permute-start(f32[512,512]{1,0:T(8,128)} %bitcast.20), channel_id=1, source_target_pairs={{1,0},{2,1},{3,2},{4,3},{5,4},{6,5},{7,6},{8,7},{9,8},{10,9},{11,1... | collective-permute-start | bytes 3145736 | tf_op jit(solution)/shard_map/ppermute | solution.py:802
  23.0 12.4 %copy-start.2 = (f32[512,512]{1,0:T(8,128)}, f32[512,512]{1,0:T(8,128)S(1)}, u32[]{:S(2)}) copy-start(f32[512,512]{1,0:T(8,128)S(1)} %get-tuple-element.18.dec_ref.dec_hbm) | copy-start | bytes 3145732
  23.0 13.3 %copy-start = (f32[6,512,512]{2,1,0:T(8,128)}, f32[6,512,512]{2,1,0:T(8,128)S(1)}, u32[]{:S(2)}) copy-start(f32[6,512,512]{2,1,0:T(8,128)S(1)} %get-tuple-element.20.unit_hbm) | copy-start | bytes 18874372
  23.0 13.3 %copy-start.1 = (f32[512,512]{1,0:T(8,128)}, f32[512,512]{1,0:T(8,128)S(1)}, u32[]{:S(2)}) copy-start(f32[512,512]{1,0:T(8,128)S(1)} %get-tuple-element.17.kin_ref.kin_hbm) | copy-start | bytes 3145732
  24.2 20.0 %collective-permute-start.4 = (f32[512,512]{1,0:T(8,128)S(1)}, f32[512,512]{1,0:T(8,128)}, u32[]{:S(2)}, u32[]{:S(2)}) collective-permute-start(f32[512,512]{1,0:T(8,128)S(1)} %order_step.1.new_ref.p_ref), channel_id=1, source_target_pairs={{0,1},{1,2},{2,3},{3,4},{4,5},{5,6},{6,7},{7,8},{8,9},{9,10},{10,1... | collective-permute-start | bytes 3145736 | tf_op jit(solution)/shard_map/ppermute | solution.py:802
  24.3 19.9 %collective-permute-start.5 = (f32[512,512]{1,0:T(8,128)S(1)}, f32[512,512]{1,0:T(8,128)}, u32[]{:S(2)}, u32[]{:S(2)}) collective-permute-start(f32[512,512]{1,0:T(8,128)S(1)} %order_step.1.new_ref.p_ref), channel_id=1, source_target_pairs={{1,0},{2,1},{3,2},{4,3},{5,4},{6,5},{7,6},{8,7},{9,8},{10,9},{11,1... | collective-permute-start | bytes 3145736 | tf_op jit(solution)/shard_map/ppermute | solution.py:802
  36.3 20.5 %collective-permute-start.6 = (f32[512,512]{1,0:T(8,128)S(1)}, f32[512,512]{1,0:T(8,128)}, u32[]{:S(2)}, u32[]{:S(2)}) collective-permute-start(f32[512,512]{1,0:T(8,128)S(1)} %conc_step.2.c_ref), channel_id=1, source_target_pairs={{0,1},{1,2},{2,3},{3,4},{4,5},{5,6},{6,7},{7,8},{8,9},{9,10},{10,1... | collective-permute-start | bytes 3145736 | tf_op jit(solution)/shard_map/ppermute | solution.py:802
  36.4 20.4 %collective-permute-start.7 = (f32[512,512]{1,0:T(8,128)S(1)}, f32[512,512]{1,0:T(8,128)S(1)}, u32[]{:S(2)}, u32[]{:S(2)}) collective-permute-start(f32[512,512]{1,0:T(8,128)S(1)} %conc_step.2.c_ref), channel_id=1, source_target_pairs={{1,0},{2,1},{3,2},{4,3},{5,4},{6,5},{7,6},{8,7},{9,8},{10,9},{11,1... | collective-permute-start | bytes 3145736 | tf_op jit(solution)/shard_map/ppermute | solution.py:802
  56.9 1.0 copy-start.6
  57.8 73.4 %all-to-all-start = ((f32[128,80,128]{2,1,0:T(8,128)}), f32[128,80,128]{2,1,0:T(8,128)}, u32[]{:S(2)}, u32[]{:S(2)}) async-start(f32[128,80,128]{2,1,0:T(8,128)} %bitcast.28), calls=%async_computation | async-start | bytes 10485760 | tf_op jit(solution)/shard_map/all_to_all | solution.py:795
  140.5 6.0 %copy-start.5 = (f32[512,512]{1,0:T(8,128)S(1)}, f32[512,512]{1,0:T(8,128)}, u32[]{:S(2)}) copy-start(f32[512,512]{1,0:T(8,128)} %get-tuple-element.22.new_ref) | copy-start | bytes 3145732
  140.5 69.7 %all-to-all-start.1 = ((f32[128,80,128]{2,1,0:T(8,128)}), f32[128,80,128]{2,1,0:T(8,128)}, u32[]{:S(2)}, u32[]{:S(2)}) async-start(f32[128,80,128]{2,1,0:T(8,128)} %bitcast.26), calls=%async_computation.1 | async-start | bytes 10485760 | tf_op jit(solution)/shard_map/all_to_all | solution.py:795
  146.4 1.2 copy-start.7

commit v5 on v4

--- a/solution.py
+++ b/solution.py
@@ -171,6 +171,8 @@
 
 
 def rows_of(index):
+    if isinstance(index, int):
+        return pl.ds(index * TILE, TILE)
     return pl.ds(pl.multiple_of(index * TILE, TILE), TILE)
 
 
@@ -282,8 +284,13 @@
 
 def planar_sum(ref, start):
     center = ref[pl.ds(start, STRIP), :]
-    before = ref[pl.ds(pl.multiple_of((start + N - 8) & (N - 1), 8), 8), :]
-    after = ref[pl.ds(pl.multiple_of((start + STRIP) & (N - 1), 8), 8), :]
+    before_start = (start + N - 8) & (N - 1)
+    after_start = (start + STRIP) & (N - 1)
+    if not isinstance(start, int):
+        before_start = pl.multiple_of(before_start, 8)
+        after_start = pl.multiple_of(after_start, 8)
+    before = ref[pl.ds(before_start, 8), :]
+    after = ref[pl.ds(after_start, 8), :]
     tall = jnp.concatenate([before, center, after], axis=0)
     height = STRIP + 16
     above = pltpu.roll(tall, 1, 0)[8 : 8 + STRIP]
@@ -370,6 +377,34 @@
         compiler_params=params(8),
         name="conc_step",
     )(*planes, *map(in_hbm, after))
+
+
+def last_conc_body(c_ref, p_ref, new_ref, up_hbm, down_hbm, c_out, up_ref, down_ref, sems):
+    halos = [
+        pltpu.make_async_copy(up_hbm, up_ref, sems.at[0]),
+        pltpu.make_async_copy(down_hbm, down_ref, sems.at[1]),
+    ]
+    for copy in halos:
+        copy.start()
+    for copy in halos:
+        copy.wait()
+    conc_body(c_ref, p_ref, new_ref, up_ref, down_ref, c_out)
+
+
+def last_conc(conc_now, order_now, order_new, halos):
+    return pl.pallas_call(
+        last_conc_body,
+        in_specs=[RESIDENT] * 3 + [REMAIN] * 2,
+        out_specs=RESIDENT,
+        out_shape=PLANE,
+        scratch_shapes=[
+            pltpu.VMEM((N, N), f32),
+            pltpu.VMEM((N, N), f32),
+            pltpu.SemaphoreType.DMA((2,)),
+        ],
+        compiler_params=params(8),
+        name="last_conc",
+    )(conc_now, order_now, order_new, *map(in_hbm, halos))
 
 
 def waves_x(rows):
@@ -426,9 +461,12 @@
 
 def forward_body(
     p_ref, c_ref, up_hbm, down_hbm, kin_hbm, dec_hbm, unit_hbm, txf_hbm, mq_hbm,
-    out_ref, p_hbm, up_ref, down_ref, kin_ref, dec_ref, unit_ref, txf_ref, mq_ref, p_out, spectra, packed, highs, lows,
+    out_ref, p_hbm, up_ref, down_ref, kin_ref, dec_ref, unit_ref, txf_ref, mq_ref, p_out, spectra, packed,
+    high_a, high_b, low_a, low_b,
     in_sems, table_sems, order_sems, sems,
 ):
+    highs, lows = (high_a, high_b), (low_a, low_b)
+
     def fetch(index):
         rows = rows_of(index)
         singles = (
@@ -453,11 +491,10 @@
     mq_copy = pltpu.make_async_copy(mq_hbm, mq_ref, table_sems.at[1])
     txf_copy.start()
 
-    def tile(index):
-        base = pl.multiple_of(index * TILE, TILE)
-
-        def strip(local):
-            start = pl.multiple_of(base + local, STRIP)
+    def stress_tile(index):
+        slot = index % 2
+        for local in range(0, TILE, STRIP):
+            start = index * TILE + local
             where = pl.ds(start, STRIP)
             order = next_order(
                 p_ref,
@@ -473,31 +510,41 @@
                 part = scale * unit_ref[comp, where, :]
                 left = part[:, :HALF]
                 right = part[:, HALF:]
-                here = pl.ds(pl.multiple_of(comp * TILE + local, STRIP), STRIP)
+                here = pl.ds(comp * TILE + local, STRIP)
                 for parity, folded in ((0, left + right), (1, left - right)):
-                    highs[parity, here, :], lows[parity, here, :] = split(folded)
-
-        strips(TILE, strip)
+                    highs[slot][parity, here, :], lows[slot][parity, here, :] = split(folded)
         keep(index).start()
 
-        @pl.when(index == 0)
-        def _():
-            mq_copy.start()
-            txf_copy.wait()
-
+    def transform_tile(index):
+        slot = index % 2
         for parity in range(2):
-            high = highs[parity]
+            high = highs[slot][parity]
             result = (
                 mul(high, txf_ref[parity, 0])
-                + mul(lows[parity], txf_ref[parity, 0])
+                + mul(lows[slot][parity], txf_ref[parity, 0])
                 + mul(high, txf_ref[parity, 1])
             )
             for comp in range(COMPS):
-                spectra[comp, pl.ds(base, TILE), pl.ds(HALF * parity, HALF)] = result[
+                spectra[comp, pl.ds(index * TILE, TILE), pl.ds(HALF * parity, HALF)] = result[
                     comp * TILE : (comp + 1) * TILE
                 ]
 
-    stream(fetch, tile)
+    for copy in fetch(0):
+        copy.start()
+    for copy in fetch(0):
+        copy.wait()
+    for index in range(1, TILES):
+        for copy in fetch(index):
+            copy.start()
+    mq_copy.start()
+    stress_tile(0)
+    txf_copy.wait()
+    for index in range(1, TILES):
+        for copy in fetch(index):
+            copy.wait()
+        transform_tile(index - 1)
+        stress_tile(index)
+    transform_tile(TILES - 1)
     mq_copy.wait()
 
     flat = packed.reshape(LANE * PITCH, LANE)
@@ -553,16 +600,15 @@
             pltpu.VMEM((N, N), f32),
             pltpu.VMEM((COMPS, N, N), f32),
             pltpu.VMEM(SPACED, f32),
-            pltpu.VMEM((2, COMPS * TILE, HALF), bf16),
-            pltpu.VMEM((2, COMPS * TILE, HALF), bf16),
+            *[pltpu.VMEM((2, COMPS * TILE, HALF), bf16)] * 4,
             pltpu.SemaphoreType.DMA((N // TILE, COMPS + 4)),
             pltpu.SemaphoreType.DMA((2,)),
             pltpu.SemaphoreType.DMA((N // TILE,)),
             pltpu.SemaphoreType.DMA((BLOCKS,)),
         ],
-        compiler_params=params(40),
+        compiler_params=params(44),
         name="forward",
-    )(order, conc, *map(in_hbm, (*halos, kinetic, decay, unit, txf, mq)))
+    )(order, conc, *halos, *map(in_hbm, (kinetic, decay, unit, txf, mq)))
 
 
 def middle_body(
@@ -593,9 +639,7 @@
             for field in range(FIELDS):
                 fetch(FIELDS + field).wait()
 
-        middle_step(band_ref[0], source, mz_ref, flat, odd)
-        for field in range(FIELDS):
-            send(odd * FIELDS + field).start()
+        middle_step(band_ref[0], source, mz_ref, flat, odd, lambda block: send(block).start())
         return carry
 
     lax.fori_loop(0, 2, step, 0)
@@ -603,7 +647,7 @@
         send(block).wait()
 
 
-def middle_step(band, source, mz_ref, flat, odd):
+def middle_step(band, source, mz_ref, flat, odd, done):
     onward = (mz_ref[0, 0], mz_ref[0, 1])
     backward = (mz_ref[1, 0], mz_ref[1, 1])
     fields = [
@@ -647,6 +691,8 @@
         for field in range(FIELDS):
             value = jnp.concatenate([parts[0][field], parts[1][field]], axis=0)
             give(flat, odd * FIELDS + field, half, table_times(backward, value))
+            if half == 1:
+                done(odd * FIELDS + field)
 
 
 def middle(band, received, mz):
@@ -736,14 +782,19 @@
     start(tables)
     wait(fetch(2))
     wait(tables)
-    for comp, fields in zip(order, needs):
-        start(fetch_strain(comp))
-        for field in fields:
-            if field != 2:
-                start(fetch(field))
+    def start_for(place):
+        if place < COMPS:
+            for field in needs[place]:
+                if field != 2:
+                    start(fetch(field))
+            start(fetch_strain(order[place]))
+
+    for place in range(2):
+        start_for(place)
 
     planes = inverse_y(source, mqi_ref, order[0])
     for place, comp in enumerate(order):
+        start_for(place + 2)
         wait(fetch_strain(comp))
         if place + 1 < COMPS:
             for field in needs[place + 1]:
@@ -840,7 +891,7 @@
     spectra, band, conc_halos = lax.optimization_barrier((spectra, band, conc_halos))
     received = exchange(spectra)
     mz, mqi, txi = backward_tables(band)
-    conc_next = conc_step(conc_now, order_now, order_next, conc_halos)
+    conc_next = last_conc(conc_now, order_now, order_next, conc_halos)
     returned = exchange(middle(band, received, mz))
     strain_next = inverse(returned, planes, mqi, txi)
     return (

time: 223 us -> 221 us (level)
    pallas_call x0 -> x1, Pallas kernels: none -> 3.47 us  [last_conc(): pl.pallas_call(last_conc_body, in_specs=[RESIDENT] * 3 + [REMAIN] * 2, ou...]
    pallas_call x2 -> x1, Pallas kernels: 4.05 us -> 0.92 us  [conc_step(): pl.pallas_call(conc_body, in_specs=[RESIDENT] * 5 + [REMAIN] * len(after)...]
  transfers between devices with their start and end apart: 10 -> 10, of which waited for: 4 -> 4; matrix products, arithmetic and copies ran while one was open for 0% -> 0% of each run, Pallas kernels for 13% -> 14%
where the time goes in v5:
time: 221 us
  waiting for transfers between devices  123 us (56%)
  Pallas kernels  49.7 us (22%)
  starting transfers between devices  45.8 us (21%)
    all_to_all x2, waiting for transfers between devices, exchange(): lax.all_to_all(packed, 'gz', split_axis=0, concat_axis=0, tiled=True)  121 us
    ppermute x8, starting transfers between devices, neighbours(): return (lax.ppermute(plane, 'gz', ahead), lax.ppermute(plane, 'gz', behind))  30 us
    all_to_all x2, starting transfers between devices, exchange(): lax.all_to_all(packed, 'gz', split_axis=0, concat_axis=0, tiled=True)  15.8 us
    pallas_call x1, Pallas kernels, forward(): pl.pallas_call(forward_body, in_specs=[RESIDENT] * 2 + [REMAIN] * 7, out_...  12.2 us
    pallas_call x1, Pallas kernels, inverse(): pl.pallas_call(inverse_body, in_specs=[REMAIN] * 4, out_specs=REMAIN, out...  10.9 us
    pallas_call x1, Pallas kernels, middle(): pl.pallas_call(middle_body, in_specs=[SCALAR, REMAIN, REMAIN], out_specs=...  8.95 us
    pallas_call x1, Pallas kernels, coefficients(): pl.pallas_call(coef_body, grid=(TILES,), in_specs=[REMAIN, REMAIN, REMAIN...  6.82 us
    pallas_call x2, Pallas kernels, table_call(): pl.pallas_call(body, in_specs=[spec], out_shape=tuple((pltpu.HBM(tables_o...  5.36 us
  transfers between devices with their start and end apart: 10, of which 4 were waited for; matrix products, arithmetic and copies ran while one was open for 0% of the time, Pallas kernels for 14%

profile of v5, /device:TPU:0, one launch (start us, length us, event | category | flops | bytes accessed | tf_op | source)
XLA Modules:
  0.0 220.6 jit_solution(4038850532956970890)
XLA Ops:
  0.7 0.1 collective-permute-start
  0.7 8.3 %collective-permute-start.1 = (f32[512,512]{1,0:T(8,128)}, f32[512,512]{1,0:T(8,128)S(1)}, u32[]{:S(2)}, u32[]{:S(2)}) collective-permute-start(f32[512,512]{1,0:T(8,128)} %bitcast.16), channel_id=1, source_target_pairs={{1,0},{2,1},{3,2},{4,3},{5,4},{6,5},{7,6},{8,7},{9,8},{10,9},{11,1... | collective-permute-start | bytes 3145736 | tf_op jit(solution)/shard_map/ppermute | solution.py:853
  9.0 0.0 collective-permute-start.2
  9.0 7.2 %collective-permute-start.3 = (f32[512,512]{1,0:T(8,128)}, f32[512,512]{1,0:T(8,128)S(1)}, u32[]{:S(2)}, u32[]{:S(2)}) collective-permute-start(f32[512,512]{1,0:T(8,128)} %bitcast.20), channel_id=1, source_target_pairs={{1,0},{2,1},{3,2},{4,3},{5,4},{6,5},{7,6},{8,7},{9,8},{10,9},{11,1... | collective-permute-start | bytes 3145736 | tf_op jit(solution)/shard_map/ppermute | solution.py:853
  16.2 6.8 %coefficients.1 = (f32[6,512,512]{2,1,0:T(8,128)S(1)}, f32[512,512]{1,0:T(8,128)S(1)}, f32[512,512]{1,0:T(8,128)S(1)}) custom-call(f32[2,16]{1,0:T(2,128)} %moduli_hbm.1, f32[16]{0:T(128)} %mobility_hbm.1, f32[8]{0:T(128)} %rates_hbm.1, s32[512,512]{1,0:T(8,128)} %bitcast.29, s32[512,512]{1,0:T(8,128)} %bitcast.30, f32[6,512,512]{2,1,0:T(8,128)} %bitcast.24), custom_call_target="tpu_custom_call" | custom-call | tf_op jit(solution)/shard_map/coefficients/pallas_call | solution.py:267
  23.0 0.0 copy-start
  23.0 0.0 collective-permute-done.up_ref
  23.1 0.0 collective-permute-done.1.down_ref
  23.1 1.1 order_step.1.new_ref.p_ref
  24.2 0.1 collective-permute-start.4
  24.3 7.2 %collective-permute-start.5 = (f32[512,512]{1,0:T(8,128)S(1)}, f32[512,512]{1,0:T(8,128)}, u32[]{:S(2)}, u32[]{:S(2)}) collective-permute-start(f32[512,512]{1,0:T(8,128)S(1)} %order_step.1.new_ref.p_ref), channel_id=1, source_target_pairs={{1,0},{2,1},{3,2},{4,3},{5,4},{6,5},{7,6},{8,7},{9,8},{10,9},{11,1... | collective-permute-start | bytes 3145736 | tf_op jit(solution)/shard_map/ppermute | solution.py:853
  31.4 1.4 collective-permute-done.2.order_ref.up_ref
  32.9 2.5 %onward_tables.1 = (bf16[2,2,256,256]{3,2,1,0:T(8,128)(2,1)}, bf16[4,2,256,256]{3,2,1,0:T(8,128)(2,1)}) custom-call(f32[512,512]{1,0:T(8,128)S(1)} %collective-permute-done.2.order_ref.up_ref), custom_call_target="tpu_custom_call" | custom-call | tf_op jit(solution)/shard_map/onward_tables/pallas_call | solution.py:127
  35.4 0.0 collective-permute-done.3.down_ref
  35.4 0.9 conc_step.1.c_ref
  36.3 0.1 collective-permute-start.6
  36.4 7.2 %collective-permute-start.7 = (f32[512,512]{1,0:T(8,128)S(1)}, f32[512,512]{1,0:T(8,128)}, u32[]{:S(2)}, u32[]{:S(2)}) collective-permute-start(f32[512,512]{1,0:T(8,128)S(1)} %conc_step.1.c_ref), channel_id=1, source_target_pairs={{1,0},{2,1},{3,2},{4,3},{5,4},{6,5},{7,6},{8,7},{9,8},{10,9},{11,1... | collective-permute-start | bytes 3145736 | tf_op jit(solution)/shard_map/ppermute | solution.py:853
  43.6 0.6 collective-permute-done.4.up_hbm
  44.2 0.0 collective-permute-done.5.down_hbm
  44.2 12.2 %forward.1 = (f32[128,10,8,128]{3,2,1,0:T(8,128)}, f32[512,512]{1,0:T(8,128)}) custom-call(f32[512,512]{1,0:T(8,128)S(1)} %order_step.1.new_ref.p_ref, f32[512,512]{1,0:T(8,128)S(1)} %conc_step.1.c_ref, f32[512,512]{1,0:T(8,128)} %collective-permute-done.4.up_hbm, f32[512,512]{1,0:T(8,128)} %collective-permute-done.5.down_hbm, f32[512,512]{1,0:T(8,128)} %copy-done.1, ...), custom_call_target="tpu_custom_call" | custom-call | tf_op jit(solution)/shard_map/forward/pallas_call | solution.py:590
  56.4 0.0 collective-permute-done.6.up_hbm
  56.5 0.0 collective-permute-done.7.down_hbm
  56.5 1.0 copy-done.6
  57.4 9.9 %all-to-all-start = ((f32[128,80,128]{2,1,0:T(8,128)}), f32[128,80,128]{2,1,0:T(8,128)}, u32[]{:S(2)}, u32[]{:S(2)}) async-start(f32[128,80,128]{2,1,0:T(8,128)} %bitcast.28), calls=%async_computation | async-start | bytes 10485760 | tf_op jit(solution)/shard_map/all_to_all | solution.py:846
  67.3 2.8 %backward_tables.1 = (bf16[2,2,256,256]{3,2,1,0:T(8,128)(2,1)}, bf16[4,2,256,256]{3,2,1,0:T(8,128)(2,1)}, bf16[2,2,256,256]{3,2,1,0:T(8,128)(2,1)}) custom-call(s32[1]{0:T(128)} %bitcast.6.order_ref.band_ref), custom_call_target="tpu_custom_call" | custom-call | tf_op jit(solution)/shard_map/backward_tables/pallas_call | solution.py:127
  70.2 60.7 %all-to-all-done = f32[128,80,128]{2,1,0:T(8,128)} async-done(((f32[128,80,128]{2,1,0:T(8,128)}), f32[128,80,128]{2,1,0:T(8,128)}, u32[]{:S(2)}, u32[]{:S(2)}) %all-to-all-start) | async-done | bytes 5242912 | tf_op jit(solution)/shard_map/all_to_all | solution.py:846
  130.9 9.0 %middle.1 = f32[128,10,8,128]{3,2,1,0:T(8,128)} custom-call(s32[1]{0:T(128)} %bitcast.6.order_ref.band_ref, f32[128,10,8,128]{3,2,1,0:T(8,128)} %bitcast.9.in_ref, bf16[2,2,256,256]{3,2,1,0:T(8,128)(2,1)} %get-tuple-element.28.mz_hbm), custom_call_target="tpu_custom_call" | custom-call | tf_op jit(solution)/shard_map/middle/pallas_call | solution.py:699
  139.8 0.0 copy-start.5
  139.8 5.9 %all-to-all-start.1 = ((f32[128,80,128]{2,1,0:T(8,128)}), f32[128,80,128]{2,1,0:T(8,128)}, u32[]{:S(2)}, u32[]{:S(2)}) async-start(f32[128,80,128]{2,1,0:T(8,128)} %bitcast.26), calls=%async_computation.1 | async-start | bytes 10485760 | tf_op jit(solution)/shard_map/all_to_all | solution.py:846
  145.8 3.5 %last_conc.1 = f32[512,512]{1,0:T(8,128)} custom-call(f32[512,512]{1,0:T(8,128)S(1)} %conc_step.1.c_ref, f32[512,512]{1,0:T(8,128)S(1)} %order_step.1.new_ref.p_ref, f32[512,512]{1,0:T(8,128)S(1)} %copy-done.5, f32[512,512]{1,0:T(8,128)} %copy-done.6, f32[512,512]{1,0:T(8,128)} %collective-permute-done.7.down_hbm), custom_call_target="tpu_custom_call" | custom-call | tf_op jit(solution)/shard_map/last_conc/pallas_call | solution.py:395
  149.3 60.2 %all-to-all-done.1 = f32[128,80,128]{2,1,0:T(8,128)} async-done(((f32[128,80,128]{2,1,0:T(8,128)}), f32[128,80,128]{2,1,0:T(8,128)}, u32[]{:S(2)}, u32[]{:S(2)}) %all-to-all-start.1) | async-done | bytes 5242912 | tf_op jit(solution)/shard_map/all_to_all | solution.py:846
  209.5 10.9 %inverse.1 = f32[6,512,512]{2,1,0:T(8,128)} custom-call(f32[128,10,8,128]{3,2,1,0:T(8,128)} %bitcast.11.in_ref, f32[6,512,512]{2,1,0:T(8,128)} %bitcast.25, bf16[4,2,256,256]{3,2,1,0:T(8,128)(2,1)} %get-tuple-element.29.mqi_hbm, bf16[2,2,256,256]{3,2,1,0:T(8,128)(2,1)} %get-tuple-element.30.txi_hbm), custom_call_target="tpu_custom_call" | custom-call | tf_op jit(solution)/shard_map/inverse/pallas_call | solution.py:823
  (11 shorter events, 0.0 us)
Async XLA Ops:
  0.6 22.4 %copy-start.3 = (f32[1,512,512]{2,1,0:T(8,128)S(1)}, f32[1,512,512]{2,1,0:T(8,128)}, u32[]{:S(2)}) copy-start(f32[1,512,512]{2,1,0:T(8,128)} %param.8) | copy-start | bytes 3145732
  0.6 22.4 %copy-start.4 = (f32[1,512,512]{2,1,0:T(8,128)S(1)}, f32[1,512,512]{2,1,0:T(8,128)}, u32[]{:S(2)}) copy-start(f32[1,512,512]{2,1,0:T(8,128)} %param.9) | copy-start | bytes 3145732
  0.7 22.4 %collective-permute-start = (f32[512,512]{1,0:T(8,128)}, f32[512,512]{1,0:T(8,128)S(1)}, u32[]{:S(2)}, u32[]{:S(2)}) collective-permute-start(f32[512,512]{1,0:T(8,128)} %bitcast.15), channel_id=1, source_target_pairs={{0,1},{1,2},{2,3},{3,4},{4,5},{5,6},{6,7},{7,8},{8,9},{9,10},{10,1... | collective-permute-start | bytes 3145736 | tf_op jit(solution)/shard_map/ppermute | solution.py:853
  0.7 22.3 %collective-permute-start.1 = (f32[512,512]{1,0:T(8,128)}, f32[512,512]{1,0:T(8,128)S(1)}, u32[]{:S(2)}, u32[]{:S(2)}) collective-permute-start(f32[512,512]{1,0:T(8,128)} %bitcast.16), channel_id=1, source_target_pairs={{1,0},{2,1},{3,2},{4,3},{5,4},{6,5},{7,6},{8,7},{9,8},{10,9},{11,1... | collective-permute-start | bytes 3145736 | tf_op jit(solution)/shard_map/ppermute | solution.py:853
  9.0 23.8 %collective-permute-start.2 = (f32[512,512]{1,0:T(8,128)}, f32[512,512]{1,0:T(8,128)S(1)}, u32[]{:S(2)}, u32[]{:S(2)}) collective-permute-start(f32[512,512]{1,0:T(8,128)} %bitcast.19), channel_id=1, source_target_pairs={{0,1},{1,2},{2,3},{3,4},{4,5},{5,6},{6,7},{7,8},{8,9},{9,10},{10,1... | collective-permute-start | bytes 3145736 | tf_op jit(solution)/shard_map/ppermute | solution.py:853
  9.0 26.4 %collective-permute-start.3 = (f32[512,512]{1,0:T(8,128)}, f32[512,512]{1,0:T(8,128)S(1)}, u32[]{:S(2)}, u32[]{:S(2)}) collective-permute-start(f32[512,512]{1,0:T(8,128)} %bitcast.20), channel_id=1, source_target_pairs={{1,0},{2,1},{3,2},{4,3},{5,4},{6,5},{7,6},{8,7},{9,8},{10,9},{11,1... | collective-permute-start | bytes 3145736 | tf_op jit(solution)/shard_map/ppermute | solution.py:853
  23.0 12.4 %copy-start.2 = (f32[512,512]{1,0:T(8,128)}, f32[512,512]{1,0:T(8,128)S(1)}, u32[]{:S(2)}) copy-start(f32[512,512]{1,0:T(8,128)S(1)} %get-tuple-element.18.dec_ref.dec_hbm) | copy-start | bytes 3145732
  23.0 13.3 %copy-start = (f32[6,512,512]{2,1,0:T(8,128)}, f32[6,512,512]{2,1,0:T(8,128)S(1)}, u32[]{:S(2)}) copy-start(f32[6,512,512]{2,1,0:T(8,128)S(1)} %get-tuple-element.20.unit_hbm) | copy-start | bytes 18874372
  23.0 13.3 %copy-start.1 = (f32[512,512]{1,0:T(8,128)}, f32[512,512]{1,0:T(8,128)S(1)}, u32[]{:S(2)}) copy-start(f32[512,512]{1,0:T(8,128)S(1)} %get-tuple-element.17.kin_ref.kin_hbm) | copy-start | bytes 3145732
  24.2 20.0 %collective-permute-start.4 = (f32[512,512]{1,0:T(8,128)S(1)}, f32[512,512]{1,0:T(8,128)}, u32[]{:S(2)}, u32[]{:S(2)}) collective-permute-start(f32[512,512]{1,0:T(8,128)S(1)} %order_step.1.new_ref.p_ref), channel_id=1, source_target_pairs={{0,1},{1,2},{2,3},{3,4},{4,5},{5,6},{6,7},{7,8},{8,9},{9,10},{10,1... | collective-permute-start | bytes 3145736 | tf_op jit(solution)/shard_map/ppermute | solution.py:853
  24.3 19.9 %collective-permute-start.5 = (f32[512,512]{1,0:T(8,128)S(1)}, f32[512,512]{1,0:T(8,128)}, u32[]{:S(2)}, u32[]{:S(2)}) collective-permute-start(f32[512,512]{1,0:T(8,128)S(1)} %order_step.1.new_ref.p_ref), channel_id=1, source_target_pairs={{1,0},{2,1},{3,2},{4,3},{5,4},{6,5},{7,6},{8,7},{9,8},{10,9},{11,1... | collective-permute-start | bytes 3145736 | tf_op jit(solution)/shard_map/ppermute | solution.py:853
  36.3 20.1 %collective-permute-start.6 = (f32[512,512]{1,0:T(8,128)S(1)}, f32[512,512]{1,0:T(8,128)S(1)}, u32[]{:S(2)}, u32[]{:S(2)}) collective-permute-start(f32[512,512]{1,0:T(8,128)S(1)} %conc_step.1.c_ref), channel_id=1, source_target_pairs={{0,1},{1,2},{2,3},{3,4},{4,5},{5,6},{6,7},{7,8},{8,9},{9,10},{10,1... | collective-permute-start | bytes 3145736 | tf_op jit(solution)/shard_map/ppermute | solution.py:853
  36.4 20.1 %collective-permute-start.7 = (f32[512,512]{1,0:T(8,128)S(1)}, f32[512,512]{1,0:T(8,128)}, u32[]{:S(2)}, u32[]{:S(2)}) collective-permute-start(f32[512,512]{1,0:T(8,128)S(1)} %conc_step.1.c_ref), channel_id=1, source_target_pairs={{1,0},{2,1},{3,2},{4,3},{5,4},{6,5},{7,6},{8,7},{9,8},{10,9},{11,1... | collective-permute-start | bytes 3145736 | tf_op jit(solution)/shard_map/ppermute | solution.py:853
  56.5 1.0 copy-start.6
  57.4 73.4 %all-to-all-start = ((f32[128,80,128]{2,1,0:T(8,128)}), f32[128,80,128]{2,1,0:T(8,128)}, u32[]{:S(2)}, u32[]{:S(2)}) async-start(f32[128,80,128]{2,1,0:T(8,128)} %bitcast.28), calls=%async_computation | async-start | bytes 10485760 | tf_op jit(solution)/shard_map/all_to_all | solution.py:846
  139.8 6.0 %copy-start.5 = (f32[512,512]{1,0:T(8,128)S(1)}, f32[512,512]{1,0:T(8,128)}, u32[]{:S(2)}) copy-start(f32[512,512]{1,0:T(8,128)} %get-tuple-element.22.new_ref) | copy-start | bytes 3145732
  139.8 69.7 %all-to-all-start.1 = ((f32[128,80,128]{2,1,0:T(8,128)}), f32[128,80,128]{2,1,0:T(8,128)}, u32[]{:S(2)}, u32[]{:S(2)}) async-start(f32[128,80,128]{2,1,0:T(8,128)} %bitcast.26), calls=%async_computation.1 | async-start | bytes 10485760 | tf_op jit(solution)/shard_map/all_to_all | solution.py:846

commit v6 on v5

--- a/solution.py
+++ b/solution.py
@@ -888,9 +888,9 @@
         order_now, conc_now, order_halos, kinetic, decay, unit, txf, mq
     )
     band = lax.axis_index("gz").astype(jnp.int32).reshape(1)
-    spectra, band, conc_halos = lax.optimization_barrier((spectra, band, conc_halos))
+    order_next, ready, conc_halos = lax.optimization_barrier((order_next, band, conc_halos))
     received = exchange(spectra)
-    mz, mqi, txi = backward_tables(band)
+    mz, mqi, txi = backward_tables(ready)
     conc_next = last_conc(conc_now, order_now, order_next, conc_halos)
     returned = exchange(middle(band, received, mz))
     strain_next = inverse(returned, planes, mqi, txi)

time: 221 us -> 234 us (1.059)
  waiting for transfers between devices: 123 us -> 137 us
    ppermute x8, waiting for transfers between devices: 2.06 us -> 76.5 us  [neighbours(): return (lax.ppermute(plane, 'gz', ahead), lax.ppermute(plane, 'gz', behind))]
    all_to_all x2, waiting for transfers between devices: 121 us -> 60.2 us  [exchange(): lax.all_to_all(packed, 'gz', split_axis=0, concat_axis=0, tiled=True)]
  transfers between devices with their start and end apart: 10 -> 10, of which waited for: 4 -> 4; matrix products, arithmetic and copies ran while one was open for 0% -> 0% of each run, Pallas kernels for 14% -> 8%
where the time goes in v6:
time: 234 us; the launch traced here: 233 us
  waiting for transfers between devices  137 us (59%)
  Pallas kernels  49.4 us (21%)
  starting transfers between devices  45.7 us (20%)
    ppermute x8, waiting for transfers between devices, neighbours(): return (lax.ppermute(plane, 'gz', ahead), lax.ppermute(plane, 'gz', behind))  76.5 us
    all_to_all x2, waiting for transfers between devices, exchange(): lax.all_to_all(packed, 'gz', split_axis=0, concat_axis=0, tiled=True)  60.2 us
    ppermute x8, starting transfers between devices, neighbours(): return (lax.ppermute(plane, 'gz', ahead), lax.ppermute(plane, 'gz', behind))  30.1 us
    all_to_all x2, starting transfers between devices, exchange(): lax.all_to_all(packed, 'gz', split_axis=0, concat_axis=0, tiled=True)  15.6 us
    pallas_call x1, Pallas kernels, forward(): pl.pallas_call(forward_body, in_specs=[RESIDENT] * 2 + [REMAIN] * 7, out_...  11.9 us
    pallas_call x1, Pallas kernels, inverse(): pl.pallas_call(inverse_body, in_specs=[REMAIN] * 4, out_specs=REMAIN, out...  10.9 us
    pallas_call x1, Pallas kernels, middle(): pl.pallas_call(middle_body, in_specs=[SCALAR, REMAIN, REMAIN], out_specs=...  8.99 us
    pallas_call x1, Pallas kernels, coefficients(): pl.pallas_call(coef_body, grid=(TILES,), in_specs=[REMAIN, REMAIN, REMAIN...  6.82 us
  transfers between devices with their start and end apart: 10, of which 4 were waited for; matrix products, arithmetic and copies ran while one was open for 0% of the time, Pallas kernels for 8%

profile of v6, /device:TPU:0, one launch (start us, length us, event | category | flops | bytes accessed | tf_op | source)
XLA Modules:
  0.0 232.9 jit_solution(18170399613184268675)
XLA Ops:
  0.7 0.1 collective-permute-start
  0.7 8.3 %collective-permute-start.1 = (f32[512,512]{1,0:T(8,128)}, f32[512,512]{1,0:T(8,128)S(1)}, u32[]{:S(2)}, u32[]{:S(2)}) collective-permute-start(f32[512,512]{1,0:T(8,128)} %bitcast.16), channel_id=1, source_target_pairs={{1,0},{2,1},{3,2},{4,3},{5,4},{6,5},{7,6},{8,7},{9,8},{10,9},{11,1... | collective-permute-start | bytes 3145736 | tf_op jit(solution)/shard_map/ppermute | solution.py:853
  9.0 0.0 collective-permute-start.2
  9.0 7.2 %collective-permute-start.3 = (f32[512,512]{1,0:T(8,128)}, f32[512,512]{1,0:T(8,128)S(1)}, u32[]{:S(2)}, u32[]{:S(2)}) collective-permute-start(f32[512,512]{1,0:T(8,128)} %bitcast.20), channel_id=1, source_target_pairs={{1,0},{2,1},{3,2},{4,3},{5,4},{6,5},{7,6},{8,7},{9,8},{10,9},{11,1... | collective-permute-start | bytes 3145736 | tf_op jit(solution)/shard_map/ppermute | solution.py:853
  16.2 6.8 %coefficients.1 = (f32[6,512,512]{2,1,0:T(8,128)S(1)}, f32[512,512]{1,0:T(8,128)S(1)}, f32[512,512]{1,0:T(8,128)S(1)}) custom-call(f32[2,16]{1,0:T(2,128)} %moduli_hbm.1, f32[16]{0:T(128)} %mobility_hbm.1, f32[8]{0:T(128)} %rates_hbm.1, s32[512,512]{1,0:T(8,128)} %bitcast.29, s32[512,512]{1,0:T(8,128)} %bitcast.30, f32[6,512,512]{2,1,0:T(8,128)} %bitcast.24), custom_call_target="tpu_custom_call" | custom-call | tf_op jit(solution)/shard_map/coefficients/pallas_call | solution.py:267
  23.0 0.0 copy-start
  23.0 0.0 copy-start.1
  23.0 0.0 collective-permute-done.up_ref
  23.1 0.0 collective-permute-done.1.down_ref
  23.1 1.1 order_step.1.new_ref.p_ref
  24.2 0.1 collective-permute-start.4
  24.3 7.2 %collective-permute-start.5 = (f32[512,512]{1,0:T(8,128)S(1)}, f32[512,512]{1,0:T(8,128)S(1)}, u32[]{:S(2)}, u32[]{:S(2)}) collective-permute-start(f32[512,512]{1,0:T(8,128)S(1)} %order_step.1.new_ref.p_ref), channel_id=1, source_target_pairs={{1,0},{2,1},{3,2},{4,3},{5,4},{6,5},{7,6},{8,7},{9,8},{10,9},{11,1... | collective-permute-start | bytes 3145736 | tf_op jit(solution)/shard_map/ppermute | solution.py:853
  31.4 1.4 collective-permute-done.2.order_ref.up_ref
  32.9 2.5 %onward_tables.1 = (bf16[2,2,256,256]{3,2,1,0:T(8,128)(2,1)}, bf16[4,2,256,256]{3,2,1,0:T(8,128)(2,1)}) custom-call(f32[512,512]{1,0:T(8,128)S(1)} %collective-permute-done.2.order_ref.up_ref), custom_call_target="tpu_custom_call" | custom-call | tf_op jit(solution)/shard_map/onward_tables/pallas_call | solution.py:127
  35.4 0.0 collective-permute-done.3.down_ref
  35.4 0.9 conc_step.1.c_ref
  36.3 7.8 %collective-permute-done.4.up_hbm = f32[512,512]{1,0:T(8,128)S(1)} collective-permute-done((f32[512,512]{1,0:T(8,128)S(1)}, f32[512,512]{1,0:T(8,128)S(1)}, u32[]{:S(2)}, u32[]{:S(2)}) %collective-permute-start.4) | collective-permute-done | bytes 1048608 | tf_op jit(solution)/shard_map/ppermute | solution.py:853
  44.1 0.0 collective-permute-done.5.down_hbm
  44.1 11.9 %forward.1 = (f32[128,10,8,128]{3,2,1,0:T(8,128)}, f32[512,512]{1,0:T(8,128)}) custom-call(f32[512,512]{1,0:T(8,128)S(1)} %order_step.1.new_ref.p_ref, f32[512,512]{1,0:T(8,128)S(1)} %conc_step.1.c_ref, f32[512,512]{1,0:T(8,128)S(1)} %collective-permute-done.4.up_hbm, f32[512,512]{1,0:T(8,128)S(1)} %collective-permute-done.5.down_hbm, f32[512,512]{1,0:T(8,128)} %copy-done.1, ...), custom_call_target="tpu_custom_call" | custom-call | tf_op jit(solution)/shard_map/forward/pallas_call | solution.py:590
  56.0 9.7 %all-to-all-start = ((f32[128,80,128]{2,1,0:T(8,128)}), f32[128,80,128]{2,1,0:T(8,128)}, u32[]{:S(2)}, u32[]{:S(2)}) async-start(f32[128,80,128]{2,1,0:T(8,128)} %bitcast.28), calls=%async_computation | async-start | bytes 10485760 | tf_op jit(solution)/shard_map/all_to_all | solution.py:846
  65.7 0.1 collective-permute-start.6
  65.7 7.3 %collective-permute-start.7 = (f32[512,512]{1,0:T(8,128)S(1)}, f32[512,512]{1,0:T(8,128)}, u32[]{:S(2)}, u32[]{:S(2)}) collective-permute-start(f32[512,512]{1,0:T(8,128)S(1)} %conc_step.1.c_ref), channel_id=1, source_target_pairs={{1,0},{2,1},{3,2},{4,3},{5,4},{6,5},{7,6},{8,7},{9,8},{10,9},{11,1... | collective-permute-start | bytes 3145736 | tf_op jit(solution)/shard_map/ppermute | solution.py:853
  73.0 67.3 %collective-permute-done.6.up_hbm = f32[512,512]{1,0:T(8,128)S(1)} collective-permute-done((f32[512,512]{1,0:T(8,128)S(1)}, f32[512,512]{1,0:T(8,128)S(1)}, u32[]{:S(2)}, u32[]{:S(2)}) %collective-permute-start.6) | collective-permute-done | bytes 1048608 | tf_op jit(solution)/shard_map/ppermute | solution.py:853
  140.3 0.0 collective-permute-done.7.down_hbm
  140.3 2.8 %backward_tables.1 = (bf16[2,2,256,256]{3,2,1,0:T(8,128)(2,1)}, bf16[4,2,256,256]{3,2,1,0:T(8,128)(2,1)}, bf16[2,2,256,256]{3,2,1,0:T(8,128)(2,1)}) custom-call(s32[1]{0:T(128)} %bitcast.5.order_ref.band_ref), custom_call_target="tpu_custom_call" | custom-call | tf_op jit(solution)/shard_map/backward_tables/pallas_call | solution.py:127
  143.2 0.0 all-to-all-done
  143.2 9.0 %middle.1 = f32[128,10,8,128]{3,2,1,0:T(8,128)} custom-call(s32[1]{0:T(128)} %bitcast.5.order_ref.band_ref, f32[128,10,8,128]{3,2,1,0:T(8,128)} %bitcast.9.in_ref, bf16[2,2,256,256]{3,2,1,0:T(8,128)(2,1)} %get-tuple-element.28.mz_hbm), custom_call_target="tpu_custom_call" | custom-call | tf_op jit(solution)/shard_map/middle/pallas_call | solution.py:699
  152.2 0.0 copy-start.5
  152.2 5.9 %all-to-all-start.1 = ((f32[128,80,128]{2,1,0:T(8,128)}), f32[128,80,128]{2,1,0:T(8,128)}, u32[]{:S(2)}, u32[]{:S(2)}) async-start(f32[128,80,128]{2,1,0:T(8,128)} %bitcast.26), calls=%async_computation.1 | async-start | bytes 10485760 | tf_op jit(solution)/shard_map/all_to_all | solution.py:846
  158.2 3.5 %last_conc.1 = f32[512,512]{1,0:T(8,128)} custom-call(f32[512,512]{1,0:T(8,128)S(1)} %conc_step.1.c_ref, f32[512,512]{1,0:T(8,128)S(1)} %order_step.1.new_ref.p_ref, f32[512,512]{1,0:T(8,128)S(1)} %copy-done.5, f32[512,512]{1,0:T(8,128)} %copy-done.6, f32[512,512]{1,0:T(8,128)} %collective-permute-done.7.down_hbm), custom_call_target="tpu_custom_call" | custom-call | tf_op jit(solution)/shard_map/last_conc/pallas_call | solution.py:395
  161.6 60.2 %all-to-all-done.1 = f32[128,80,128]{2,1,0:T(8,128)} async-done(((f32[128,80,128]{2,1,0:T(8,128)}), f32[128,80,128]{2,1,0:T(8,128)}, u32[]{:S(2)}, u32[]{:S(2)}) %all-to-all-start.1) | async-done | bytes 5242912 | tf_op jit(solution)/shard_map/all_to_all | solution.py:846
  221.9 10.9 %inverse.1 = f32[6,512,512]{2,1,0:T(8,128)} custom-call(f32[128,10,8,128]{3,2,1,0:T(8,128)} %bitcast.11.in_ref, f32[6,512,512]{2,1,0:T(8,128)} %bitcast.25, bf16[4,2,256,256]{3,2,1,0:T(8,128)(2,1)} %get-tuple-element.29.mqi_hbm, bf16[2,2,256,256]{3,2,1,0:T(8,128)(2,1)} %get-tuple-element.30.txi_hbm), custom_call_target="tpu_custom_call" | custom-call | tf_op jit(solution)/shard_map/inverse/pallas_call | solution.py:823
  (11 shorter events, 0.0 us)
Async XLA Ops:
  0.6 22.4 %copy-start.3 = (f32[1,512,512]{2,1,0:T(8,128)S(1)}, f32[1,512,512]{2,1,0:T(8,128)}, u32[]{:S(2)}) copy-start(f32[1,512,512]{2,1,0:T(8,128)} %param.8) | copy-start | bytes 3145732
  0.6 22.4 %copy-start.4 = (f32[1,512,512]{2,1,0:T(8,128)S(1)}, f32[1,512,512]{2,1,0:T(8,128)}, u32[]{:S(2)}) copy-start(f32[1,512,512]{2,1,0:T(8,128)} %param.9) | copy-start | bytes 3145732
  0.7 22.4 %collective-permute-start = (f32[512,512]{1,0:T(8,128)}, f32[512,512]{1,0:T(8,128)S(1)}, u32[]{:S(2)}, u32[]{:S(2)}) collective-permute-start(f32[512,512]{1,0:T(8,128)} %bitcast.15), channel_id=1, source_target_pairs={{0,1},{1,2},{2,3},{3,4},{4,5},{5,6},{6,7},{7,8},{8,9},{9,10},{10,1... | collective-permute-start | bytes 3145736 | tf_op jit(solution)/shard_map/ppermute | solution.py:853
  0.7 22.3 %collective-permute-start.1 = (f32[512,512]{1,0:T(8,128)}, f32[512,512]{1,0:T(8,128)S(1)}, u32[]{:S(2)}, u32[]{:S(2)}) collective-permute-start(f32[512,512]{1,0:T(8,128)} %bitcast.16), channel_id=1, source_target_pairs={{1,0},{2,1},{3,2},{4,3},{5,4},{6,5},{7,6},{8,7},{9,8},{10,9},{11,1... | collective-permute-start | bytes 3145736 | tf_op jit(solution)/shard_map/ppermute | solution.py:853
  9.0 23.8 %collective-permute-start.2 = (f32[512,512]{1,0:T(8,128)}, f32[512,512]{1,0:T(8,128)S(1)}, u32[]{:S(2)}, u32[]{:S(2)}) collective-permute-start(f32[512,512]{1,0:T(8,128)} %bitcast.19), channel_id=1, source_target_pairs={{0,1},{1,2},{2,3},{3,4},{4,5},{5,6},{6,7},{7,8},{8,9},{9,10},{10,1... | collective-permute-start | bytes 3145736 | tf_op jit(solution)/shard_map/ppermute | solution.py:853
  9.0 26.4 %collective-permute-start.3 = (f32[512,512]{1,0:T(8,128)}, f32[512,512]{1,0:T(8,128)S(1)}, u32[]{:S(2)}, u32[]{:S(2)}) collective-permute-start(f32[512,512]{1,0:T(8,128)} %bitcast.20), channel_id=1, source_target_pairs={{1,0},{2,1},{3,2},{4,3},{5,4},{6,5},{7,6},{8,7},{9,8},{10,9},{11,1... | collective-permute-start | bytes 3145736 | tf_op jit(solution)/shard_map/ppermute | solution.py:853
  23.0 13.3 %copy-start = (f32[6,512,512]{2,1,0:T(8,128)}, f32[6,512,512]{2,1,0:T(8,128)S(1)}, u32[]{:S(2)}) copy-start(f32[6,512,512]{2,1,0:T(8,128)S(1)} %get-tuple-element.20.unit_hbm) | copy-start | bytes 18874372
  23.0 13.3 %copy-start.1 = (f32[512,512]{1,0:T(8,128)}, f32[512,512]{1,0:T(8,128)S(1)}, u32[]{:S(2)}) copy-start(f32[512,512]{1,0:T(8,128)S(1)} %get-tuple-element.17.kin_ref.kin_hbm) | copy-start | bytes 3145732
  23.0 13.3 %copy-start.2 = (f32[512,512]{1,0:T(8,128)}, f32[512,512]{1,0:T(8,128)S(1)}, u32[]{:S(2)}) copy-start(f32[512,512]{1,0:T(8,128)S(1)} %get-tuple-element.18.dec_ref.dec_hbm) | copy-start | bytes 3145732
  24.2 19.9 %collective-permute-start.4 = (f32[512,512]{1,0:T(8,128)S(1)}, f32[512,512]{1,0:T(8,128)S(1)}, u32[]{:S(2)}, u32[]{:S(2)}) collective-permute-start(f32[512,512]{1,0:T(8,128)S(1)} %order_step.1.new_ref.p_ref), channel_id=1, source_target_pairs={{0,1},{1,2},{2,3},{3,4},{4,5},{5,6},{6,7},{7,8},{8,9},{9,10},{10,1... | collective-permute-start | bytes 3145736 | tf_op jit(solution)/shard_map/ppermute | solution.py:853
  24.3 19.8 %collective-permute-start.5 = (f32[512,512]{1,0:T(8,128)S(1)}, f32[512,512]{1,0:T(8,128)S(1)}, u32[]{:S(2)}, u32[]{:S(2)}) collective-permute-start(f32[512,512]{1,0:T(8,128)S(1)} %order_step.1.new_ref.p_ref), channel_id=1, source_target_pairs={{1,0},{2,1},{3,2},{4,3},{5,4},{6,5},{7,6},{8,7},{9,8},{10,9},{11,1... | collective-permute-start | bytes 3145736 | tf_op jit(solution)/shard_map/ppermute | solution.py:853
  56.0 87.2 %all-to-all-start = ((f32[128,80,128]{2,1,0:T(8,128)}), f32[128,80,128]{2,1,0:T(8,128)}, u32[]{:S(2)}, u32[]{:S(2)}) async-start(f32[128,80,128]{2,1,0:T(8,128)} %bitcast.28), calls=%async_computation | async-start | bytes 10485760 | tf_op jit(solution)/shard_map/all_to_all | solution.py:846
  65.7 74.7 %collective-permute-start.6 = (f32[512,512]{1,0:T(8,128)S(1)}, f32[512,512]{1,0:T(8,128)S(1)}, u32[]{:S(2)}, u32[]{:S(2)}) collective-permute-start(f32[512,512]{1,0:T(8,128)S(1)} %conc_step.1.c_ref), channel_id=1, source_target_pairs={{0,1},{1,2},{2,3},{3,4},{4,5},{5,6},{6,7},{7,8},{8,9},{9,10},{10,1... | collective-permute-start | bytes 3145736 | tf_op jit(solution)/shard_map/ppermute | solution.py:853
  65.7 74.6 %collective-permute-start.7 = (f32[512,512]{1,0:T(8,128)S(1)}, f32[512,512]{1,0:T(8,128)}, u32[]{:S(2)}, u32[]{:S(2)}) collective-permute-start(f32[512,512]{1,0:T(8,128)S(1)} %conc_step.1.c_ref), channel_id=1, source_target_pairs={{1,0},{2,1},{3,2},{4,3},{5,4},{6,5},{7,6},{8,7},{9,8},{10,9},{11,1... | collective-permute-start | bytes 3145736 | tf_op jit(solution)/shard_map/ppermute | solution.py:853
  140.3 11.8 %copy-start.6 = (f32[512,512]{1,0:T(8,128)}, f32[512,512]{1,0:T(8,128)S(1)}, u32[]{:S(2)}) copy-start(f32[512,512]{1,0:T(8,128)S(1)} %collective-permute-done.6.up_hbm) | copy-start | bytes 3145732
  152.2 6.0 %copy-start.5 = (f32[512,512]{1,0:T(8,128)S(1)}, f32[512,512]{1,0:T(8,128)}, u32[]{:S(2)}) copy-start(f32[512,512]{1,0:T(8,128)} %get-tuple-element.23.new_ref) | copy-start | bytes 3145732
  152.2 69.7 %all-to-all-start.1 = ((f32[128,80,128]{2,1,0:T(8,128)}), f32[128,80,128]{2,1,0:T(8,128)}, u32[]{:S(2)}, u32[]{:S(2)}) async-start(f32[128,80,128]{2,1,0:T(8,128)} %bitcast.26), calls=%async_computation.1 | async-start | bytes 10485760 | tf_op jit(solution)/shard_map/all_to_all | solution.py:846
